TPU v7x, 32 devices: a whole 2x2x4 slice. The times are simulated.
32 devices in a mesh: fsdp: 4 (over x, core), ctx: 4 (over z), tp: 2 (over y).
Axes of the slice: x: 2, y: 2, z: 4, core: 2. Of those that a mesh axis runs over, the one named last changes fastest.
Arguments:
- tokens: bfloat16 [8, 1024, 2048], P('fsdp', ('ctx', 'tp')), may hold values from -6 to 6
- side_input: bfloat16 [8, 1024, 256], P('fsdp', ('ctx', 'tp')), may hold values from -6 to 6
- prefix: int32 [8], P('fsdp'), may hold values from 102 to 512
- positions: int32 [8, 1024], P('fsdp', 'ctx'), may hold values from 0 to 2046, as said below
- cotangent: bfloat16 [8, 1024, 2048], P('fsdp', ('ctx', 'tp')), may hold values from -6 to 6
- query_weight: bfloat16 [2048, 2048], P(('fsdp', 'ctx'), 'tp'), may hold values from -0.125 to 0.125
- key_matrix: bfloat16 [2048, 512], P(('fsdp', 'ctx'), 'tp'), may hold values from -0.125 to 0.125
- value_matrix: bfloat16 [2048, 512], P(('fsdp', 'ctx'), 'tp'), may hold values from -0.125 to 0.125
- out_weight: bfloat16 [2048, 2048], P('tp', ('fsdp', 'ctx')), may hold values from -0.125 to 0.125
- gate_weight: bfloat16 [2048, 8192], P(('fsdp', 'ctx'), 'tp'), may hold values from -0.125 to 0.125
- up_weight: bfloat16 [2048, 8192], P(('fsdp', 'ctx'), 'tp'), may hold values from -0.125 to 0.125
- down_weight: bfloat16 [8192, 2048], P('tp', ('fsdp', 'ctx')), may hold values from -0.0625 to 0.0625
- laurel_left: bfloat16 [2048, 64], P(('fsdp', 'ctx', 'tp')), may hold values from -0.125 to 0.125
- laurel_right: bfloat16 [64, 2048], P(None, ('fsdp', 'ctx', 'tp')), may hold values from -0.75 to 0.75
- side_gate_weight: bfloat16 [2048, 256], P(('fsdp', 'ctx', 'tp')), may hold values from -0.125 to 0.125
- side_out_weight: bfloat16 [256, 2048], P(None, ('fsdp', 'ctx', 'tp')), may hold values from -0.375 to 0.375
- input_gain: float32 [2048], replicated, may hold values from 0.25 to 1.75
- laurel_gain: float32 [2048], replicated, may hold values from 0.25 to 1.75
- attention_gain: float32 [2048], replicated, may hold values from 0.25 to 1.75
- hidden_in_gain: float32 [2048], replicated, may hold values from 0.25 to 1.75
- hidden_out_gain: float32 [2048], replicated, may hold values from 0.25 to 1.75
- side_gain: float32 [2048], replicated, may hold values from 0.25 to 1.75
- query_gain: float32 [256], replicated, may hold values from 0.08 to 0.18
- key_gain: float32 [256], replicated, may hold values from 0.5 to 1.5
Outputs:
- output: bfloat16 [8, 1024, 2048], P('fsdp', ('ctx', 'tp'))
- tokens_grad: float32 [8, 1024, 2048], P('fsdp', ('ctx', 'tp'))
- side_input_grad: float32 [8, 1024, 256], P('fsdp', ('ctx', 'tp'))
- query_weight_grad: float32 [2048, 2048], P(('fsdp', 'ctx'), 'tp')
- key_weight_grad: float32 [2048, 512], P(('fsdp', 'ctx'), 'tp')
- value_weight_grad: float32 [2048, 512], P(('fsdp', 'ctx'), 'tp')
- out_weight_grad: float32 [2048, 2048], P('tp', ('fsdp', 'ctx'))
- gate_weight_grad: float32 [2048, 8192], P(('fsdp', 'ctx'), 'tp')
- up_weight_grad: float32 [2048, 8192], P(('fsdp', 'ctx'), 'tp')
- down_weight_grad: float32 [8192, 2048], P('tp', ('fsdp', 'ctx'))
- laurel_left_grad: float32 [2048, 64], P(('fsdp', 'ctx', 'tp'))
- laurel_right_grad: float32 [64, 2048], P(None, ('fsdp', 'ctx', 'tp'))
- side_gate_weight_grad: float32 [2048, 256], P(('fsdp', 'ctx', 'tp'))
- side_out_weight_grad: float32 [256, 2048], P(None, ('fsdp', 'ctx', 'tp'))
- input_gain_grad: float32 [2048], replicated
- laurel_gain_grad: float32 [2048], replicated
- attention_gain_grad: float32 [2048], replicated
- hidden_in_gain_grad: float32 [2048], replicated
- hidden_out_gain_grad: float32 [2048], replicated
- side_gain_grad: float32 [2048], replicated
- query_gain_grad: float32 [256], replicated
- key_gain_grad: float32 [256], replicated
Inputs may be any that keep to these rules, and one draw needn't show every extreme that they name: The first prefix[b] tokens of sequence b see one another in both directions. Within each sequence positions rise strictly, from 0 at the first token to 2046 at the last.
All inputs are finite; a program needn't handle non-finite values.
Results may differ from a plain program's by a relative error of at most 0.022.
Values may be sent and summed in bfloat16 or wider, within the bound.
No kernel may reach another device: no remote copies, remote signals or barrier semaphores. Data moves between devices by JAX's collectives and lax.ppermute only.
A program may use at most 320 MiB of HBM per device.

v0:
```python
import jax
import jax.numpy as jnp
from jax import lax
from jax.sharding import PartitionSpec as P

HEAD_SIZE = 256


EPS = 1e-06
THETA = 1000000.0
MASKED = -1e30
SQRT_HALF = 0.7071067811865476


def scaled_norm(value, gain):
    return value * lax.rsqrt(jnp.mean(value * value, axis=-1, keepdims=True) + EPS) * gain


def plain_norm(value):
    return value * lax.rsqrt(jnp.mean(value * value, axis=-1, keepdims=True) + EPS)


def rotate(value, positions):
    half = value.shape[-1] // 2
    freq = THETA ** (-(jnp.arange(half, dtype=jnp.float32) * 2.0) / value.shape[-1])
    angle = positions.astype(jnp.float32)[..., None] * freq
    cosine = jnp.cos(angle)[..., None, :]
    sine = jnp.sin(angle)[..., None, :]
    first = value[..., :half]
    second = value[..., half:]
    return jnp.concatenate(
        [first * cosine - second * sine, second * cosine + first * sine], axis=-1
    )


def geglu(gate, upward):
    return jax.nn.gelu(gate, approximate=True) * upward


def attention_mix(inputs, attention, normed, laurel, attention_gain, laurel_gain):
    return (
        inputs + scaled_norm(attention, attention_gain) + normed + scaled_norm(laurel, laurel_gain)
    ) * SQRT_HALF


def residual_mix(residual, branch, gain):
    return residual + scaled_norm(branch, gain)


def matmul(left, right):
    return jnp.dot(left, right, preferred_element_type=jnp.float32)


def gather_rows(value):
    return lax.all_gather(value, "tp", axis=1, tiled=True)


def sum_rows(value):
    return lax.psum_scatter(
        value.astype(jnp.bfloat16), "tp", scatter_dimension=1, tiled=True
    ).astype(jnp.float32)


def on_device(
    tokens,
    side_input,
    prefix,
    positions,
    cotangent,
    query_weight,
    key_matrix,
    value_matrix,
    out_weight,
    gate_weight,
    up_weight,
    down_weight,
    laurel_left,
    laurel_right,
    side_gate_weight,
    side_out_weight,
    input_gain,
    laurel_gain,
    attention_gain,
    hidden_in_gain,
    hidden_out_gain,
    side_gain,
    query_gain,
    key_gain,
):
    sequences, own_rows, width = tokens.shape
    side_width = side_input.shape[2]
    block_rows = positions.shape[1]
    seq_length = block_rows * lax.axis_size("ctx")
    first_row = lax.axis_index("ctx") * block_rows
    row_index = first_row + jnp.arange(block_rows, dtype=jnp.int32)
    layer = (
        lax.all_gather(query_weight, ("fsdp", "ctx"), axis=0, tiled=True),
        lax.all_gather(key_matrix, ("fsdp", "ctx"), axis=0, tiled=True),
        lax.all_gather(value_matrix, ("fsdp", "ctx"), axis=0, tiled=True),
        lax.all_gather(out_weight, ("fsdp", "ctx"), axis=1, tiled=True),
        lax.all_gather(gate_weight, ("fsdp", "ctx"), axis=0, tiled=True),
        lax.all_gather(up_weight, ("fsdp", "ctx"), axis=0, tiled=True),
        lax.all_gather(down_weight, ("fsdp", "ctx"), axis=1, tiled=True),
    )
    query_full, key_full, value_full, out_full, gate_full, up_full, down_full = layer
    laurel_down, laurel_up, side_gate_full, side_out_full = (
        lax.all_gather(laurel_left, ("fsdp", "ctx", "tp"), axis=0, tiled=True),
        lax.all_gather(laurel_right, ("fsdp", "ctx", "tp"), axis=1, tiled=True),
        lax.all_gather(side_gate_weight, ("fsdp", "ctx", "tp"), axis=0, tiled=True),
        lax.all_gather(side_out_weight, ("fsdp", "ctx", "tp"), axis=1, tiled=True),
    )
    local_heads = query_full.shape[1] // HEAD_SIZE
    local_groups = key_full.shape[1] // HEAD_SIZE
    per_group = local_heads // local_groups
    key_block = min(512, seq_length)
    block_count = seq_length // key_block
    inputs = tokens.astype(jnp.float32)
    normed, input_pull = jax.vjp(scaled_norm, inputs, input_gain)
    normed_reduced = normed.astype(jnp.bfloat16)
    flat_in = gather_rows(normed_reduced).reshape(-1, width)
    query_raw = matmul(flat_in, query_full)
    key_unrotated = matmul(flat_in, key_full)
    value_unprojected = matmul(flat_in, value_full)

    def heads_of(query_part, key_part, value_part, gain_query, gain_key):
        rotated_queries = rotate(
            scaled_norm(
                query_part.reshape(sequences, block_rows, local_heads, HEAD_SIZE), gain_query
            ),
            positions,
        )
        rotated_keys = rotate(
            scaled_norm(key_part.reshape(sequences, block_rows, local_groups, HEAD_SIZE), gain_key),
            positions,
        )
        normed_values = plain_norm(
            value_part.reshape(sequences, block_rows, local_groups, HEAD_SIZE)
        )
        return (rotated_queries, rotated_keys, normed_values)

    (query_rows, keys, values), heads_pull = jax.vjp(
        heads_of, query_raw, key_unrotated, value_unprojected, query_gain, key_gain
    )
    query_low = query_rows.astype(jnp.bfloat16).reshape(
        sequences, block_rows, local_groups, per_group, HEAD_SIZE
    )
    all_keys, all_values = (
        lax.all_gather(keys.astype(jnp.bfloat16), "ctx", axis=1, tiled=True),
        lax.all_gather(values.astype(jnp.bfloat16), "ctx", axis=1, tiled=True),
    )

    def block_scores(start):
        key_part = lax.dynamic_slice_in_dim(all_keys, start, key_block, 1)
        scores = jnp.einsum(
            "sbkgd,sjkd->skgbj", query_low, key_part, preferred_element_type=jnp.float32
        )
        key_index = start + jnp.arange(key_block, dtype=jnp.int32)
        visible = (key_index[None, None, :] <= row_index[None, :, None]) | (
            key_index[None, None, :] < prefix[:, None, None]
        )
        return (jnp.where(visible[:, None, None], scores, MASKED), key_part)

    stat_shape = (sequences, local_groups, per_group, block_rows)

    def stat_step(index, carry):
        start = index * key_block
        highest, total = carry
        scores, unused = block_scores(start)
        new_high = jnp.maximum(highest, jnp.max(scores, axis=-1))
        total = total * jnp.exp(highest - new_high) + jnp.sum(
            jnp.exp(scores - new_high[..., None]), axis=-1
        )
        return (new_high, total)

    highest, total = lax.fori_loop(
        0,
        block_count,
        stat_step,
        (jnp.full(stat_shape, MASKED, jnp.float32), jnp.zeros(stat_shape, jnp.float32)),
    )
    log_total = highest + jnp.log(total)

    def out_step(index, carry):
        start = index * key_block
        scores, unused = block_scores(start)
        weights = jnp.exp(scores - log_total[..., None]).astype(jnp.bfloat16)
        value_part = lax.dynamic_slice_in_dim(all_values, start, key_block, 1)
        return carry + jnp.einsum(
            "skgbj,sjkd->sbkgd", weights, value_part, preferred_element_type=jnp.float32
        )

    attended = lax.fori_loop(
        0,
        block_count,
        out_step,
        jnp.zeros((sequences, block_rows, local_groups, per_group, HEAD_SIZE), jnp.float32),
    )
    attended_low = attended.astype(jnp.bfloat16).reshape(
        sequences * block_rows, local_heads * HEAD_SIZE
    )
    attention = sum_rows(matmul(attended_low, out_full).reshape(sequences, block_rows, width))
    flat_normed = normed_reduced.reshape(-1, width)
    laurel_mid = matmul(flat_normed, laurel_down).astype(jnp.bfloat16)
    laurel_out = matmul(laurel_mid, laurel_up).reshape(sequences, own_rows, width)
    mixed, mix_pull = jax.vjp(
        attention_mix, inputs, attention, normed, laurel_out, attention_gain, laurel_gain
    )
    hidden_in, pre_pull = jax.vjp(scaled_norm, mixed, hidden_in_gain)
    hidden_block = gather_rows(hidden_in.astype(jnp.bfloat16)).reshape(-1, width)
    gate = matmul(hidden_block, gate_full)
    upward = matmul(hidden_block, up_full)
    hidden, hidden_pull = jax.vjp(geglu, gate, upward)
    hidden_low = hidden.astype(jnp.bfloat16)
    hidden_out = sum_rows(matmul(hidden_low, down_full).reshape(sequences, block_rows, width))
    layer_out, post_pull = jax.vjp(residual_mix, mixed, hidden_out, hidden_out_gain)
    layer_low = layer_out.astype(jnp.bfloat16).reshape(-1, width)
    side_pre = matmul(layer_low, side_gate_full)
    side_act, side_pull = jax.vjp(
        geglu, side_pre, side_input.astype(jnp.float32).reshape(-1, side_width)
    )
    side_low = side_act.astype(jnp.bfloat16)
    projected = matmul(side_low, side_out_full).reshape(sequences, own_rows, width)
    result, final_pull = jax.vjp(residual_mix, layer_out, projected, side_gain)
    out_grad_first, projected_grad, side_gain_grad = final_pull(cotangent.astype(jnp.float32))
    projected_low = projected_grad.astype(jnp.bfloat16).reshape(-1, width)
    side_out_grad = matmul(side_low.T, projected_low)
    side_grad = matmul(projected_low, side_out_full.T)
    side_pre_grad, side_input_grad = side_pull(side_grad)
    side_pre_low = side_pre_grad.astype(jnp.bfloat16)
    side_gate_grad = matmul(layer_low.T, side_pre_low)
    layer_grad = out_grad_first + matmul(side_pre_low, side_gate_full.T).reshape(
        sequences, own_rows, width
    )
    mixed_grad_first, hidden_out_grad, hidden_out_gain_grad = post_pull(layer_grad)
    query_full, key_full, value_full, out_full, gate_full, up_full, down_full = layer
    hidden_out_block = gather_rows(hidden_out_grad.astype(jnp.bfloat16)).reshape(-1, width)
    down_grad = matmul(hidden_low.T, hidden_out_block)
    hidden_grad = matmul(hidden_out_block, down_full.T)
    gate_grad_full, up_grad_full = hidden_pull(hidden_grad)
    gate_low = gate_grad_full.astype(jnp.bfloat16)
    up_low = up_grad_full.astype(jnp.bfloat16)
    gate_grad = matmul(hidden_block.T, gate_low)
    up_grad = matmul(hidden_block.T, up_low)
    hidden_in_part = (matmul(gate_low, gate_full.T) + matmul(up_low, up_full.T)).reshape(
        sequences, block_rows, width
    )
    mixed_grad_second, hidden_in_gain_grad = pre_pull(sum_rows(hidden_in_part))
    mixed_grad = mixed_grad_first + mixed_grad_second
    (
        inputs_grad_first,
        attention_grad,
        normed_grad_first,
        laurel_grad,
        attention_gain_grad,
        laurel_gain_grad,
    ) = mix_pull(mixed_grad)
    laurel_low = laurel_grad.astype(jnp.bfloat16).reshape(-1, width)
    laurel_right_grad = matmul(laurel_mid.T, laurel_low)
    laurel_mid_grad = matmul(laurel_low, laurel_up.T).astype(jnp.bfloat16)
    laurel_left_grad = matmul(flat_normed.T, laurel_mid_grad)
    normed_grad_second = matmul(laurel_mid_grad, laurel_down.T).reshape(sequences, own_rows, width)
    attention_block = gather_rows(attention_grad.astype(jnp.bfloat16)).reshape(-1, width)
    out_grad = matmul(attended_low.T, attention_block)
    attended_grad = (
        matmul(attention_block, out_full.T)
        .astype(jnp.bfloat16)
        .reshape(sequences, block_rows, local_groups, per_group, HEAD_SIZE)
    )
    delta = jnp.transpose(
        jnp.sum(attended_grad.astype(jnp.float32) * attended, axis=-1), (0, 2, 3, 1)
    )

    def back_step(index, carry):
        start = index * key_block
        query_grad, keys_grad, values_grad = carry
        scores, key_part = block_scores(start)
        value_part = lax.dynamic_slice_in_dim(all_values, start, key_block, 1)
        probs = jnp.exp(scores - log_total[..., None])
        probs_low = probs.astype(jnp.bfloat16)
        probs_grad = jnp.einsum(
            "sbkgd,sjkd->skgbj", attended_grad, value_part, preferred_element_type=jnp.float32
        )
        scores_grad = (probs * (probs_grad - delta[..., None])).astype(jnp.bfloat16)
        query_grad = query_grad + jnp.einsum(
            "skgbj,sjkd->sbkgd", scores_grad, key_part, preferred_element_type=jnp.float32
        )
        key_piece = jnp.einsum(
            "skgbj,sbkgd->sjkd", scores_grad, query_low, preferred_element_type=jnp.float32
        )
        value_piece = jnp.einsum(
            "skgbj,sbkgd->sjkd", probs_low, attended_grad, preferred_element_type=jnp.float32
        )
        keys_grad = lax.dynamic_update_slice_in_dim(keys_grad, key_piece, start, 1)
        values_grad = lax.dynamic_update_slice_in_dim(values_grad, value_piece, start, 1)
        return (query_grad, keys_grad, values_grad)

    kv_zeros = jnp.zeros((sequences, seq_length, local_groups, HEAD_SIZE), jnp.float32)
    query_grad, keys_grad, values_grad = lax.fori_loop(
        0,
        block_count,
        back_step,
        (
            jnp.zeros((sequences, block_rows, local_groups, per_group, HEAD_SIZE), jnp.float32),
            kv_zeros,
            kv_zeros,
        ),
    )
    keys_own, values_own = (
        lax.psum_scatter(
            keys_grad.astype(jnp.bfloat16), "ctx", scatter_dimension=1, tiled=True
        ).astype(jnp.float32),
        lax.psum_scatter(
            values_grad.astype(jnp.bfloat16), "ctx", scatter_dimension=1, tiled=True
        ).astype(jnp.float32),
    )
    query_raw_grad, key_raw_grad, value_raw_grad, query_gain_grad, key_gain_grad = heads_pull(
        (query_grad.reshape(sequences, block_rows, local_heads, HEAD_SIZE), keys_own, values_own)
    )
    query_raw_low = query_raw_grad.astype(jnp.bfloat16)
    key_raw_low = key_raw_grad.astype(jnp.bfloat16)
    value_raw_low = value_raw_grad.astype(jnp.bfloat16)
    query_weight_grad = matmul(flat_in.T, query_raw_low)
    key_weight_grad = matmul(flat_in.T, key_raw_low)
    value_weight_grad = matmul(flat_in.T, value_raw_low)
    block_in_grad = (
        matmul(query_raw_low, query_full.T)
        + matmul(key_raw_low, key_full.T)
        + matmul(value_raw_low, value_full.T)
    ).reshape(sequences, block_rows, width)
    normed_grad = normed_grad_first + normed_grad_second + sum_rows(block_in_grad)
    inputs_grad_second, input_gain_grad = input_pull(normed_grad)
    tokens_grad = inputs_grad_first + inputs_grad_second
    weight_grads = (
        lax.psum_scatter(query_weight_grad, ("fsdp", "ctx"), scatter_dimension=0, tiled=True),
        lax.psum_scatter(key_weight_grad, ("fsdp", "ctx"), scatter_dimension=0, tiled=True),
        lax.psum_scatter(value_weight_grad, ("fsdp", "ctx"), scatter_dimension=0, tiled=True),
        lax.psum_scatter(out_grad, ("fsdp", "ctx"), scatter_dimension=1, tiled=True),
        lax.psum_scatter(gate_grad, ("fsdp", "ctx"), scatter_dimension=0, tiled=True),
        lax.psum_scatter(up_grad, ("fsdp", "ctx"), scatter_dimension=0, tiled=True),
        lax.psum_scatter(down_grad, ("fsdp", "ctx"), scatter_dimension=1, tiled=True),
    )
    side_grads = (
        lax.psum_scatter(laurel_left_grad, ("fsdp", "ctx", "tp"), scatter_dimension=0, tiled=True),
        lax.psum_scatter(laurel_right_grad, ("fsdp", "ctx", "tp"), scatter_dimension=1, tiled=True),
        lax.psum_scatter(side_gate_grad, ("fsdp", "ctx", "tp"), scatter_dimension=0, tiled=True),
        lax.psum_scatter(side_out_grad, ("fsdp", "ctx", "tp"), scatter_dimension=1, tiled=True),
    )
    gain_grads = lax.psum(
        (
            input_gain_grad,
            laurel_gain_grad,
            attention_gain_grad,
            hidden_in_gain_grad,
            hidden_out_gain_grad,
            side_gain_grad,
            query_gain_grad,
            key_gain_grad,
        ),
        ("fsdp", "ctx", "tp"),
    )
    side_input_grad = side_input_grad.reshape(sequences, own_rows, side_width)
    return (
        (result.astype(jnp.bfloat16), tokens_grad, side_input_grad)
        + tuple(weight_grads)
        + tuple(side_grads)
        + tuple(gain_grads)
    )


def solution(mesh):
    placed = (
        P("fsdp", ("ctx", "tp"), None),
        P("fsdp", ("ctx", "tp"), None),
        P("fsdp"),
        P("fsdp", "ctx"),
        P("fsdp", ("ctx", "tp"), None),
        P(("fsdp", "ctx"), "tp"),
        P(("fsdp", "ctx"), "tp"),
        P(("fsdp", "ctx"), "tp"),
        P("tp", ("fsdp", "ctx")),
        P(("fsdp", "ctx"), "tp"),
        P(("fsdp", "ctx"), "tp"),
        P("tp", ("fsdp", "ctx")),
        P(("fsdp", "ctx", "tp"), None),
        P(None, ("fsdp", "ctx", "tp")),
        P(("fsdp", "ctx", "tp"), None),
        P(None, ("fsdp", "ctx", "tp")),
        P(),
        P(),
        P(),
        P(),
        P(),
        P(),
        P(),
        P(),
    )
    return jax.shard_map(
        on_device,
        mesh=mesh,
        in_specs=placed,
        out_specs=(
            P("fsdp", ("ctx", "tp"), None),
            P("fsdp", ("ctx", "tp"), None),
            P("fsdp", ("ctx", "tp"), None),
            P(("fsdp", "ctx"), "tp"),
            P(("fsdp", "ctx"), "tp"),
            P(("fsdp", "ctx"), "tp"),
            P("tp", ("fsdp", "ctx")),
            P(("fsdp", "ctx"), "tp"),
            P(("fsdp", "ctx"), "tp"),
            P("tp", ("fsdp", "ctx")),
            P(("fsdp", "ctx", "tp"), None),
            P(None, ("fsdp", "ctx", "tp")),
            P(("fsdp", "ctx", "tp"), None),
            P(None, ("fsdp", "ctx", "tp")),
            P(),
            P(),
            P(),
            P(),
            P(),
            P(),
            P(),
            P(),
        ),
        check_vma=False,
    )
```

profile of v0, /device:TPU:0, one launch (start us, length us, event | category | flops | bytes accessed | tf_op | source)
XLA Modules:
  0.0 3210.7 jit_solution(15251591550420104598)
XLA Ops:
  14.9 36.9 %all-gather.22.cloned.1.call-done = bf16[2048,256]{1,0:T(8,128)(2,1)} async-done(((bf16[128,256]{1,0:T(8,128)(2,1)}), bf16[2048,256]{1,0:T(8,128)(2,1)}) %all-gather.22.cloned.1.call-update) | async-done | bytes 1048592 | tf_op jit(solution)/shard_map/all_gather | solution.py:98
  51.8 33.6 %all-gather.16.cloned.1.call-done = bf16[2,256,2048]{2,1,0:T(8,128)(2,1)} async-done(((bf16[2,128,2048]{2,1,0:T(8,128)(2,1)}), bf16[2,256,2048]{2,1,0:T(8,128)(2,1)}) %all-gather.16.cloned.1.call-update) | async-done | bytes 2097168 | tf_op jit(solution)/shard_map/all_gather | solution.py:55
  90.3 35.3 %all-gather.18.cloned.1.call-done = bf16[2048,256]{1,0:T(8,128)(2,1)} async-done(((bf16[128,256]{1,0:T(8,128)(2,1)}), bf16[2048,256]{1,0:T(8,128)(2,1)}) %all-gather.18.cloned.1.call-update) | async-done | bytes 1048592 | tf_op jit(solution)/shard_map/all_gather | solution.py:99
  130.6 46.6 %all-gather.26.cloned.1.call-done = bf16[2048,1024]{1,0:T(8,128)(2,1)} async-done(((bf16[128,1024]{1,0:T(8,128)(2,1)}), bf16[2048,1024]{1,0:T(8,128)(2,1)}) %all-gather.26.cloned.1.call-update) | async-done | bytes 4194320 | tf_op jit(solution)/shard_map/all_gather | solution.py:97
  177.2 6.5 copy.73
  190.8 14.9 all-gather.24.cloned.1.call-done
  205.6 14.7 while.48
  220.4 14.7 all-gather.20.cloned.1.call-done
  235.1 7.4 while.49
  243.8 46.1 %all-gather.28.cloned.1.call-done = bf16[1024,2048]{1,0:T(8,128)(2,1)} async-done(((bf16[1024,128]{1,0:T(8,128)(2,1)}), bf16[1024,2048]{1,0:T(8,128)(2,1)}) %all-gather.28.cloned.1.call-update) | async-done | bytes 4194320 | tf_op jit(solution)/shard_map/all_gather | solution.py:100
  297.0 69.3 %all_gather.58 = bf16[2048,64]{1,0:T(8,128)(2,1)S(1)} all-gather(bf16[64,64]{1,0:T(8,128)(2,1)S(1)} %copy-done.98), channel_id=1, replica_groups=mesh['fsdp'=4,'ctx'=4,'tp'=2] {'fsdp','ctx','tp'}, dimensions={0}, use_global_device_ids=true | all-gather | bytes 270336 | tf_op jit(solution)/shard_map/all_gather | solution.py:107
  366.2 66.8 %all_gather.59 = bf16[64,2048]{0,1:T(8,128)(2,1)S(1)} all-gather(bf16[64,64]{0,1:T(8,128)(2,1)S(1)} %copy.78), channel_id=1, replica_groups=mesh['fsdp'=4,'ctx'=4,'tp'=2] {'fsdp','ctx','tp'}, dimensions={1}, use_global_device_ids=true | all-gather | bytes 270336 | tf_op jit(solution)/shard_map/all_gather | solution.py:108
  444.4 30.2 all-gather.30.cloned.1.call-done
  474.5 129.2 %all-gather.32.cloned.1.call-done = bf16[2048,4096]{1,0:T(8,128)(2,1)} async-done(((bf16[128,4096]{1,0:T(8,128)(2,1)}), bf16[2048,4096]{1,0:T(8,128)(2,1)}) %all-gather.32.cloned.1.call-update) | async-done | bytes 16777232 | tf_op jit(solution)/shard_map/all_gather | solution.py:101
  603.8 14.9 fusion.156
  618.7 112.5 %all-gather.34.cloned.1.call-done = bf16[2048,4096]{1,0:T(8,128)(2,1)} async-done(((bf16[128,4096]{1,0:T(8,128)(2,1)}), bf16[2048,4096]{1,0:T(8,128)(2,1)}) %all-gather.34.cloned.1.call-update) | async-done | bytes 16777232 | tf_op jit(solution)/shard_map/all_gather | solution.py:102
  731.2 20.1 multiply_convert_fusion.1
  751.3 110.6 %all-gather.36.cloned.1.call-done = bf16[4096,2048]{1,0:T(8,128)(2,1)} async-done(((bf16[4096,128]{1,0:T(8,128)(2,1)}), bf16[4096,2048]{1,0:T(8,128)(2,1)}) %all-gather.36.cloned.1.call-update) | async-done | bytes 16777232 | tf_op jit(solution)/shard_map/all_gather | solution.py:103
  861.9 14.5 convolution_convert_fusion
  878.1 28.7 reduce-scatter.22.cloned.1.call-done
  910.1 37.4 %all-gather.38.cloned.1.call-done = bf16[2048,256]{1,0:T(8,128)(2,1)} async-done(((bf16[64,256]{1,0:T(8,128)(2,1)}), bf16[2048,256]{1,0:T(8,128)(2,1)}) %all-gather.38.cloned.1.call-update) | async-done | bytes 1048592 | tf_op jit(solution)/shard_map/all_gather | solution.py:109
  949.9 53.3 %all-gather.40.cloned.1.call-done = bf16[256,2048]{0,1:T(8,128)(2,1)} async-done(((bf16[256,64]{0,1:T(8,128)(2,1)}), bf16[256,2048]{0,1:T(8,128)(2,1)}) %all-gather.40.cloned.1.call-update) | async-done | bytes 1048592 | tf_op jit(solution)/shard_map/all_gather | solution.py:110
  1014.6 32.0 all-gather.42.cloned.1.call-done
  1046.6 21.6 multiply_convert_fusion
  1068.2 16.4 fusion.158
  1084.7 14.3 add_convert_fusion.1
  1099.7 31.3 reduce-scatter.24.cloned.1.call-done
  1140.6 33.2 %all-gather.44.cloned.1.call-done = bf16[2,256,2048]{2,1,0:T(8,128)(2,1)} async-done(((bf16[2,128,2048]{2,1,0:T(8,128)(2,1)}), bf16[2,256,2048]{2,1,0:T(8,128)(2,1)}) %all-gather.44.cloned.1.call-update) | async-done | bytes 2097168 | tf_op jit(solution)/shard_map/all_gather | solution.py:55
  1185.8 26.6 while.50
  1220.3 6.6 fusion.160
  1226.9 12.9 reduce-scatter.28.cloned.1.call-done
  1241.0 27.3 reduce-scatter.26.cloned.1.call-done
  1308.7 17.5 fusion.168
  1327.9 17.6 fusion.166
  1345.7 17.7 fusion.167
  1366.4 37.9 %reduce-scatter.52.cloned.1.call-done = f32[64,64]{1,0:T(8,128)} async-done(((f32[2048,64]{1,0:T(8,128)}), f32[64,64]{1,0:T(8,128)}) %reduce-scatter.52.cloned.1.call-update) | async-done | bytes 16400
  1405.7 28.9 reduce-scatter.30.cloned.1.call-done
  1439.0 41.2 %all-reduce.4 = (f32[2048]{0:T(1024)}, f32[2048]{0:T(1024)}, f32[2048]{0:T(1024)}, f32[2048]{0:T(1024)}, f32[2048]{0:T(1024)}, /*index=5*/f32[2048]{0:T(1024)}, f32[256]{0:T(256)}, f32[256]{0:T(256)}) all-reduce(f32[2048]{0:T(1024)S(1)} %get-tuple-element.675, ...), channel_id=1, replica_groups=mesh['fsdp'=4,'ctx'=4,'tp'=2] {'fsdp','ctx','tp'}, use_global_device_ids=true, to_apply=%region_45.46 | all-reduce | flops 12800 | bytes 102400 | tf_op jit(solution)/shard_map/psum | solution.py:348
  1484.4 91.1 %reduce-scatter.50.cloned.1.call-done = f32[256,64]{0,1:T(8,128)} async-done(((f32[256,2048]{0,1:T(8,128)}), f32[256,64]{0,1:T(8,128)}) %reduce-scatter.50.cloned.1.call-update) | async-done | bytes 65552 | tf_op jit(solution)/shard_map/reduce_scatter | solution.py:346
  1575.6 137.3 %reduce-scatter.48.cloned.1.call-done = f32[64,256]{1,0:T(8,128)} async-done(((f32[2048,256]{1,0:T(8,128)}), f32[64,256]{1,0:T(8,128)}) %reduce-scatter.48.cloned.1.call-update) | async-done | bytes 65552 | tf_op jit(solution)/shard_map/reduce_scatter | solution.py:345
  1712.9 134.6 %reduce-scatter.46.cloned.1.call-done = f32[64,64]{1,0:T(8,128)} async-done(((f32[2048,64]{1,0:T(8,128)}), f32[64,64]{1,0:T(8,128)}) %reduce-scatter.46.cloned.1.call-update) | async-done | bytes 16400 | tf_op jit(solution)/shard_map/reduce_scatter | solution.py:343
  1847.5 62.1 %reduce-scatter.36.cloned.1.call-done = f32[128,256]{1,0:T(8,128)} async-done(((f32[2048,256]{1,0:T(8,128)}), f32[128,256]{1,0:T(8,128)}) %reduce-scatter.36.cloned.1.call-update) | async-done | bytes 131088 | tf_op jit(solution)/shard_map/reduce_scatter | solution.py:336
  1909.7 65.4 %reduce-scatter.34.cloned.1.call-done = f32[128,256]{1,0:T(8,128)} async-done(((f32[2048,256]{1,0:T(8,128)}), f32[128,256]{1,0:T(8,128)}) %reduce-scatter.34.cloned.1.call-update) | async-done | bytes 131088 | tf_op jit(solution)/shard_map/reduce_scatter | solution.py:335
  1975.1 108.4 %reduce-scatter.38.cloned.1.call-done = f32[1024,128]{1,0:T(8,128)} async-done(((f32[1024,2048]{1,0:T(8,128)}), f32[1024,128]{1,0:T(8,128)}) %reduce-scatter.38.cloned.1.call-update) | async-done | bytes 524304 | tf_op jit(solution)/shard_map/reduce_scatter | solution.py:337
  2083.5 109.0 %reduce-scatter.32.cloned.1.call-done = f32[128,1024]{1,0:T(8,128)} async-done(((f32[2048,1024]{1,0:T(8,128)}), f32[128,1024]{1,0:T(8,128)}) %reduce-scatter.32.cloned.1.call-update) | async-done | bytes 524304 | tf_op jit(solution)/shard_map/reduce_scatter | solution.py:334
  2192.4 337.4 %reduce-scatter.44.cloned.1.call-done = f32[4096,128]{1,0:T(8,128)} async-done(((f32[4096,2048]{1,0:T(8,128)}), f32[4096,128]{1,0:T(8,128)}) %reduce-scatter.44.cloned.1.call-update) | async-done | bytes 2097168 | tf_op jit(solution)/shard_map/reduce_scatter | solution.py:340
  2529.8 336.6 %reduce-scatter.40.cloned.1.call-done = f32[128,4096]{1,0:T(8,128)} async-done(((f32[2048,4096]{1,0:T(8,128)}), f32[128,4096]{1,0:T(8,128)}) %reduce-scatter.40.cloned.1.call-update) | async-done | bytes 2097168 | tf_op jit(solution)/shard_map/reduce_scatter | solution.py:338
  2866.5 336.5 %reduce-scatter.42.cloned.1.call-done = f32[128,4096]{1,0:T(8,128)} async-done(((f32[2048,4096]{1,0:T(8,128)}), f32[128,4096]{1,0:T(8,128)}) %reduce-scatter.42.cloned.1.call-update) | async-done | bytes 2097168 | tf_op jit(solution)/shard_map/reduce_scatter | solution.py:339
  (482 shorter events, 195.7 us)
Async XLA Ops:
  8.0 43.7 %all-gather.22.cloned.1.call-start = ((), (), s32[]{:S(2)}) async-start(), calls=%async_computation.20 | async-start | bytes 1114112 | tf_op jit(solution)/shard_map/all_gather | solution.py:98
  8.8 76.6 %all-gather.16.cloned.1.call-start = ((), (), s32[]{:S(2)}) async-start(), calls=%async_computation.17 | async-start | bytes 3145728 | tf_op jit(solution)/shard_map/all_gather | solution.py:55
  10.9 426.5 %copy-start.86 = (f32[2,128]{1,0:T(2,128)}, f32[2,128]{1,0:T(2,128)S(1)}, u32[]{:S(2)}) copy-start(f32[2,128]{1,0:T(2,128)S(1)} %fusion.152) | copy-start | bytes 3076
  13.5 112.1 %all-gather.18.cloned.1.call-start = ((), (), s32[]{:S(2)}) async-start(), calls=%async_computation.18 | async-start | bytes 1114112 | tf_op jit(solution)/shard_map/all_gather | solution.py:99
  14.2 163.0 %all-gather.26.cloned.1.call-start = ((), (), s32[]{:S(2)}) async-start(), calls=%async_computation.22 | async-start | bytes 4456448 | tf_op jit(solution)/shard_map/all_gather | solution.py:97
  14.8 73.3 %copy-start.108 = (f32[256]{0:T(256)S(1)}, f32[256]{0:T(256)}, u32[]{:S(2)}) copy-start(f32[256]{0:T(256)} %param.53) | copy-start | bytes 3076
  14.8 190.8 %all-gather.24.cloned.1.call-start = ((), (), s32[]{:S(2)}) async-start(), calls=%async_computation.21 | async-start | bytes 1310720 | tf_op jit(solution)/shard_map/all_gather | solution.py:148
  14.9 114.7 %copy-start.73 = (f32[2,256]{1,0:T(2,128)}, f32[2,256]{1,0:T(2,128)S(1)}, u32[]{:S(2)}) copy-start(f32[2,256]{1,0:T(2,128)S(1)} %convert_element_type.191) | copy-start | bytes 6148
  14.9 114.7 %copy-start.114 = (f32[128]{0:T(128)}, f32[128]{0:T(128)S(1)}, u32[]{:S(2)}) copy-start(f32[128]{0:T(128)S(1)} %multiply_power_fusion) | copy-start | bytes 1540
  90.2 144.9 %all-gather.20.cloned.1.call-start = ((), (), s32[]{:S(2)}) async-start(), calls=%async_computation.19 | async-start | bytes 1310720 | tf_op jit(solution)/shard_map/all_gather | solution.py:149
  127.6 56.1 %copy-start.28 = (f32[512,256]{1,0:T(8,128)}, f32[512,256]{1,0:T(8,128)S(1)}, u32[]{:S(2)}) copy-start(f32[512,256]{1,0:T(8,128)S(1)} %get-tuple-element.774) | copy-start | bytes 1572868
  127.7 56.0 %copy-start.92 = (f32[2,256]{1,0:T(2,128)}, f32[2,256]{1,0:T(2,128)S(1)}, u32[]{:S(2)}) copy-start(f32[2,256]{1,0:T(2,128)S(1)} %add.377) | copy-start | bytes 6148
  127.7 56.0 %copy-start.88 = (f32[2,256]{1,0:T(2,128)}, f32[2,256]{1,0:T(2,128)S(1)}, u32[]{:S(2)}) copy-start(f32[2,256]{1,0:T(2,128)S(1)} %rsqrt.93) | copy-start | bytes 6148
  128.6 161.4 %all-gather.28.cloned.1.call-start = ((), (), s32[]{:S(2)}) async-start(), calls=%async_computation.23 | async-start | bytes 4456448 | tf_op jit(solution)/shard_map/all_gather | solution.py:100
  129.3 306.0 %reduce-scatter.20.cloned.1.call-start = ((), (), s32[]{:S(2)}) async-start(), calls=%async_computation.24 | async-start | bytes 3145728 | tf_op jit(solution)/shard_map/reduce_scatter | solution.py:59
  130.5 59.2 %copy-start.41 = (f32[2,256,128]{1,2,0:T(8,128)}, f32[2,256,128]{1,2,0:T(8,128)S(1)}, u32[]{:S(2)}) copy-start(f32[2,256,128]{1,2,0:T(8,128)S(1)} %get-tuple-element.767) | copy-start | bytes 786436
  130.6 59.2 %copy-start.43 = (f32[2,256,128]{1,2,0:T(8,128)}, f32[2,256,128]{1,2,0:T(8,128)S(1)}, u32[]{:S(2)}) copy-start(f32[2,256,128]{1,2,0:T(8,128)S(1)} %get-tuple-element.768) | copy-start | bytes 786436
  296.2 136.8 %copy-start.19 = (bf16[2,128,2048]{2,1,0:T(8,128)(2,1)S(1)}, bf16[2,128,2048]{2,1,0:T(8,128)(2,1)}, u32[]{:S(2)}) copy-start(bf16[2,128,2048]{2,1,0:T(8,128)(2,1)} %fusion.97) | copy-start | bytes 3145732
  296.2 178.3 %all-gather.30.cloned.1.call-start = ((), (), s32[]{:S(2)}) async-start(), calls=%async_computation.25 | async-start | bytes 3145728 | tf_op jit(solution)/shard_map/all_gather | solution.py:55
  366.2 69.1 %copy-start.30 = (bf16[2048,64]{1,0:T(8,128)(2,1)}, bf16[2048,64]{1,0:T(8,128)(2,1)S(1)}, u32[]{:S(2)}) copy-start(bf16[2048,64]{1,0:T(8,128)(2,1)S(1)} %all_gather.58) | copy-start | bytes 786436
  442.4 161.3 %all-gather.32.cloned.1.call-start = ((), (), s32[]{:S(2)}) async-start(), calls=%async_computation.26 | async-start | bytes 17825792 | tf_op jit(solution)/shard_map/all_gather | solution.py:101
  443.0 288.2 %all-gather.34.cloned.1.call-start = ((), (), s32[]{:S(2)}) async-start(), calls=%async_computation.27 | async-start | bytes 17825792 | tf_op jit(solution)/shard_map/all_gather | solution.py:102
  443.7 418.2 %all-gather.36.cloned.1.call-start = ((), (), s32[]{:S(2)}) async-start(), calls=%async_computation.28 | async-start | bytes 17825792 | tf_op jit(solution)/shard_map/all_gather | solution.py:103
  444.3 462.5 %reduce-scatter.22.cloned.1.call-start = ((), (), s32[]{:S(2)}) async-start(), calls=%async_computation.29 | async-start | bytes 3145728 | tf_op jit(solution)/shard_map/reduce_scatter | solution.py:59
  876.5 71.0 %all-gather.38.cloned.1.call-start = ((), (), s32[]{:S(2)}) async-start(), calls=%async_computation.30 | async-start | bytes 1081344 | tf_op jit(solution)/shard_map/all_gather | solution.py:109
  877.1 126.2 %all-gather.40.cloned.1.call-start = ((), (), s32[]{:S(2)}) async-start(), calls=%async_computation.31 | async-start | bytes 1081344 | tf_op jit(solution)/shard_map/all_gather | solution.py:110
  877.7 168.9 %all-gather.42.cloned.1.call-start = ((), (), s32[]{:S(2)}) async-start(), calls=%async_computation.32 | async-start | bytes 3145728 | tf_op jit(solution)/shard_map/all_gather | solution.py:55
  949.9 55.5 %copy-start.55 = (bf16[256,256]{1,0:T(8,128)(2,1)}, bf16[256,256]{1,0:T(8,128)(2,1)S(1)}, u32[]{:S(2)}) copy-start(bf16[256,256]{1,0:T(8,128)(2,1)S(1)} %get-tuple-element.783) | copy-start | bytes 393220
  1014.4 116.6 %reduce-scatter.24.cloned.1.call-start = ((), (), s32[]{:S(2)}) async-start(), calls=%async_computation.33 | async-start | bytes 3145728 | tf_op jit(solution)/shard_map/reduce_scatter | solution.py:59
  1099.0 74.8 %all-gather.44.cloned.1.call-start = ((), (), s32[]{:S(2)}) async-start(), calls=%async_computation.34 | async-start | bytes 3145728 | tf_op jit(solution)/shard_map/all_gather | solution.py:55
  1140.5 99.2 %reduce-scatter.28.cloned.1.call-start = ((), (), s32[]{:S(2)}) async-start(), calls=%async_computation.36 | async-start | bytes 1310720 | tf_op jit(solution)/shard_map/reduce_scatter | solution.py:312
  1212.4 55.8 %reduce-scatter.26.cloned.1.call-start = ((), (), s32[]{:S(2)}) async-start(), calls=%async_computation.35 | async-start | bytes 1310720 | tf_op jit(solution)/shard_map/reduce_scatter | solution.py:309
  1213.0 191.3 %reduce-scatter.52.cloned.1.call-start = ((), (), s32[]{:S(2)}) async-start(), calls=%async_computation.48 | async-start | bytes 1081344
  1215.2 219.4 %reduce-scatter.30.cloned.1.call-start = ((), (), s32[]{:S(2)}) async-start(), calls=%async_computation.37 | async-start | bytes 3145728 | tf_op jit(solution)/shard_map/reduce_scatter | solution.py:59
  1276.3 299.3 %reduce-scatter.50.cloned.1.call-start = ((), (), s32[]{:S(2)}) async-start(), calls=%async_computation.47 | async-start | bytes 2162688 | tf_op jit(solution)/shard_map/reduce_scatter | solution.py:346
  1279.4 433.5 %reduce-scatter.48.cloned.1.call-start = ((), (), s32[]{:S(2)}) async-start(), calls=%async_computation.46 | async-start | bytes 2162688 | tf_op jit(solution)/shard_map/reduce_scatter | solution.py:345
  1281.3 566.2 %reduce-scatter.46.cloned.1.call-start = ((), (), s32[]{:S(2)}) async-start(), calls=%async_computation.45 | async-start | bytes 1081344 | tf_op jit(solution)/shard_map/reduce_scatter | solution.py:343
  1284.8 624.8 %reduce-scatter.36.cloned.1.call-start = ((), (), s32[]{:S(2)}) async-start(), calls=%async_computation.40 | async-start | bytes 2228224 | tf_op jit(solution)/shard_map/reduce_scatter | solution.py:336
  1287.0 688.1 %reduce-scatter.34.cloned.1.call-start = ((), (), s32[]{:S(2)}) async-start(), calls=%async_computation.39 | async-start | bytes 2228224 | tf_op jit(solution)/shard_map/reduce_scatter | solution.py:335
  1290.0 793.5 %reduce-scatter.38.cloned.1.call-start = ((), (), s32[]{:S(2)}) async-start(), calls=%async_computation.41 | async-start | bytes 8912896 | tf_op jit(solution)/shard_map/reduce_scatter | solution.py:337
  1300.2 892.2 %reduce-scatter.32.cloned.1.call-start = ((), (), s32[]{:S(2)}) async-start(), calls=%async_computation.38 | async-start | bytes 8912896 | tf_op jit(solution)/shard_map/reduce_scatter | solution.py:334
  1307.1 1222.7 %reduce-scatter.44.cloned.1.call-start = ((), (), s32[]{:S(2)}) async-start(), calls=%async_computation.44 | async-start | bytes 35651584 | tf_op jit(solution)/shard_map/reduce_scatter | solution.py:340
  1326.3 1540.2 %reduce-scatter.40.cloned.1.call-start = ((), (), s32[]{:S(2)}) async-start(), calls=%async_computation.42 | async-start | bytes 35651584 | tf_op jit(solution)/shard_map/reduce_scatter | solution.py:338
  1345.4 1857.6 %reduce-scatter.42.cloned.1.call-start = ((), (), s32[]{:S(2)}) async-start(), calls=%async_computation.43 | async-start | bytes 35651584 | tf_op jit(solution)/shard_map/reduce_scatter | solution.py:339
  1363.4 71.2 %copy-start.11 = (bf16[2,128,2048]{2,1,0:T(8,128)(2,1)S(1)}, bf16[2,128,2048]{2,1,0:T(8,128)(2,1)}, u32[]{:S(2)}) copy-start(bf16[2,128,2048]{2,1,0:T(8,128)(2,1)} %param.30) | copy-start | bytes 3145732
  1363.4 71.2 %copy-start.7 = (f32[2,128,2048]{2,1,0:T(8,128)S(1)}, f32[2,128,2048]{2,1,0:T(8,128)}, u32[]{:S(2)}) copy-start(f32[2,128,2048]{2,1,0:T(8,128)} %copy-done.6) | copy-start | bytes 6291460
  1363.4 71.2 %copy-start.64 = (f32[2048]{0:T(1024)S(1)}, f32[2048]{0:T(1024)}, u32[]{:S(2)}) copy-start(f32[2048]{0:T(1024)} %param.46) | copy-start | bytes 24580
  1363.5 71.2 %copy-start.87 = (f32[2,128]{1,0:T(2,128)S(1)}, f32[2,128]{1,0:T(2,128)}, u32[]{:S(2)}) copy-start(f32[2,128]{1,0:T(2,128)} %copy-done.86) | copy-start | bytes 3076
  (116 other events, 1293.3 us)
Sparse Core Ops, SparseCore 0:
  11.1 40.6 all-gather.21
  53.3 32.0 all-gather.15
  87.6 37.9 all-gather.17
  127.7 49.4 all-gather.25
  179.2 26.4 all-gather.23
  207.6 27.4 all-gather.19
  237.2 52.7 all-gather.27
  296.3 34.7 reduce-scatter.19
  442.5 31.9 all-gather.29
  476.8 126.8 all-gather.31
  606.2 124.9 all-gather.33
  733.4 128.5 all-gather.35
  876.6 30.1 reduce-scatter.21
  1014.5 32.0 all-gather.41
  1099.1 31.8 reduce-scatter.23
  1140.7 33.0 all-gather.43
  1212.6 27.1 reduce-scatter.27
  1242.5 25.7 reduce-scatter.25
  1270.6 133.6 reduce-scatter.51
  1406.4 28.1 reduce-scatter.29
  1437.6 137.9 reduce-scatter.49
  1578.4 134.4 reduce-scatter.47
  1715.8 131.6 reduce-scatter.45
  1851.7 57.9 reduce-scatter.35
  1914.4 60.6 reduce-scatter.33
  1979.6 103.8 reduce-scatter.37
  2088.0 104.4 reduce-scatter.31
  2197.3 332.5 reduce-scatter.43
  2534.7 331.7 reduce-scatter.39
  2871.1 331.8 reduce-scatter.41
Sparse Core Ops, SparseCore 1:
  880.0 67.4 all-gather.37
  950.5 52.7 all-gather.39
where the time goes:
time: 3220 us; the launch traced here: 3210 us
  waiting for transfers between devices  2660 us (83%)
  matrix products  253 us (8%)
  blocking collectives  177 us (5%)
  other arithmetic  57.1 us (2%)
  local copies, waits for them, and re-layouts  44.5 us (1%)
    reduce_scatter x1, waiting for transfers between devices, on_device(): lax.psum_scatter(down_grad, ('fsdp', 'ctx'), scatter_dimension=1, tiled=T...  337 us
    reduce_scatter x1, waiting for transfers between devices, on_device(): lax.psum_scatter(gate_grad, ('fsdp', 'ctx'), scatter_dimension=0, tiled=T...  337 us
    reduce_scatter x1, waiting for transfers between devices, on_device(): lax.psum_scatter(up_grad, ('fsdp', 'ctx'), scatter_dimension=0, tiled=True)  337 us
    dot_general x32, matrix products, matmul(): return jnp.dot(left, right, preferred_element_type=jnp.float32)  219 us
    reduce_scatter x1, waiting for transfers between devices, on_device(): lax.psum_scatter(side_gate_grad, ('fsdp', 'ctx', 'tp'), scatter_dimension...  137 us
    reduce_scatter x1, waiting for transfers between devices, on_device(): lax.psum_scatter(laurel_left_grad, ('fsdp', 'ctx', 'tp'), scatter_dimensi...  135 us
    all_gather x1, waiting for transfers between devices, on_device(): lax.all_gather(gate_weight, ('fsdp', 'ctx'), axis=0, tiled=True)  129 us
    all_gather x4, waiting for transfers between devices, gather_rows(): return lax.all_gather(value, 'tp', axis=1, tiled=True)  129 us
  transfers between devices with their start and end apart: 32, of which 31 were waited for; matrix products, arithmetic and copies ran while one was open for 6% of the time, Pallas kernels for 0%

commit v1 on v0

v1 whole, which is shorter than its diff:
```python
import jax
import jax.numpy as jnp
from jax import lax
from jax.sharding import PartitionSpec as P

HEAD_SIZE = 256


EPS = 1e-06
THETA = 1000000.0
MASKED = -1e30
SQRT_HALF = 0.7071067811865476


def scaled_norm(value, gain):
    return value * lax.rsqrt(jnp.mean(value * value, axis=-1, keepdims=True) + EPS) * gain


def plain_norm(value):
    return value * lax.rsqrt(jnp.mean(value * value, axis=-1, keepdims=True) + EPS)


def rotate(value, positions):
    half = value.shape[-1] // 2
    freq = THETA ** (-(jnp.arange(half, dtype=jnp.float32) * 2.0) / value.shape[-1])
    angle = positions.astype(jnp.float32)[..., None] * freq
    cosine = jnp.cos(angle)[..., None, :]
    sine = jnp.sin(angle)[..., None, :]
    first = value[..., :half]
    second = value[..., half:]
    return jnp.concatenate(
        [first * cosine - second * sine, second * cosine + first * sine], axis=-1
    )


def geglu(gate, upward):
    return jax.nn.gelu(gate, approximate=True) * upward


def attention_mix(inputs, attention, normed, laurel, attention_gain, laurel_gain):
    return (
        inputs + scaled_norm(attention, attention_gain) + normed + scaled_norm(laurel, laurel_gain)
    ) * SQRT_HALF


def residual_mix(residual, branch, gain):
    return residual + scaled_norm(branch, gain)


def matmul(left, right):
    return jnp.dot(left, right, preferred_element_type=jnp.float32)


def matmul_t(left, right):
    return lax.dot_general(
        left, right, (((1,), (1,)), ((), ())), preferred_element_type=jnp.float32
    )


def low(value):
    return value.astype(jnp.bfloat16)


def wide(value):
    return value.astype(jnp.float32)


def core_swap(value):
    size = lax.axis_size("fsdp")
    return lax.ppermute(value, "fsdp", [(i, i ^ 1) for i in range(size)])


def x_shift(value, step=1):
    size = lax.axis_size("fsdp")
    return lax.ppermute(value, "fsdp", [(i, (i + 2 * step) % size) for i in range(size)])


def z_shift(value, step=1):
    size = lax.axis_size("ctx")
    return lax.ppermute(value, "ctx", [(i, (i + step) % size) for i in range(size)])


def y_swap(value):
    return lax.ppermute(value, "tp", [(0, 1), (1, 0)])


def by_core(core, mine, other, axis):
    first = jnp.where(core == 0, mine, other)
    second = jnp.where(core == 0, other, mine)
    return jnp.stack([first, second], axis)


class Place:
    def __init__(self):
        self.chips = lax.axis_size("fsdp") // 2
        self.depth = lax.axis_size("ctx")
        index = lax.axis_index("fsdp")
        self.core = index % 2
        self.x = index // 2
        self.z = lax.axis_index("ctx")
        self.y = lax.axis_index("tp")

    def source(self, dx, dz):
        return (self.x - dx) % self.chips, (self.z - dz) % self.depth


def gather_pieces(place, shard):
    pieces = {(0, 0): shard}
    for dz in range(1, place.depth):
        pieces[0, dz] = z_shift(pieces[0, dz - 1])
    for dz in range(place.depth):
        for dx in range(1, place.chips):
            pieces[dx, dz] = x_shift(pieces[dx - 1, dz])
    return pieces


def assemble(place, pieces, cores):
    piece = pieces[0, 0]
    if cores:
        whole = jnp.zeros((place.chips, 2, place.depth) + piece.shape[1:], piece.dtype)
    else:
        whole = jnp.zeros((place.chips, place.depth) + piece.shape, piece.dtype)
    for (dx, dz), piece in pieces.items():
        x, z = place.source(dx, dz)
        if cores:
            whole = lax.dynamic_update_slice(whole, piece[None, :, None], (x, 0, z, 0, 0))
        else:
            whole = lax.dynamic_update_slice(whole, piece[None, None], (x, z, 0, 0))
    return whole


def scatter_pieces(place, partial):
    passing = None
    for step in range(1, place.depth + 1):
        dz = step % place.depth
        arrived = None
        for dx in range(1, place.chips):
            value = partial(dx, dz)
            if arrived is not None:
                value = value + wide(arrived)
            arrived = x_shift(low(value))
        value = partial(0, dz)
        if arrived is not None:
            value = value + wide(arrived)
        if passing is not None:
            value = value + wide(passing)
        if dz == 0:
            return value
        passing = z_shift(low(value))


def sum_everywhere(place, value):
    value = value + core_swap(value)
    value = value + y_swap(value)
    value = sum([x_shift(value, step) for step in range(1, place.chips)], value)
    return sum([z_shift(value, step) for step in range(1, place.depth)], value)


def split_core(place, shard):
    rows, columns = shard.shape
    halves = shard.reshape(rows, 2, columns // 2)
    kept = lax.dynamic_index_in_dim(halves, place.core, 1, False)
    sent = lax.dynamic_index_in_dim(halves, 1 - place.core, 1, False)
    return by_core(place.core, kept, core_swap(sent), 0)


def join_core(place, value):
    kept = lax.dynamic_index_in_dim(value, place.core, 0, False)
    sent = lax.dynamic_index_in_dim(value, 1 - place.core, 0, False)
    both = by_core(place.core, kept, core_swap(sent), 1)
    return both.reshape(both.shape[0], -1)


def share_four(value):
    pair = jnp.concatenate([value, y_swap(value)], 0)
    return jnp.concatenate([pair, core_swap(pair)], 0)


def sum_four(value):
    rows = value.shape[0] // 4
    pair = value[: 2 * rows] + wide(core_swap(low(value[2 * rows :])))
    return pair[:rows] + wide(y_swap(low(pair[rows:])))


def share_two(value):
    return jnp.concatenate([value, y_swap(value)], 1)


def sum_two(value):
    rows = value.shape[1] // 2
    return value[:, :rows] + wide(y_swap(low(value[:, rows:])))


def columns_of(place, value, dx, dz, core, rows):
    x, z = place.source(dx, dz)
    start = ((x * 2 + core) * place.depth + z) * rows
    return lax.dynamic_slice_in_dim(value, start, rows, 1)


def on_device(
    tokens,
    side_input,
    prefix,
    positions,
    cotangent,
    query_weight,
    key_matrix,
    value_matrix,
    out_weight,
    gate_weight,
    up_weight,
    down_weight,
    laurel_left,
    laurel_right,
    side_gate_weight,
    side_out_weight,
    input_gain,
    laurel_gain,
    attention_gain,
    hidden_in_gain,
    hidden_out_gain,
    side_gain,
    query_gain,
    key_gain,
):
    place = Place()
    chips, depth = place.chips, place.depth
    sequences, own_rows, width = tokens.shape
    side_width = side_input.shape[2]
    rank = laurel_left.shape[1]
    block_rows = positions.shape[1]
    shard_rows = query_weight.shape[0]
    query_width = query_weight.shape[1]
    key_width = key_matrix.shape[1]
    hidden_half = gate_weight.shape[1] // 2
    local_heads = query_width // HEAD_SIZE
    local_groups = key_width // HEAD_SIZE
    per_group = local_heads // local_groups

    near = place.y * own_rows + jnp.arange(own_rows, dtype=jnp.int32)
    far = (1 - place.y) * own_rows + jnp.arange(own_rows, dtype=jnp.int32)
    block_index = jnp.concatenate([near, far])
    row_index = place.z * block_rows + block_index
    near_positions = lax.dynamic_slice_in_dim(positions, place.y * own_rows, own_rows, 1)
    far_positions = lax.dynamic_slice_in_dim(positions, (1 - place.y) * own_rows, own_rows, 1)
    positions = jnp.concatenate([near_positions, far_positions], 1)

    mixed_shard = jnp.concatenate([query_weight, key_matrix, value_matrix], 1)
    half = assemble(place, gather_pieces(place, mixed_shard), False)
    mixed_full = by_core(place.core, half, core_swap(half), 1).reshape(width, -1)
    half = assemble(place, gather_pieces(place, out_weight.T), False)
    out_full = by_core(place.core, half, core_swap(half), 1).reshape(width, query_width)

    small = jnp.concatenate(
        [laurel_left, laurel_right.T, side_gate_weight, side_out_weight.T], 1
    )
    small_rows = small.shape[0]
    small = jnp.where(
        place.y == 0,
        jnp.concatenate([small, y_swap(small)], 0),
        jnp.concatenate([y_swap(small), small], 0),
    )
    half = assemble(place, gather_pieces(place, small), False)
    small_full = by_core(place.core, half, core_swap(half), 1).reshape(width, -1)
    laurel_down = small_full[:, :rank]
    laurel_up_t = small_full[:, rank : 2 * rank]
    side_gate_full = small_full[:, 2 * rank : 2 * rank + side_width]
    side_out_t = small_full[:, 2 * rank + side_width :]

    gate_up = jnp.concatenate(
        [split_core(place, gate_weight), split_core(place, up_weight)], 2
    )
    gate_up_full = assemble(place, gather_pieces(place, gate_up), True).reshape(width, -1)
    down_t = split_core(place, down_weight.T)
    down_full_t = assemble(place, gather_pieces(place, down_t), True).reshape(width, -1)

    inputs = tokens.astype(jnp.float32)
    normed, input_pull = jax.vjp(scaled_norm, inputs, input_gain)
    normed_reduced = normed.astype(jnp.bfloat16)
    flat_in = share_two(normed_reduced).reshape(-1, width)
    mixed_raw = matmul(flat_in, mixed_full)
    query_raw = mixed_raw[:, :query_width]
    key_unrotated = mixed_raw[:, query_width : query_width + key_width]
    value_unprojected = mixed_raw[:, query_width + key_width :]

    def heads_of(query_part, key_part, value_part, gain_query, gain_key):
        rotated_queries = rotate(
            scaled_norm(
                query_part.reshape(sequences, block_rows, local_heads, HEAD_SIZE), gain_query
            ),
            positions,
        )
        rotated_keys = rotate(
            scaled_norm(key_part.reshape(sequences, block_rows, local_groups, HEAD_SIZE), gain_key),
            positions,
        )
        normed_values = plain_norm(
            value_part.reshape(sequences, block_rows, local_groups, HEAD_SIZE)
        )
        return (rotated_queries, rotated_keys, normed_values)

    (query_rows, keys, values), heads_pull = jax.vjp(
        heads_of, query_raw, key_unrotated, value_unprojected, query_gain, key_gain
    )
    query_low = query_rows.astype(jnp.bfloat16).reshape(
        sequences, block_rows, local_groups, per_group, HEAD_SIZE
    )
    both = jnp.concatenate([low(keys), low(values)], 2)
    pieces = [both]
    for dz in range(1, depth):
        pieces.append(z_shift(pieces[-1]))
    key_index = jnp.concatenate(
        [((place.z - dz) % depth) * block_rows + block_index for dz in range(depth)]
    )
    everyone = jnp.concatenate(pieces, 1)
    all_keys = everyone[:, :, :local_groups]
    all_values = everyone[:, :, local_groups:]
    visible = (key_index[None, None, :] <= row_index[None, :, None]) | (
        key_index[None, None, :] < prefix[:, None, None]
    )

    def all_scores():
        scores = jnp.einsum(
            "sbkgd,sjkd->skgbj", query_low, all_keys, preferred_element_type=jnp.float32
        )
        return jnp.where(visible[:, None, None], scores, MASKED)

    scores = all_scores()
    highest = jnp.max(scores, axis=-1, keepdims=True)
    log_total = highest + jnp.log(jnp.sum(jnp.exp(scores - highest), axis=-1, keepdims=True))
    probs = jnp.exp(scores - log_total)
    probs_low = low(probs)
    attended = jnp.einsum(
        "skgbj,sjkd->sbkgd", probs_low, all_values, preferred_element_type=jnp.float32
    )
    attended_low = attended.astype(jnp.bfloat16).reshape(
        sequences * block_rows, local_heads * HEAD_SIZE
    )
    attention = sum_two(matmul_t(attended_low, out_full).reshape(sequences, block_rows, width))
    flat_normed = normed_reduced.reshape(-1, width)
    laurel_mid = matmul(flat_normed, laurel_down).astype(jnp.bfloat16)
    laurel_out = matmul_t(laurel_mid, laurel_up_t).reshape(sequences, own_rows, width)
    mixed, mix_pull = jax.vjp(
        attention_mix, inputs, attention, normed, laurel_out, attention_gain, laurel_gain
    )
    hidden_in, pre_pull = jax.vjp(scaled_norm, mixed, hidden_in_gain)
    hidden_block = share_four(low(hidden_in).reshape(-1, width))
    gate_up_out = matmul(hidden_block, gate_up_full)
    hidden, hidden_pull = jax.vjp(
        geglu, gate_up_out[:, :hidden_half], gate_up_out[:, hidden_half:]
    )
    hidden_low = low(hidden)
    hidden_out = sum_four(matmul_t(hidden_low, down_full_t)).reshape(inputs.shape)
    layer_out, post_pull = jax.vjp(residual_mix, mixed, hidden_out, hidden_out_gain)
    layer_low = layer_out.astype(jnp.bfloat16).reshape(-1, width)
    side_pre = matmul(layer_low, side_gate_full)
    side_act, side_pull = jax.vjp(
        geglu, side_pre, side_input.astype(jnp.float32).reshape(-1, side_width)
    )
    side_low = side_act.astype(jnp.bfloat16)
    projected = matmul_t(side_low, side_out_t).reshape(sequences, own_rows, width)
    result, final_pull = jax.vjp(residual_mix, layer_out, projected, side_gain)
    out_grad_first, projected_grad, side_gain_grad = final_pull(cotangent.astype(jnp.float32))
    projected_low = projected_grad.astype(jnp.bfloat16).reshape(-1, width)
    side_out_grad_t = matmul(projected_low.T, side_low)
    side_grad = matmul(projected_low, side_out_t)
    side_pre_grad, side_input_grad = side_pull(side_grad)
    side_pre_low = side_pre_grad.astype(jnp.bfloat16)
    side_gate_grad = matmul(layer_low.T, side_pre_low)
    layer_grad = out_grad_first + matmul_t(side_pre_low, side_gate_full).reshape(inputs.shape)
    mixed_grad_first, hidden_out_grad, hidden_out_gain_grad = post_pull(layer_grad)
    hidden_out_block = share_four(low(hidden_out_grad).reshape(-1, width))

    def cores_columns(value, dx, dz):
        return jnp.concatenate(
            [columns_of(place, value, dx, dz, core, shard_rows) for core in range(2)], 1
        )

    down_grad_t = join_core(
        place,
        scatter_pieces(
            place, lambda dx, dz: matmul(cores_columns(hidden_out_block, dx, dz).T, hidden_low)
        ).reshape(2, shard_rows, -1),
    )
    hidden_grad = matmul(hidden_out_block, down_full_t)
    gate_grad_full, up_grad_full = hidden_pull(hidden_grad)
    gate_up_low = jnp.concatenate([low(gate_grad_full), low(up_grad_full)], 1)
    gate_up_grad = scatter_pieces(
        place, lambda dx, dz: matmul(cores_columns(hidden_block, dx, dz).T, gate_up_low)
    ).reshape(2, shard_rows, -1)
    gate_grad = join_core(place, gate_up_grad[:, :, :hidden_half])
    up_grad = join_core(place, gate_up_grad[:, :, hidden_half:])
    hidden_in_sum = sum_four(matmul_t(gate_up_low, gate_up_full)).reshape(inputs.shape)
    mixed_grad_second, hidden_in_gain_grad = pre_pull(hidden_in_sum)
    mixed_grad = mixed_grad_first + mixed_grad_second
    (
        inputs_grad_first,
        attention_grad,
        normed_grad_first,
        laurel_grad,
        attention_gain_grad,
        laurel_gain_grad,
    ) = mix_pull(mixed_grad)
    attention_block = share_two(low(attention_grad)).reshape(-1, width)

    def scatter_attention(left, right):
        def rows(core, dx, dz):
            return columns_of(place, left, dx, dz, core, shard_rows)

        order = [(dx, dz) for dz in range(depth) for dx in range(chips)]
        sent = jnp.concatenate([rows(1 - place.core, dx, dz) for dx, dz in order], 1)
        arrived = core_swap(low(matmul(sent.T, right)))
        arrived = arrived.reshape(len(order), shard_rows, right.shape[1])
        return scatter_pieces(
            place,
            lambda dx, dz: matmul(rows(place.core, dx, dz).T, right)
            + wide(arrived[order.index((dx, dz))]),
        )

    out_grad_t = scatter_attention(attention_block, attended_low)
    attended_grad = (
        matmul(attention_block, out_full)
        .astype(jnp.bfloat16)
        .reshape(sequences, block_rows, local_groups, per_group, HEAD_SIZE)
    )
    laurel_low = laurel_grad.astype(jnp.bfloat16).reshape(-1, width)
    laurel_right_grad_t = matmul(laurel_low.T, laurel_mid)
    laurel_mid_grad = matmul(laurel_low, laurel_up_t).astype(jnp.bfloat16)
    laurel_left_grad = matmul(flat_normed.T, laurel_mid_grad)
    normed_grad_second = matmul_t(laurel_mid_grad, laurel_down).reshape(inputs.shape)

    def scatter_small(value):
        value = value.reshape(chips, 2, depth, 2 * small_rows, -1)
        kept = lax.dynamic_index_in_dim(value, place.core, 1, False)
        sent = lax.dynamic_index_in_dim(value, 1 - place.core, 1, False)
        value = kept + wide(core_swap(low(sent)))

        def partial(dx, dz):
            x, z = place.source(dx, dz)
            return lax.dynamic_slice(
                value, (x, z, 0, 0), (1, 1) + value.shape[2:]
            ).reshape(value.shape[2:])

        own = scatter_pieces(place, partial).reshape(2, small_rows, -1)
        kept = lax.dynamic_index_in_dim(own, place.y, 0, False)
        sent = lax.dynamic_index_in_dim(own, 1 - place.y, 0, False)
        return kept + wide(y_swap(low(sent)))

    side_grads = scatter_small(jnp.concatenate([side_gate_grad, side_out_grad_t], 1))
    laurel_grads = scatter_small(jnp.concatenate([laurel_left_grad, laurel_right_grad_t], 1))

    delta = jnp.transpose(
        jnp.sum(attended_grad.astype(jnp.float32) * attended, axis=-1), (0, 2, 3, 1)
    )
    probs = jnp.exp(all_scores() - log_total)
    probs_grad = jnp.einsum(
        "sbkgd,sjkd->skgbj", attended_grad, all_values, preferred_element_type=jnp.float32
    )
    scores_grad = low(probs * (probs_grad - delta[..., None]))
    query_grad = jnp.einsum(
        "skgbj,sjkd->sbkgd", scores_grad, all_keys, preferred_element_type=jnp.float32
    )
    keys_grad = jnp.einsum(
        "skgbj,sbkgd->sjkd", scores_grad, query_low, preferred_element_type=jnp.float32
    )
    values_grad = jnp.einsum(
        "skgbj,sbkgd->sjkd", low(probs), attended_grad, preferred_element_type=jnp.float32
    )
    both_grad = jnp.concatenate([keys_grad, values_grad], 2)
    passing = None
    for step in range(1, depth + 1):
        dz = step % depth
        value = both_grad[:, dz * block_rows : (dz + 1) * block_rows]
        if passing is not None:
            value = value + wide(passing)
        if dz:
            passing = z_shift(low(value))
    query_raw_grad, key_raw_grad, value_raw_grad, query_gain_grad, key_gain_grad = heads_pull(
        (
            query_grad.reshape(sequences, block_rows, local_heads, HEAD_SIZE),
            value[:, :, :local_groups],
            value[:, :, local_groups:],
        )
    )
    mixed_low = jnp.concatenate(
        [low(query_raw_grad), low(key_raw_grad), low(value_raw_grad)], 1
    )
    mixed_weight_grad = scatter_attention(flat_in, mixed_low)
    block_in_grad = matmul_t(mixed_low, mixed_full).reshape(sequences, block_rows, width)
    normed_grad = normed_grad_first + normed_grad_second + sum_two(block_in_grad)
    inputs_grad_second, input_gain_grad = input_pull(normed_grad)
    tokens_grad = inputs_grad_first + inputs_grad_second
    early = sum_everywhere(
        place,
        jnp.stack(
            [
                laurel_gain_grad,
                attention_gain_grad,
                hidden_in_gain_grad,
                hidden_out_gain_grad,
                side_gain_grad,
            ]
        ),
    )
    late = sum_everywhere(
        place, jnp.concatenate([input_gain_grad, query_gain_grad, key_gain_grad])
    )
    gain_grads = (late[:width],) + tuple(early) + (
        late[width : width + HEAD_SIZE],
        late[width + HEAD_SIZE :],
    )
    side_input_grad = side_input_grad.reshape(sequences, own_rows, side_width)
    return (
        (result.astype(jnp.bfloat16), tokens_grad, side_input_grad)
        + (
            mixed_weight_grad[:, :query_width],
            mixed_weight_grad[:, query_width : query_width + key_width],
            mixed_weight_grad[:, query_width + key_width :],
            out_grad_t.T,
            gate_grad,
            up_grad,
            down_grad_t.T,
        )
        + (
            laurel_grads[:, :rank],
            laurel_grads[:, rank:].T,
            side_grads[:, :side_width],
            side_grads[:, side_width:].T,
        )
        + gain_grads
    )


def solution(mesh):
    placed = (
        P("fsdp", ("ctx", "tp"), None),
        P("fsdp", ("ctx", "tp"), None),
        P("fsdp"),
        P("fsdp", "ctx"),
        P("fsdp", ("ctx", "tp"), None),
        P(("fsdp", "ctx"), "tp"),
        P(("fsdp", "ctx"), "tp"),
        P(("fsdp", "ctx"), "tp"),
        P("tp", ("fsdp", "ctx")),
        P(("fsdp", "ctx"), "tp"),
        P(("fsdp", "ctx"), "tp"),
        P("tp", ("fsdp", "ctx")),
        P(("fsdp", "ctx", "tp"), None),
        P(None, ("fsdp", "ctx", "tp")),
        P(("fsdp", "ctx", "tp"), None),
        P(None, ("fsdp", "ctx", "tp")),
        P(),
        P(),
        P(),
        P(),
        P(),
        P(),
        P(),
        P(),
    )
    return jax.shard_map(
        on_device,
        mesh=mesh,
        in_specs=placed,
        out_specs=(
            P("fsdp", ("ctx", "tp"), None),
            P("fsdp", ("ctx", "tp"), None),
            P("fsdp", ("ctx", "tp"), None),
            P(("fsdp", "ctx"), "tp"),
            P(("fsdp", "ctx"), "tp"),
            P(("fsdp", "ctx"), "tp"),
            P("tp", ("fsdp", "ctx")),
            P(("fsdp", "ctx"), "tp"),
            P(("fsdp", "ctx"), "tp"),
            P("tp", ("fsdp", "ctx")),
            P(("fsdp", "ctx", "tp"), None),
            P(None, ("fsdp", "ctx", "tp")),
            P(("fsdp", "ctx", "tp"), None),
            P(None, ("fsdp", "ctx", "tp")),
            P(),
            P(),
            P(),
            P(),
            P(),
            P(),
            P(),
            P(),
        ),
        check_vma=False,
    )
```

time: 3220 us -> 1210 us (0.38)
  waiting for transfers between devices: 2660 us -> 508 us
  local copies, waits for them, and re-layouts: 44.5 us -> 236 us
  blocking collectives: 177 us -> 0 us
  starting transfers between devices: 2.52 us -> 105 us
  other arithmetic: 57.1 us -> 116 us
    reduce_scatter x16 -> x0, waiting for transfers between devices: 1850 us -> none  [the longest x1 337 us: on_device(): lax.psum_scatter(down_grad, ('fsdp', 'ctx'), scatter_dimension=1, tiled=T...]
    all_gather x15 -> x0, waiting for transfers between devices: 767 us -> none  [the longest x1 129 us: on_device(): lax.all_gather(gate_weight, ('fsdp', 'ctx'), axis=0, tiled=True)]
    ppermute x0 -> x123, waiting for transfers between devices: none -> 508 us  [the longest x45 215 us: z_shift(): lax.ppermute(value, 'ctx', [(i, (i + step) % size) for i in range(size)])]
    all_gather x2 -> x0, blocking collectives: 136 us -> none  [the longest x1 69.3 us: on_device(): lax.all_gather(laurel_left, ('fsdp', 'ctx', 'tp'), axis=0, tiled=True)]
    ppermute x0 -> x123, starting transfers between devices: none -> 105 us  [the longest x46 50.7 us: x_shift(): lax.ppermute(value, 'fsdp', [(i, (i + 2 * step) % size) for i in range(si...]
    dynamic_update_slice x0 -> x37, local copies, waits for them, and re-layouts: none -> 66.5 us  [the longest x14 34.2 us: assemble(): lax.dynamic_update_slice(whole, piece[None, :, None], (x, 0, z, 0, 0))]
    dot_general x32 -> x46, matrix products: 219 us -> 163 us  [matmul(): return jnp.dot(left, right, preferred_element_type=jnp.float32)]
    unnamed x242 -> x387, local copies, waits for them, and re-layouts: 24.1 us -> 73.8 us
  transfers between devices with their start and end apart: 32 -> 123, of which waited for: 31 -> 46; matrix products, arithmetic and copies ran while one was open for 6% -> 40% of each run, Pallas kernels for 0% -> 0%
where the time goes in v1:
time: 1210 us; the launch traced here: 1200 us
  waiting for transfers between devices  508 us (42%)
  local copies, waits for them, and re-layouts  236 us (20%)
  matrix products  230 us (19%)
  other arithmetic  116 us (10%)
  starting transfers between devices  105 us (9%)
    ppermute x45, waiting for transfers between devices, z_shift(): lax.ppermute(value, 'ctx', [(i, (i + step) % size) for i in range(size)])  215 us
    ppermute x46, waiting for transfers between devices, x_shift(): lax.ppermute(value, 'fsdp', [(i, (i + 2 * step) % size) for i in range(si...  213 us
    dot_general x46, matrix products, matmul(): return jnp.dot(left, right, preferred_element_type=jnp.float32)  163 us
    ppermute x13, waiting for transfers between devices, y_swap(): return lax.ppermute(value, 'tp', [(0, 1), (1, 0)])  76 us
    unnamed x387, local copies, waits for them, and re-layouts  73.8 us
    ppermute x46, starting transfers between devices, x_shift(): lax.ppermute(value, 'fsdp', [(i, (i + 2 * step) % size) for i in range(si...  50.7 us
    dot_general x8, matrix products, matmul_t(): lax.dot_general(left, right, (((1,), (1,)), ((), ())), preferred_element_...  49.4 us
    ppermute x45, starting transfers between devices, z_shift(): lax.ppermute(value, 'ctx', [(i, (i + step) % size) for i in range(size)])  35.8 us
  transfers between devices with their start and end apart: 123, of which 46 were waited for; matrix products, arithmetic and copies ran while one was open for 40% of the time, Pallas kernels for 0%

profile of v1, /device:TPU:0, one launch (start us, length us, event | category | flops | bytes accessed | tf_op | source)
XLA Modules:
  0.0 1198.7 jit_solution(389130561057510192)
XLA Ops:
  28.3 6.0 constant_dynamic-slice_fusion.41
  59.8 6.7 collective-permute-done.23
  73.2 6.1 broadcast_in_dim.238
  104.2 6.3 collective-permute-done.27
  146.1 13.4 %collective-permute-done.3 = bf16[128,1536]{1,0:T(8,128)(2,1)} collective-permute-done((bf16[128,1536]{1,0:T(8,128)(2,1)}, bf16[128,1536]{1,0:T(8,128)(2,1)}, u32[]{:S(2)}, u32[]{:S(2)}) %collective-permute-start.3) | collective-permute-done | bytes 393248 | tf_op jit(solution)/shard_map/ppermute | solution.py:80
  166.3 8.7 collective-permute-done.6
  179.4 8.2 collective-permute-done.7
  194.3 34.2 %collective-permute-done.43 = bf16[2,128,2048]{2,1,0:T(8,128)(2,1)} collective-permute-done((bf16[2,128,2048]{2,1,0:T(8,128)(2,1)}, bf16[2,128,2048]{2,1,0:T(8,128)(2,1)}, u32[]{:S(2)}, u32[]{:S(2)}) %collective-permute-start.43) | collective-permute-done | bytes 1048608 | tf_op jit(solution)/shard_map/ppermute | solution.py:80
  240.5 11.7 collective-permute-done.44
  271.0 28.9 %collective-permute-done.46 = bf16[2,128,2048]{2,1,0:T(8,128)(2,1)} collective-permute-done((bf16[2,128,2048]{2,1,0:T(8,128)(2,1)}, bf16[2,128,2048]{2,1,0:T(8,128)(2,1)}, u32[]{:S(2)}, u32[]{:S(2)}) %collective-permute-start.46) | collective-permute-done | bytes 1048608 | tf_op jit(solution)/shard_map/ppermute | solution.py:75
  303.2 19.0 %collective-permute-done.47 = bf16[2,128,2048]{2,1,0:T(8,128)(2,1)S(1)} collective-permute-done((bf16[2,128,2048]{2,1,0:T(8,128)(2,1)}, bf16[2,128,2048]{2,1,0:T(8,128)(2,1)S(1)}, u32[]{:S(2)}, u32[]{:S(2)}) %collective-permute-start.47) | collective-permute-done | bytes 1048608 | tf_op jit(solution)/shard_map/ppermute | solution.py:75
  331.9 8.3 collective-permute-done.10
  342.1 42.5 %collective-permute-done.11 = bf16[2,256,2,256]{3,1,0,2:T(8,128)(2,1)S(1)} collective-permute-done((bf16[2,256,2,256]{3,1,0,2:T(8,128)(2,1)}, bf16[2,256,2,256]{3,1,0,2:T(8,128)(2,1)S(1)}, u32[]{:S(2)}, u32[]{:S(2)}) %collective-permute-start.11) | collective-permute-done | bytes 524320 | tf_op jit(solution)/shard_map/ppermute | solution.py:80
  405.8 12.9 %collective-permute-done.20 = bf16[2,128,2048]{2,1,0:T(8,128)(2,1)S(1)} collective-permute-done((bf16[2,128,2048]{2,1,0:T(8,128)(2,1)S(1)}, bf16[2,128,2048]{2,1,0:T(8,128)(2,1)S(1)}, u32[]{:S(2)}, u32[]{:S(2)}) %collective-permute-start.20) | collective-permute-done | bytes 1048608 | tf_op jit(solution)/shard_map/ppermute | solution.py:84
  429.3 6.9 collective-permute-done.30
  439.8 10.4 collective-permute-done.39
  451.7 30.7 %collective-permute-done.40 = bf16[2,128,4096]{2,1,0:T(8,128)(2,1)S(1)} collective-permute-done((bf16[2,128,4096]{2,1,0:T(8,128)(2,1)}, bf16[2,128,4096]{2,1,0:T(8,128)(2,1)S(1)}, u32[]{:S(2)}, u32[]{:S(2)}) %collective-permute-start.40) | collective-permute-done | bytes 2097184 | tf_op jit(solution)/shard_map/ppermute | solution.py:75
  485.2 21.1 %fusion.275 = f32[1024,4096]{1,0:T(8,128)S(1)} fusion(bf16[2048,4096]{1,0:T(8,128)(2,1)} %bitcast.82, bf16[512,2048]{1,0:T(8,128)(2,1)} %copy-done.69, bf16[256,2048]{1,0:T(8,128)(2,1)S(1)} %collective-permute-done.30, bf16[256,2048]{1,0:T(8,128)(2,1)S(1)} %bitcast.569), kind=kOutput, calls=%fused_computation.622 | convolution fusion | flops 17192452096 | bytes 37748736 | tf_op jit(solution)/shard_map/dot_general | solution.py:51
  512.0 13.0 %fusion.284 = f32[1024,2048]{1,0:T(8,128)S(1)} fusion(bf16[1024,2048]{1,0:T(8,128)(2,1)S(1)} %multiply_convert_fusion.1, bf16[2048,2048]{1,0:T(8,128)(2,1)} %bitcast.106), kind=kOutput, calls=%fused_computation.630 | convolution fusion | flops 8589934592 | bytes 20971520 | tf_op jit(solution)/shard_map/dot_general | solution.py:55
  539.3 18.4 %collective-permute-done.50 = bf16[256,2048]{1,0:T(8,128)(2,1)} collective-permute-done((bf16[256,2048]{1,0:T(8,128)(2,1)S(1)}, bf16[256,2048]{1,0:T(8,128)(2,1)}, u32[]{:S(2)}, u32[]{:S(2)}) %collective-permute-start.50) | collective-permute-done | bytes 1048608 | tf_op jit(solution)/shard_map/ppermute | solution.py:84
  571.8 6.0 reshape.888
  583.1 7.2 fusion.36
  606.9 10.9 collective-permute-done.51
  663.3 23.7 %fusion.6 = (bf16[1024,2048]{1,0:T(8,128)(2,1)}, bf16[1024,2048]{1,0:T(8,128)(2,1)}) fusion(f32[1024,4096]{1,0:T(8,128)} %copy-done.20, bf16[2048,2048]{1,0:T(8,128)(2,1)} %bitcast.106, bf16[512,2048]{1,0:T(8,128)(2,1)} %collective-permute-done.52, bf16[256,2048]{1,0:T(8,128)(2,1)} %collective-permute-done.51, bf16[256,2048]{1,0:T(8,128)(2,1)} %bitcast.116), kind=kOutput, calls=%fused_computation.8 | convolution fusion | flops 8652849152 | bytes 37748736 | tf_op jit(solution)/shard_map/dot_general | solution.py:51
  687.0 21.4 %fusion.276 = f32[1024,2048]{1,0:T(8,128)S(1)} fusion(bf16[2048,4096]{1,0:T(8,128)(2,1)} %bitcast.82, bf16[1024,2048]{1,0:T(8,128)(2,1)} %get-tuple-element.175, bf16[1024,2048]{1,0:T(8,128)(2,1)} %get-tuple-element.174), kind=kOutput, calls=%fused_computation.623 | convolution fusion | flops 17196646400 | bytes 33554432 | tf_op jit(solution)/shard_map/dot_general | solution.py:55
  709.4 7.3 convolution_convert_fusion
  722.3 6.6 fusion.97
  731.5 6.7 fusion.104
  738.3 6.7 fusion.111
  745.0 6.4 convolution_convert_fusion.3
  751.5 5.9 convolution_convert_fusion.2
  762.5 6.0 convolution_convert_fusion.1
  772.1 10.8 collective-permute-done.54
  805.3 7.9 add_convert_fusion.2
  821.4 9.7 collective-permute-done.98
  836.3 31.7 %collective-permute-done.119 = f32[5,2048]{1,0:T(8,128)S(1)} collective-permute-done((f32[5,2048]{1,0:T(8,128)S(1)}, f32[5,2048]{1,0:T(8,128)S(1)}, u32[]{:S(2)}, u32[]{:S(2)}) %collective-permute-start.119) | collective-permute-done | bytes 40992 | tf_op jit(solution)/shard_map/ppermute | solution.py:75
  882.1 19.1 %collective-permute-done.94 = bf16[128,128]{1,0:T(8,128)(2,1)S(1)} collective-permute-done((bf16[128,128]{1,0:T(8,128)(2,1)S(1)}, bf16[128,128]{1,0:T(8,128)(2,1)S(1)}, u32[]{:S(2)}, u32[]{:S(2)}) %collective-permute-start.94) | collective-permute-done | bytes 32800 | tf_op jit(solution)/shard_map/ppermute | solution.py:75
  916.6 13.7 %collective-permute-done.55 = bf16[2,128,2048]{2,1,0:T(8,128)(2,1)S(1)} collective-permute-done((bf16[2,128,2048]{2,1,0:T(8,128)(2,1)S(1)}, bf16[2,128,2048]{2,1,0:T(8,128)(2,1)S(1)}, u32[]{:S(2)}, u32[]{:S(2)}) %collective-permute-start.55) | collective-permute-done | bytes 1048608 | tf_op jit(solution)/shard_map/ppermute | solution.py:84
  969.0 5.3 convolution_bitcast_fusion.1
  978.9 9.8 collective-permute-done.56
  993.7 8.7 collective-permute-done.57
  1008.0 11.8 collective-permute-done.58
  1024.0 5.6 fusion.48
  1045.8 8.4 collective-permute-done.72
  1061.3 32.6 %collective-permute-done.73 = bf16[128,1024]{1,0:T(8,128)(2,1)S(1)} collective-permute-done((bf16[128,1024]{1,0:T(8,128)(2,1)S(1)}, bf16[128,1024]{1,0:T(8,128)(2,1)S(1)}, u32[]{:S(2)}, u32[]{:S(2)}) %collective-permute-start.73) | collective-permute-done | bytes 262176 | tf_op jit(solution)/shard_map/ppermute | solution.py:80
  1140.3 12.7 %collective-permute-done.64 = bf16[128,1536]{1,0:T(8,128)(2,1)S(1)} collective-permute-done((bf16[128,1536]{1,0:T(8,128)(2,1)S(1)}, bf16[128,1536]{1,0:T(8,128)(2,1)S(1)}, u32[]{:S(2)}, u32[]{:S(2)}) %collective-permute-start.64) | collective-permute-done | bytes 393248 | tf_op jit(solution)/shard_map/ppermute | solution.py:75
  1156.2 12.3 %collective-permute-done.63 = bf16[128,1536]{1,0:T(8,128)(2,1)S(1)} collective-permute-done((bf16[128,1536]{1,0:T(8,128)(2,1)S(1)}, bf16[128,1536]{1,0:T(8,128)(2,1)S(1)}, u32[]{:S(2)}, u32[]{:S(2)}) %collective-permute-start.63) | collective-permute-done | bytes 393248 | tf_op jit(solution)/shard_map/ppermute | solution.py:75
  1171.4 10.3 collective-permute-done.66
  (883 shorter events, 556.5 us)
Async XLA Ops:
  0.7 52.9 %collective-permute-start.12 = (bf16[128,1024]{0,1:T(8,128)(2,1)}, bf16[128,1024]{0,1:T(8,128)(2,1)}, u32[]{:S(2)}, u32[]{:S(2)}) collective-permute-start(bf16[128,1024]{0,1:T(8,128)(2,1)} %bitcast.664), channel_id=1, source_target_pairs={{0,2},{2,4},{4,6},{6,0},{1,3},{3,5},{5,7},{7,1},{8,10},{10,12},{12... | collective-permute-start | bytes 786440 | tf_op jit(solution)/shard_map/ppermute | solution.py:80
  3.8 51.4 %collective-permute-start.15 = (bf16[128,1024]{0,1:T(8,128)(2,1)}, bf16[128,1024]{0,1:T(8,128)(2,1)}, u32[]{:S(2)}, u32[]{:S(2)}) collective-permute-start(bf16[128,1024]{0,1:T(8,128)(2,1)} %bitcast.665), channel_id=1, source_target_pairs={{0,16},{8,24},{16,0},{24,8},{1,17},{9,25},{17,1},{25,9},{2,18},{10... | collective-permute-start | bytes 786440 | tf_op jit(solution)/shard_map/ppermute | solution.py:75
  9.9 151.6 %collective-permute-start.4 = (bf16[128,1536]{1,0:T(8,128)(2,1)}, bf16[128,1536]{1,0:T(8,128)(2,1)}, u32[]{:S(2)}, u32[]{:S(2)}) collective-permute-start(bf16[128,1536]{1,0:T(8,128)(2,1)} %constant_dynamic-update-slice_fusion), channel_id=1, source_target_pairs={{0,16},{8,24},{16,0},{24,8},{1,17},{9,25},{17,1},{25,9},{2,18},{10... | collective-permute-start | bytes 1179656 | tf_op jit(solution)/shard_map/ppermute | solution.py:75
  10.4 47.5 %collective-permute-start.1 = (bf16[128,1536]{1,0:T(8,128)(2,1)}, bf16[128,1536]{1,0:T(8,128)(2,1)}, u32[]{:S(2)}, u32[]{:S(2)}) collective-permute-start(bf16[128,1536]{1,0:T(8,128)(2,1)} %constant_dynamic-update-slice_fusion), channel_id=1, source_target_pairs={{0,2},{2,4},{4,6},{6,0},{1,3},{3,5},{5,7},{7,1},{8,10},{10,12},{12... | collective-permute-start | bytes 1179656 | tf_op jit(solution)/shard_map/ppermute | solution.py:80
  53.6 90.4 %collective-permute-start = (bf16[2,128,2048]{2,1,0:T(8,128)(2,1)S(1)}, bf16[2,128,2048]{2,1,0:T(8,128)(2,1)}, u32[]{:S(2)}, u32[]{:S(2)}) collective-permute-start(bf16[2,128,2048]{2,1,0:T(8,128)(2,1)S(1)} %fusion.32), channel_id=1, source_target_pairs={{0,1},{1,0},{2,3},{3,2},{4,5},{5,4},{6,7},{7,6},{8,9},{9,8},{10,11... | collective-permute-start | bytes 3145736 | tf_op jit(solution)/shard_map/ppermute | solution.py:84
  95.9 67.4 %collective-permute-start.5 = (bf16[128,1536]{1,0:T(8,128)(2,1)}, bf16[128,1536]{1,0:T(8,128)(2,1)}, u32[]{:S(2)}, u32[]{:S(2)}) collective-permute-start(bf16[128,1536]{1,0:T(8,128)(2,1)} %collective-permute-done.1), channel_id=1, source_target_pairs={{0,16},{8,24},{16,0},{24,8},{1,17},{9,25},{17,1},{25,9},{2,18},{10... | collective-permute-start | bytes 1179656 | tf_op jit(solution)/shard_map/ppermute | solution.py:75
  122.7 53.1 %collective-permute-start.42 = (bf16[2,128,2048]{2,1,0:T(8,128)(2,1)S(1)}, bf16[2,128,2048]{2,1,0:T(8,128)(2,1)}, u32[]{:S(2)}, u32[]{:S(2)}) collective-permute-start(bf16[2,128,2048]{2,1,0:T(8,128)(2,1)S(1)} %copy-done.77), channel_id=1, source_target_pairs={{0,2},{2,4},{4,6},{6,0},{1,3},{3,5},{5,7},{7,1},{8,10},{10,12},{12... | collective-permute-start | bytes 3145736 | tf_op jit(solution)/shard_map/ppermute | solution.py:80
  144.0 124.6 %collective-permute-start.45 = (bf16[2,128,2048]{2,1,0:T(8,128)(2,1)S(1)}, bf16[2,128,2048]{2,1,0:T(8,128)(2,1)}, u32[]{:S(2)}, u32[]{:S(2)}) collective-permute-start(bf16[2,128,2048]{2,1,0:T(8,128)(2,1)S(1)} %copy-done.77), channel_id=1, source_target_pairs={{0,16},{8,24},{16,0},{24,8},{1,17},{9,25},{17,1},{25,9},{2,18},{10... | collective-permute-start | bytes 3145736 | tf_op jit(solution)/shard_map/ppermute | solution.py:75
  159.5 70.0 %collective-permute-start.34 = (bf16[2,128,4096]{2,1,0:T(8,128)(2,1)}, bf16[2,128,4096]{2,1,0:T(8,128)(2,1)}, u32[]{:S(2)}, u32[]{:S(2)}) collective-permute-start(bf16[2,128,4096]{2,1,0:T(8,128)(2,1)} %maximum_maximum_fusion), channel_id=1, source_target_pairs={{0,2},{2,4},{4,6},{6,0},{1,3},{3,5},{5,7},{7,1},{8,10},{10,12},{12... | collective-permute-start | bytes 6291464 | tf_op jit(solution)/shard_map/ppermute | solution.py:80
  175.0 60.0 %collective-permute-start.19 = (bf16[2,4,128,1024]{3,2,1,0:T(8,128)(2,1)}, bf16[2,4,128,1024]{3,2,1,0:T(8,128)(2,1)S(1)}, u32[]{:S(2)}, u32[]{:S(2)}) collective-permute-start(bf16[2,4,128,1024]{3,2,1,0:T(8,128)(2,1)} %constant_dynamic-update-slice_fusion.3), channel_id=1, source_target_pairs={{0,8},{8,0},{16,24},{24,16},{1,9},{9,1},{17,25},{25,17},{2,10},{10... | collective-permute-start | bytes 6291464 | tf_op jit(solution)/shard_map/ppermute | solution.py:70
  187.6 40.9 %collective-permute-start.43 = (bf16[2,128,2048]{2,1,0:T(8,128)(2,1)}, bf16[2,128,2048]{2,1,0:T(8,128)(2,1)}, u32[]{:S(2)}, u32[]{:S(2)}) collective-permute-start(bf16[2,128,2048]{2,1,0:T(8,128)(2,1)} %collective-permute-done.42), channel_id=1, source_target_pairs={{0,2},{2,4},{4,6},{6,0},{1,3},{3,5},{5,7},{7,1},{8,10},{10,12},{12... | collective-permute-start | bytes 3145736 | tf_op jit(solution)/shard_map/ppermute | solution.py:80
  190.8 64.8 %collective-permute-start.8 = (bf16[2,4,128,1536]{3,2,1,0:T(8,128)(2,1)}, bf16[2,4,128,1536]{3,2,1,0:T(8,128)(2,1)S(1)}, u32[]{:S(2)}, u32[]{:S(2)}) collective-permute-start(bf16[2,4,128,1536]{3,2,1,0:T(8,128)(2,1)} %bitcast_dynamic-update-slice_fusion.16), channel_id=1, source_target_pairs={{0,8},{8,0},{16,24},{24,16},{1,9},{9,1},{17,25},{25,17},{2,10},{10... | collective-permute-start | bytes 9437192 | tf_op jit(solution)/shard_map/ppermute | solution.py:70
  228.5 197.6 %collective-permute-start.37 = (bf16[2,128,4096]{2,1,0:T(8,128)(2,1)}, bf16[2,128,4096]{2,1,0:T(8,128)(2,1)}, u32[]{:S(2)}, u32[]{:S(2)}) collective-permute-start(bf16[2,128,4096]{2,1,0:T(8,128)(2,1)} %maximum_maximum_fusion), channel_id=1, source_target_pairs={{0,16},{8,24},{16,0},{24,8},{1,17},{9,25},{17,1},{25,9},{2,18},{10... | collective-permute-start | bytes 6291464 | tf_op jit(solution)/shard_map/ppermute | solution.py:75
  235.0 64.8 %collective-permute-start.46 = (bf16[2,128,2048]{2,1,0:T(8,128)(2,1)}, bf16[2,128,2048]{2,1,0:T(8,128)(2,1)}, u32[]{:S(2)}, u32[]{:S(2)}) collective-permute-start(bf16[2,128,2048]{2,1,0:T(8,128)(2,1)} %collective-permute-done.42), channel_id=1, source_target_pairs={{0,16},{8,24},{16,0},{24,8},{1,17},{9,25},{17,1},{25,9},{2,18},{10... | collective-permute-start | bytes 3145736 | tf_op jit(solution)/shard_map/ppermute | solution.py:75
  252.2 70.0 %collective-permute-start.47 = (bf16[2,128,2048]{2,1,0:T(8,128)(2,1)}, bf16[2,128,2048]{2,1,0:T(8,128)(2,1)S(1)}, u32[]{:S(2)}, u32[]{:S(2)}) collective-permute-start(bf16[2,128,2048]{2,1,0:T(8,128)(2,1)} %collective-permute-done.43), channel_id=1, source_target_pairs={{0,16},{8,24},{16,0},{24,8},{1,17},{9,25},{17,1},{25,9},{2,18},{10... | collective-permute-start | bytes 3145736 | tf_op jit(solution)/shard_map/ppermute | solution.py:75
  255.6 68.7 %collective-permute-start.35 = (bf16[2,128,4096]{2,1,0:T(8,128)(2,1)}, bf16[2,128,4096]{2,1,0:T(8,128)(2,1)}, u32[]{:S(2)}, u32[]{:S(2)}) collective-permute-start(bf16[2,128,4096]{2,1,0:T(8,128)(2,1)} %collective-permute-done.34), channel_id=1, source_target_pairs={{0,2},{2,4},{4,6},{6,0},{1,3},{3,5},{5,7},{7,1},{8,10},{10,12},{12... | collective-permute-start | bytes 6291464 | tf_op jit(solution)/shard_map/ppermute | solution.py:80
  268.6 54.6 %collective-permute-start.9 = (bf16[2,256,2,256]{3,1,0,2:T(8,128)(2,1)S(1)}, bf16[2,256,2,256]{3,1,0,2:T(8,128)(2,1)}, u32[]{:S(2)}, u32[]{:S(2)}) collective-permute-start(bf16[2,256,2,256]{3,1,0,2:T(8,128)(2,1)S(1)} %pad_maximum_fusion.22), channel_id=1, source_target_pairs={{0,2},{2,4},{4,6},{6,0},{1,3},{3,5},{5,7},{7,1},{8,10},{10,12},{12... | collective-permute-start | bytes 1572872 | tf_op jit(solution)/shard_map/ppermute | solution.py:80
  299.8 136.6 %collective-permute-start.38 = (bf16[2,128,4096]{2,1,0:T(8,128)(2,1)}, bf16[2,128,4096]{2,1,0:T(8,128)(2,1)}, u32[]{:S(2)}, u32[]{:S(2)}) collective-permute-start(bf16[2,128,4096]{2,1,0:T(8,128)(2,1)} %collective-permute-done.34), channel_id=1, source_target_pairs={{0,16},{8,24},{16,0},{24,8},{1,17},{9,25},{17,1},{25,9},{2,18},{10... | collective-permute-start | bytes 6291464 | tf_op jit(solution)/shard_map/ppermute | solution.py:75
  322.2 79.1 %collective-permute-start.48 = (bf16[2,128,2048]{2,1,0:T(8,128)(2,1)}, bf16[2,128,2048]{2,1,0:T(8,128)(2,1)}, u32[]{:S(2)}, u32[]{:S(2)}) collective-permute-start(bf16[2,128,2048]{2,1,0:T(8,128)(2,1)} %collective-permute-done.44), channel_id=1, source_target_pairs={{0,16},{8,24},{16,0},{24,8},{1,17},{9,25},{17,1},{25,9},{2,18},{10... | collective-permute-start | bytes 3145736 | tf_op jit(solution)/shard_map/ppermute | solution.py:75
  324.4 80.5 %collective-permute-start.36 = (bf16[2,128,4096]{2,1,0:T(8,128)(2,1)}, bf16[2,128,4096]{2,1,0:T(8,128)(2,1)}, u32[]{:S(2)}, u32[]{:S(2)}) collective-permute-start(bf16[2,128,4096]{2,1,0:T(8,128)(2,1)} %collective-permute-done.35), channel_id=1, source_target_pairs={{0,2},{2,4},{4,6},{6,0},{1,3},{3,5},{5,7},{7,1},{8,10},{10,12},{12... | collective-permute-start | bytes 6291464 | tf_op jit(solution)/shard_map/ppermute | solution.py:80
  340.2 44.4 %collective-permute-start.11 = (bf16[2,256,2,256]{3,1,0,2:T(8,128)(2,1)}, bf16[2,256,2,256]{3,1,0,2:T(8,128)(2,1)S(1)}, u32[]{:S(2)}, u32[]{:S(2)}) collective-permute-start(bf16[2,256,2,256]{3,1,0,2:T(8,128)(2,1)} %collective-permute-done.10), channel_id=1, source_target_pairs={{0,2},{2,4},{4,6},{6,0},{1,3},{3,5},{5,7},{7,1},{8,10},{10,12},{12... | collective-permute-start | bytes 1572872 | tf_op jit(solution)/shard_map/ppermute | solution.py:80
  401.3 48.8 %collective-permute-start.39 = (bf16[2,128,4096]{2,1,0:T(8,128)(2,1)}, bf16[2,128,4096]{2,1,0:T(8,128)(2,1)S(1)}, u32[]{:S(2)}, u32[]{:S(2)}) collective-permute-start(bf16[2,128,4096]{2,1,0:T(8,128)(2,1)} %collective-permute-done.35), channel_id=1, source_target_pairs={{0,16},{8,24},{16,0},{24,8},{1,17},{9,25},{17,1},{25,9},{2,18},{10... | collective-permute-start | bytes 6291464 | tf_op jit(solution)/shard_map/ppermute | solution.py:75
  404.9 77.4 %collective-permute-start.40 = (bf16[2,128,4096]{2,1,0:T(8,128)(2,1)}, bf16[2,128,4096]{2,1,0:T(8,128)(2,1)S(1)}, u32[]{:S(2)}, u32[]{:S(2)}) collective-permute-start(bf16[2,128,4096]{2,1,0:T(8,128)(2,1)} %collective-permute-done.36), channel_id=1, source_target_pairs={{0,16},{8,24},{16,0},{24,8},{1,17},{9,25},{17,1},{25,9},{2,18},{10... | collective-permute-start | bytes 6291464 | tf_op jit(solution)/shard_map/ppermute | solution.py:75
  436.4 47.5 %collective-permute-start.31 = (bf16[512,2048]{1,0:T(8,128)(2,1)S(1)}, bf16[512,2048]{1,0:T(8,128)(2,1)S(1)}, u32[]{:S(2)}, u32[]{:S(2)}) collective-permute-start(bf16[512,2048]{1,0:T(8,128)(2,1)S(1)} %pad_maximum_fusion.9), channel_id=1, source_target_pairs={{0,8},{8,0},{16,24},{24,16},{1,9},{9,1},{17,25},{25,17},{2,10},{10... | collective-permute-start | bytes 6291464 | tf_op jit(solution)/shard_map/ppermute | solution.py:70
  655.3 177.2 %collective-permute-start.86 = (bf16[256,2048]{1,0:T(8,128)(2,1)}, bf16[256,2048]{1,0:T(8,128)(2,1)}, u32[]{:S(2)}, u32[]{:S(2)}) collective-permute-start(bf16[256,2048]{1,0:T(8,128)(2,1)} %convolution_convert_fusion.7), channel_id=1, source_target_pairs={{0,16},{8,24},{16,0},{24,8},{1,17},{9,25},{17,1},{25,9},{2,18},{10... | collective-permute-start | bytes 3145736 | tf_op jit(solution)/shard_map/ppermute | solution.py:75
  659.0 136.7 %collective-permute-start.87 = (bf16[256,2048]{1,0:T(8,128)(2,1)}, bf16[256,2048]{1,0:T(8,128)(2,1)}, u32[]{:S(2)}, u32[]{:S(2)}) collective-permute-start(bf16[256,2048]{1,0:T(8,128)(2,1)} %convolution_convert_fusion.6), channel_id=1, source_target_pairs={{0,16},{8,24},{16,0},{24,8},{1,17},{9,25},{17,1},{25,9},{2,18},{10... | collective-permute-start | bytes 3145736 | tf_op jit(solution)/shard_map/ppermute | solution.py:75
  661.9 106.6 %collective-permute-start.88 = (bf16[256,2048]{1,0:T(8,128)(2,1)}, bf16[256,2048]{1,0:T(8,128)(2,1)}, u32[]{:S(2)}, u32[]{:S(2)}) collective-permute-start(bf16[256,2048]{1,0:T(8,128)(2,1)} %convolution_convert_fusion.5), channel_id=1, source_target_pairs={{0,16},{8,24},{16,0},{24,8},{1,17},{9,25},{17,1},{25,9},{2,18},{10... | collective-permute-start | bytes 3145736 | tf_op jit(solution)/shard_map/ppermute | solution.py:75
  708.7 48.7 %collective-permute-start.53 = (bf16[512,2048]{1,0:T(8,128)(2,1)S(1)}, bf16[512,2048]{1,0:T(8,128)(2,1)S(1)}, u32[]{:S(2)}, u32[]{:S(2)}) collective-permute-start(bf16[512,2048]{1,0:T(8,128)(2,1)S(1)} %slice.450), channel_id=1, source_target_pairs={{0,8},{8,0},{16,24},{24,16},{1,9},{9,1},{17,25},{25,17},{2,10},{10... | collective-permute-start | bytes 6291464 | tf_op jit(solution)/shard_map/ppermute | solution.py:70
  716.7 88.6 %collective-permute-start.79 = (bf16[256,4096]{1,0:T(8,128)(2,1)}, bf16[256,4096]{1,0:T(8,128)(2,1)}, u32[]{:S(2)}, u32[]{:S(2)}) collective-permute-start(bf16[256,4096]{1,0:T(8,128)(2,1)} %convolution_convert_fusion), channel_id=1, source_target_pairs={{0,16},{8,24},{16,0},{24,8},{1,17},{9,25},{17,1},{25,9},{2,18},{10... | collective-permute-start | bytes 6291464 | tf_op jit(solution)/shard_map/ppermute | solution.py:75
  802.3 30.9 %collective-permute-start.90 = (bf16[256,2048]{1,0:T(8,128)(2,1)}, bf16[256,2048]{1,0:T(8,128)(2,1)}, u32[]{:S(2)}, u32[]{:S(2)}) collective-permute-start(bf16[256,2048]{1,0:T(8,128)(2,1)} %add_convert_fusion.4), channel_id=1, source_target_pairs={{0,2},{2,4},{4,6},{6,0},{1,3},{3,5},{5,7},{7,1},{8,10},{10,12},{12... | collective-permute-start | bytes 3145736 | tf_op jit(solution)/shard_map/ppermute | solution.py:80
  818.9 89.5 %collective-permute-start.78 = (bf16[256,4096]{1,0:T(8,128)(2,1)}, bf16[256,4096]{1,0:T(8,128)(2,1)S(1)}, u32[]{:S(2)}, u32[]{:S(2)}) collective-permute-start(bf16[256,4096]{1,0:T(8,128)(2,1)} %convolution_convert_fusion.1), channel_id=1, source_target_pairs={{0,16},{8,24},{16,0},{24,8},{1,17},{9,25},{17,1},{25,9},{2,18},{10... | collective-permute-start | bytes 6291464 | tf_op jit(solution)/shard_map/ppermute | solution.py:75
  820.3 89.0 %collective-permute-start.80 = (bf16[256,4096]{1,0:T(8,128)(2,1)}, bf16[256,4096]{1,0:T(8,128)(2,1)}, u32[]{:S(2)}, u32[]{:S(2)}) collective-permute-start(bf16[256,4096]{1,0:T(8,128)(2,1)} %add_convert_fusion.2), channel_id=1, source_target_pairs={{0,2},{2,4},{4,6},{6,0},{1,3},{3,5},{5,7},{7,1},{8,10},{10,12},{12... | collective-permute-start | bytes 6291464 | tf_op jit(solution)/shard_map/ppermute | solution.py:80
  831.1 36.9 %collective-permute-start.119 = (f32[5,2048]{1,0:T(8,128)S(1)}, f32[5,2048]{1,0:T(8,128)S(1)}, u32[]{:S(2)}, u32[]{:S(2)}) collective-permute-start(f32[5,2048]{1,0:T(8,128)S(1)} %add.1435), channel_id=1, source_target_pairs={{0,16},{8,24},{16,0},{24,8},{1,17},{9,25},{17,1},{25,9},{2,18},{10... | collective-permute-start | bytes 122888 | tf_op jit(solution)/shard_map/ppermute | solution.py:75
  832.5 39.4 %collective-permute-start.95 = (bf16[128,128]{1,0:T(8,128)(2,1)S(1)}, bf16[128,128]{1,0:T(8,128)(2,1)S(1)}, u32[]{:S(2)}, u32[]{:S(2)}) collective-permute-start(bf16[128,128]{1,0:T(8,128)(2,1)S(1)} %get-tuple-element.260), channel_id=1, source_target_pairs={{0,16},{8,24},{16,0},{24,8},{1,17},{9,25},{17,1},{25,9},{2,18},{10... | collective-permute-start | bytes 98312 | tf_op jit(solution)/shard_map/ppermute | solution.py:75
  833.2 42.4 %collective-permute-start.99 = (bf16[128,128]{1,0:T(8,128)(2,1)S(1)}, bf16[128,128]{1,0:T(8,128)(2,1)S(1)}, u32[]{:S(2)}, u32[]{:S(2)}) collective-permute-start(bf16[128,128]{1,0:T(8,128)(2,1)S(1)} %fusion.220), channel_id=1, source_target_pairs={{0,2},{2,4},{4,6},{6,0},{1,3},{3,5},{5,7},{7,1},{8,10},{10,12},{12... | collective-permute-start | bytes 98312 | tf_op jit(solution)/shard_map/ppermute | solution.py:80
  875.6 98.8 %collective-permute-start.85 = (bf16[256,2048]{1,0:T(8,128)(2,1)}, bf16[256,2048]{1,0:T(8,128)(2,1)}, u32[]{:S(2)}, u32[]{:S(2)}) collective-permute-start(bf16[256,2048]{1,0:T(8,128)(2,1)} %convolution_convert_fusion.8), channel_id=1, source_target_pairs={{0,16},{8,24},{16,0},{24,8},{1,17},{9,25},{17,1},{25,9},{2,18},{10... | collective-permute-start | bytes 3145736 | tf_op jit(solution)/shard_map/ppermute | solution.py:75
  901.2 134.6 %collective-permute-start.77 = (bf16[256,4096]{1,0:T(8,128)(2,1)}, bf16[256,4096]{1,0:T(8,128)(2,1)}, u32[]{:S(2)}, u32[]{:S(2)}) collective-permute-start(bf16[256,4096]{1,0:T(8,128)(2,1)} %convolution_convert_fusion.2), channel_id=1, source_target_pairs={{0,16},{8,24},{16,0},{24,8},{1,17},{9,25},{17,1},{25,9},{2,18},{10... | collective-permute-start | bytes 6291464 | tf_op jit(solution)/shard_map/ppermute | solution.py:75
  906.4 217.9 %collective-permute-start.76 = (bf16[256,4096]{1,0:T(8,128)(2,1)}, bf16[256,4096]{1,0:T(8,128)(2,1)}, u32[]{:S(2)}, u32[]{:S(2)}) collective-permute-start(bf16[256,4096]{1,0:T(8,128)(2,1)} %convolution_convert_fusion.3), channel_id=1, source_target_pairs={{0,16},{8,24},{16,0},{24,8},{1,17},{9,25},{17,1},{25,9},{2,18},{10... | collective-permute-start | bytes 6291464 | tf_op jit(solution)/shard_map/ppermute | solution.py:75
  909.3 65.2 %collective-permute-start.91 = (bf16[256,2048]{1,0:T(8,128)(2,1)}, bf16[256,2048]{1,0:T(8,128)(2,1)}, u32[]{:S(2)}, u32[]{:S(2)}) collective-permute-start(bf16[256,2048]{1,0:T(8,128)(2,1)} %add_convert_fusion.3), channel_id=1, source_target_pairs={{0,2},{2,4},{4,6},{6,0},{1,3},{3,5},{5,7},{7,1},{8,10},{10,12},{12... | collective-permute-start | bytes 3145736 | tf_op jit(solution)/shard_map/ppermute | solution.py:80
  930.4 105.4 %collective-permute-start.81 = (bf16[256,4096]{1,0:T(8,128)(2,1)}, bf16[256,4096]{1,0:T(8,128)(2,1)}, u32[]{:S(2)}, u32[]{:S(2)}) collective-permute-start(bf16[256,4096]{1,0:T(8,128)(2,1)} %add_convert_fusion.1), channel_id=1, source_target_pairs={{0,2},{2,4},{4,6},{6,0},{1,3},{3,5},{5,7},{7,1},{8,10},{10,12},{12... | collective-permute-start | bytes 6291464 | tf_op jit(solution)/shard_map/ppermute | solution.py:80
  1002.4 36.9 %collective-permute-start.68 = (bf16[1024,1024]{1,0:T(8,128)(2,1)}, bf16[1024,1024]{1,0:T(8,128)(2,1)}, u32[]{:S(2)}, u32[]{:S(2)}) collective-permute-start(bf16[1024,1024]{1,0:T(8,128)(2,1)} %convolution_convert_fusion.9), channel_id=1, source_target_pairs={{0,8},{8,0},{16,24},{24,16},{1,9},{9,1},{17,25},{25,17},{2,10},{10... | collective-permute-start | bytes 6291464 | tf_op jit(solution)/shard_map/ppermute | solution.py:70
  1039.2 85.0 %collective-permute-start.82 = (bf16[256,4096]{1,0:T(8,128)(2,1)S(1)}, bf16[256,4096]{1,0:T(8,128)(2,1)}, u32[]{:S(2)}, u32[]{:S(2)}) collective-permute-start(bf16[256,4096]{1,0:T(8,128)(2,1)S(1)} %add_convert_fusion), channel_id=1, source_target_pairs={{0,2},{2,4},{4,6},{6,0},{1,3},{3,5},{5,7},{7,1},{8,10},{10,12},{12... | collective-permute-start | bytes 6291464 | tf_op jit(solution)/shard_map/ppermute | solution.py:80
  1055.5 38.4 %collective-permute-start.73 = (bf16[128,1024]{1,0:T(8,128)(2,1)S(1)}, bf16[128,1024]{1,0:T(8,128)(2,1)S(1)}, u32[]{:S(2)}, u32[]{:S(2)}) collective-permute-start(bf16[128,1024]{1,0:T(8,128)(2,1)S(1)} %fusion.62), channel_id=1, source_target_pairs={{0,2},{2,4},{4,6},{6,0},{1,3},{3,5},{5,7},{7,1},{8,10},{10,12},{12... | collective-permute-start | bytes 786440 | tf_op jit(solution)/shard_map/ppermute | solution.py:80
  1058.7 46.4 %collective-permute-start.70 = (bf16[128,1024]{1,0:T(8,128)(2,1)S(1)}, bf16[128,1024]{1,0:T(8,128)(2,1)S(1)}, u32[]{:S(2)}, u32[]{:S(2)}) collective-permute-start(bf16[128,1024]{1,0:T(8,128)(2,1)S(1)} %fusion.66), channel_id=1, source_target_pairs={{0,16},{8,24},{16,0},{24,8},{1,17},{9,25},{17,1},{25,9},{2,18},{10... | collective-permute-start | bytes 786440 | tf_op jit(solution)/shard_map/ppermute | solution.py:75
  1060.1 35.2 %collective-permute-start.112 = (f32[2560]{0:T(1024)S(1)}, f32[2560]{0:T(1024)S(1)}, u32[]{:S(2)}, u32[]{:S(2)}) collective-permute-start(f32[2560]{0:T(1024)S(1)} %fusion.273), channel_id=1, source_target_pairs={{0,1},{1,0},{2,3},{3,2},{4,5},{5,4},{6,7},{7,6},{8,9},{9,8},{10,11... | collective-permute-start | bytes 30728 | tf_op jit(solution)/shard_map/ppermute | solution.py:84
  1129.2 41.0 %collective-permute-start.84 = (f32[128,2048]{1,0:T(8,128)S(1)}, f32[128,2048]{1,0:T(8,128)S(1)}, u32[]{:S(2)}, u32[]{:S(2)}) collective-permute-start(f32[128,2048]{1,0:T(8,128)S(1)} %dynamic-slice_bitcast_fusion.1), channel_id=1, source_target_pairs={{0,8},{8,0},{16,24},{24,16},{1,9},{9,1},{17,25},{25,17},{2,10},{10... | collective-permute-start | bytes 3145736 | tf_op jit(solution)/shard_map/ppermute | solution.py:70
  1132.4 62.8 %collective-permute-start.61 = (bf16[128,1536]{1,0:T(8,128)(2,1)}, bf16[128,1536]{1,0:T(8,128)(2,1)}, u32[]{:S(2)}, u32[]{:S(2)}) collective-permute-start(bf16[128,1536]{1,0:T(8,128)(2,1)} %fusion.27), channel_id=1, source_target_pairs={{0,16},{8,24},{16,0},{24,8},{1,17},{9,25},{17,1},{25,9},{2,18},{10... | collective-permute-start | bytes 1179656 | tf_op jit(solution)/shard_map/ppermute | solution.py:75
  1137.4 33.9 %collective-permute-start.62 = (bf16[128,1536]{1,0:T(8,128)(2,1)S(1)}, bf16[128,1536]{1,0:T(8,128)(2,1)S(1)}, u32[]{:S(2)}, u32[]{:S(2)}) collective-permute-start(bf16[128,1536]{1,0:T(8,128)(2,1)S(1)} %fusion.28), channel_id=1, source_target_pairs={{0,16},{8,24},{16,0},{24,8},{1,17},{9,25},{17,1},{25,9},{2,18},{10... | collective-permute-start | bytes 1179656 | tf_op jit(solution)/shard_map/ppermute | solution.py:75
  (254 other events, 3574.6 us)

commit v2 on v1

v2 whole, which is shorter than its diff:
```python
import jax
import jax.numpy as jnp
from jax import lax
from jax.experimental import pallas as pl
from jax.experimental.pallas import tpu as pltpu
from jax.sharding import Mesh, PartitionSpec as P

HEAD_SIZE = 256


EPS = 1e-06
THETA = 1000000.0
MASKED = -1e30
SQRT_HALF = 0.7071067811865476
LANES = 128


def scaled_norm(value, gain):
    return value * lax.rsqrt(jnp.mean(value * value, axis=-1, keepdims=True) + EPS) * gain


def plain_norm(value):
    return value * lax.rsqrt(jnp.mean(value * value, axis=-1, keepdims=True) + EPS)


def rotate(value, cosine, sine):
    half = value.shape[-1] // 2
    first = value[..., :half]
    second = value[..., half:]
    return jnp.concatenate(
        [first * cosine - second * sine, second * cosine + first * sine], axis=-1
    )


def geglu(gate, upward):
    return jax.nn.gelu(gate, approximate=True) * upward


def attention_mix(inputs, attention, normed, laurel, attention_gain, laurel_gain):
    return (
        inputs + scaled_norm(attention, attention_gain) + normed + scaled_norm(laurel, laurel_gain)
    ) * SQRT_HALF


def residual_mix(residual, branch, gain):
    return residual + scaled_norm(branch, gain)


def matmul(left, right):
    return jnp.dot(left, right, preferred_element_type=jnp.float32)


def matmul_t(left, right):
    return lax.dot_general(
        left, right, (((1,), (1,)), ((), ())), preferred_element_type=jnp.float32
    )


def low(value):
    return value.astype(jnp.bfloat16)


def wide(value):
    return value.astype(jnp.float32)


def tie(*values):
    return lax.optimization_barrier(values)


CTX = ("pair", "odd")


def core_swap(value):
    return lax.ppermute(value, "core", [(0, 1), (1, 0)])


def x_shift(value, step=1):
    size = lax.axis_size("x")
    return lax.ppermute(value, "x", [(i, (i + step) % size) for i in range(size)])


def z_shift(value, step=1):
    size = lax.axis_size(CTX)
    return lax.ppermute(value, CTX, [(i, (i + step) % size) for i in range(size)])


def pair_shift(value):
    size = lax.axis_size("pair")
    return lax.ppermute(value, "pair", [(i, (i + 1) % size) for i in range(size)])


def odd_swap(value):
    return lax.ppermute(value, "odd", [(0, 1), (1, 0)])


def y_swap(value):
    return lax.ppermute(value, "tp", [(0, 1), (1, 0)])


def in_order(own, mine, other, axis):
    first = jnp.where(own == 0, mine, other)
    second = jnp.where(own == 0, other, mine)
    return jnp.stack([first, second], axis)


def halves_of(value, axis, own):
    shape = value.shape
    value = value.reshape(shape[:axis] + (2, shape[axis] // 2) + shape[axis + 1 :])
    kept = lax.dynamic_index_in_dim(value, own, axis, False)
    return kept, lax.dynamic_index_in_dim(value, 1 - own, axis, False)


class Place:
    def __init__(self, rows):
        self.rows = rows
        self.chips = chips = lax.axis_size("x")
        self.pairs = pairs = lax.axis_size("pair")
        self.depth = depth = 2 * pairs
        self.core = core = lax.axis_index("core")
        self.x = x = lax.axis_index("x")
        self.y = lax.axis_index("tp")
        self.pair = pair = lax.axis_index("pair")
        self.odd = lax.axis_index("odd")
        self.z = z = pair * 2 + self.odd
        count = 2 * chips * depth

        def whole(xs, cores, zs):
            return (xs * 2 + cores) * depth + zs

        def near(xs, cores, zs):
            return (((core + cores) % 2) * chips + (x - xs) % chips) * depth + (z - zs) % depth

        at = jnp.arange(count, dtype=jnp.int32)
        of_whole = (at // (2 * depth), (at // depth) % 2, at % depth)
        of_near = (
            (x - (at // depth) % chips) % chips,
            (core + at // (chips * depth)) % 2,
            (z - at) % depth,
        )
        self.whole_to_near = whole(*of_near).astype(jnp.int32)
        self.near_to_whole = near(*of_whole).astype(jnp.int32)

    def move(self, value, index):
        rows = self.rows
        if rows % LANES:
            shape = value.shape
            value = value.reshape(shape[0], -1, rows)
            return jnp.take(value, index, axis=1).reshape(shape)

        def kernel(index_ref, value_ref, out_ref):
            for i in range(value.shape[1] // rows):
                start = pl.multiple_of(index_ref[i] * rows, LANES)
                out_ref[:, i * rows : (i + 1) * rows] = value_ref[:, pl.ds(start, rows)]

        return pl.pallas_call(
            kernel,
            out_shape=jax.ShapeDtypeStruct(value.shape, value.dtype),
            in_specs=[
                pl.BlockSpec(memory_space=pltpu.SMEM),
                pl.BlockSpec(memory_space=pltpu.VMEM),
            ],
            out_specs=pl.BlockSpec(memory_space=pltpu.VMEM),
            name="move_blocks",
        )(index, value)


def z_ring(place, shard):
    ring = [shard]
    for _ in range(1, place.depth):
        ring.append(z_shift(ring[-1]))
    return ring


def rows_of(place, columns):
    return jnp.concatenate(
        [column[dx] for dx in range(place.chips) for column in columns], 0
    )


def scatter_x(place, partial, splits):
    rows = place.rows
    parts = {}
    for first, last in splits:
        run = None
        for dx in range(1, place.chips):
            value = partial(dx, first, last)
            if run is not None:
                value = value + wide(run)
            run = x_shift(low(value))
        value = partial(0, first, last)
        if run is not None:
            value = value + wide(run)
        for dz in range(first, last):
            parts[dz] = value[(dz - first) * rows : (dz - first + 1) * rows]
    return parts


def scatter_z(place, parts):
    passing = None
    for step in range(1, place.depth):
        value = parts[step]
        if passing is not None:
            value = value + wide(passing)
        passing = z_shift(low(value))
    return parts[0] + wide(passing)


def sum_everywhere(place, value):
    value = value + core_swap(value)
    value = value + y_swap(value)
    value = sum([x_shift(value, step) for step in range(1, place.chips)], value)
    return sum([z_shift(value, step) for step in range(1, place.depth)], value)


def swap_middle(place, value, first):
    second = 2 * place.pairs // first
    size = 2 * place.rows
    return jnp.concatenate(
        [
            value[:, ((x * first + a) * second + b) * size :][:, :size]
            for x in range(place.chips)
            for b in range(second)
            for a in range(first)
        ],
        1,
    )


def to_fixed(place, value):
    return swap_middle(place, value, 2)


def from_fixed(place, value):
    return swap_middle(place, value, place.pairs)


def take(value, index, axis):
    return lax.dynamic_index_in_dim(value, index, axis, False)


def quarters(place, shards):
    return jnp.concatenate([shard.reshape(place.rows, 2, 2, -1) for shard in shards], 3)


def join_four(place, value, parts):
    rows = place.rows
    value = value.reshape(2, 2, rows, -1)
    kept = lax.dynamic_index_in_dim(value, place.odd, 1, False)
    sent = lax.dynamic_index_in_dim(value, 1 - place.odd, 1, False)
    value = in_order(place.odd, kept, wide(odd_swap(low(sent))), 2)
    kept = lax.dynamic_index_in_dim(value, place.core, 0, False)
    sent = lax.dynamic_index_in_dim(value, 1 - place.core, 0, False)
    value = in_order(place.core, kept, core_swap(sent), 1)
    return [part.reshape(rows, -1) for part in jnp.split(value, parts, 3)]


def x_ring(place, piece):
    pieces = [piece]
    for _ in range(1, place.chips):
        pieces.append(x_shift(pieces[-1]))
    return pieces


def share_four(value):
    half = value.shape[0] // 2
    beside = y_swap(value)
    above = odd_swap(value)
    across = [y_swap(above[:half]), odd_swap(beside[half:])]
    return jnp.concatenate([value, beside, above] + across, 0)


def add_core(value):
    return jnp.concatenate([value, core_swap(value)], 0)


def sum_across(value, arrived, product):
    rows = value.shape[0] // 8
    half = rows // 2

    def own(first, last):
        return product(value[first:last]) + wide(arrived[first:last])

    across = low(own(3 * rows, 4 * rows))
    above_half = y_swap(across[:half])
    beside_half = odd_swap(across[half:])
    beside_first = y_swap(low(own(rows, rows + half)))
    above_last = odd_swap(low(own(2 * rows + half, 3 * rows)))
    return own, across, above_half, beside_half, beside_first, above_last


def sum_beside(rows, own, above_half, beside_half):
    half = rows // 2
    beside_last = y_swap(low(own(rows + half, 2 * rows) + wide(beside_half)))
    above_first = odd_swap(low(own(2 * rows, 2 * rows + half) + wide(above_half)))
    return beside_last, above_first


def add_halves(value, beside, above):
    half = value.shape[0] // 2
    return jnp.concatenate(
        [
            value[part * half : (part + 1) * half] + wide(beside[part]) + wide(above[part])
            for part in range(2)
        ],
        0,
    )


def share_two(value):
    return jnp.concatenate([value, y_swap(value)], 1)


def sum_two(value):
    rows = value.shape[1] // 2
    return value[:, :rows] + wide(y_swap(low(value[:, rows:])))


def on_device(
    tokens,
    side_input,
    prefix,
    positions,
    cotangent,
    query_weight,
    key_matrix,
    value_matrix,
    out_weight,
    gate_weight,
    up_weight,
    down_weight,
    laurel_left,
    laurel_right,
    side_gate_weight,
    side_out_weight,
    input_gain,
    laurel_gain,
    attention_gain,
    hidden_in_gain,
    hidden_out_gain,
    side_gain,
    query_gain,
    key_gain,
):
    shard_rows = query_weight.shape[0]
    place = Place(shard_rows)
    chips, depth = place.chips, place.depth
    sequences, own_rows, width = tokens.shape
    shape = tokens.shape
    side_width = side_input.shape[2]
    rank = laurel_left.shape[1]
    block_rows = positions.shape[1]
    query_width = query_weight.shape[1]
    key_width = key_matrix.shape[1]
    hidden_part = gate_weight.shape[1] // 4
    local_heads = query_width // HEAD_SIZE
    local_groups = key_width // HEAD_SIZE
    per_group = local_heads // local_groups

    near_rows = place.y * own_rows + jnp.arange(own_rows, dtype=jnp.int32)
    far_rows = (1 - place.y) * own_rows + jnp.arange(own_rows, dtype=jnp.int32)
    block_index = jnp.concatenate([near_rows, far_rows])
    row_index = place.z * block_rows + block_index
    near_positions = lax.dynamic_slice_in_dim(positions, place.y * own_rows, own_rows, 1)
    far_positions = lax.dynamic_slice_in_dim(positions, (1 - place.y) * own_rows, own_rows, 1)
    positions = jnp.concatenate([near_positions, far_positions], 1)
    freq = THETA ** (
        -(jnp.arange(HEAD_SIZE // 2, dtype=jnp.float32) * 2.0) / HEAD_SIZE
    )
    angle = positions.astype(jnp.float32)[..., None] * freq
    cosine = jnp.cos(angle)[..., None, :]
    sine = jnp.sin(angle)[..., None, :]

    inputs = tokens.astype(jnp.float32)
    normed, input_pull = jax.vjp(scaled_norm, inputs, input_gain)
    normed_reduced = normed.astype(jnp.bfloat16)
    flat_normed = normed_reduced.reshape(-1, width)
    half_width = width // 2
    everywhere = ("x", "core", "pair", "odd", "tp")

    small = jnp.concatenate(
        [laurel_left, laurel_right.T, side_gate_weight, side_out_weight.T], 1
    )
    small_full = lax.all_gather(small, everywhere, axis=0, tiled=True)
    out_shard, small_full = tie(out_weight.T, small_full)
    out_full = lax.all_gather(out_shard, everywhere[:4], axis=0, tiled=True)
    laurel_down = small_full[:, :rank]
    laurel_up_t = small_full[:, rank : 2 * rank]
    side_gate_full = small_full[:, 2 * rank : 2 * rank + side_width]
    side_out_t = small_full[:, 2 * rank + side_width :]

    mixed_shard = jnp.concatenate([query_weight, key_matrix, value_matrix], 1)
    gate_up = quarters(place, [gate_weight, up_weight])
    gate_up_arrived = odd_swap(take(gate_up, 1 - place.odd, 2))
    down = quarters(place, [down_weight.T])
    down_arrived = core_swap(take(down, 1 - place.core, 1))
    mixed_ring = [mixed_shard, z_shift(mixed_shard)]
    mixed_columns = [x_ring(place, mixed_shard)]
    down = in_order(place.core, take(down, place.core, 1), down_arrived, 0)
    down_kept, down_sent = take(down, place.odd, 2), take(down, 1 - place.odd, 2)
    near_in = place.move(flat_normed, place.whole_to_near).reshape(shape)
    near_in, mixed_ring[-1] = tie(near_in, mixed_ring[-1])
    flat_in = share_two(near_in)
    for step in range(2, depth):
        mixed_ring.append(z_shift(mixed_ring[-1]))
        mixed_columns.append(x_ring(place, mixed_ring[-2]))
        mixed_ring[-1], mixed_columns[-2] = tie(mixed_ring[-1], mixed_columns[-2])
        if step == 2:
            mixed_ring[-1], gate_up_arrived, down_kept, down_sent = tie(
                mixed_ring[-1], gate_up_arrived, down_kept, down_sent
            )
            down_arrived = odd_swap(down_sent)
    gate_up = in_order(place.odd, take(gate_up, place.odd, 2), gate_up_arrived, 0)
    gate_up_kept = take(gate_up, place.core, 2)
    gate_up_arrived = core_swap(take(gate_up, 1 - place.core, 2))
    mixed_ring[-1], mixed_columns[-1], flat_in, gate_up_arrived = tie(
        mixed_ring[-1], mixed_columns[-1], flat_in, gate_up_arrived
    )
    flat_in = flat_in.reshape(-1, width)
    mixed_columns.append(x_ring(place, mixed_ring[-1]))
    gate_up_shard = in_order(place.core, gate_up_kept, gate_up_arrived, 0).reshape(
        4 * shard_rows, -1
    )

    mixed_near = rows_of(place, mixed_columns)
    mixed_near, gate_up_shard, down_arrived = tie(mixed_near, gate_up_shard, down_arrived)
    mixed_far = core_swap(mixed_near)
    gate_up_shard, out_full = tie(gate_up_shard, out_full)
    gate_up_full = lax.all_gather(gate_up_shard, ("x", "pair"), axis=0, tiled=True)
    down_shard = in_order(place.odd, down_kept, down_arrived, 1).reshape(4 * shard_rows, -1)
    down_shard, gate_up_full = tie(down_shard, gate_up_full)
    down_full_t = lax.all_gather(down_shard, ("x", "pair"), axis=0, tiled=True)
    def project(first, last):
        return matmul(flat_in[:, :half_width], mixed_near[:, first:last]) + matmul(
            flat_in[:, half_width:], mixed_far[:, first:last]
        )

    key_value_raw = project(query_width, query_width + 2 * key_width)
    query_raw = project(0, query_width)

    def queries_of(part, gain):
        part = part.reshape(sequences, block_rows, local_heads, HEAD_SIZE)
        return rotate(scaled_norm(part, gain), cosine, sine)

    def keys_of(part, gain):
        keys = part[:, :key_width].reshape(sequences, block_rows, local_groups, HEAD_SIZE)
        values = part[:, key_width:].reshape(sequences, block_rows, local_groups, HEAD_SIZE)
        return rotate(scaled_norm(keys, gain), cosine, sine), plain_norm(values)

    (keys, values), keys_pull = jax.vjp(keys_of, key_value_raw, key_gain)
    query_rows, queries_pull = jax.vjp(queries_of, query_raw, query_gain)
    query_low = query_rows.astype(jnp.bfloat16).reshape(
        sequences, block_rows, local_groups, per_group, HEAD_SIZE
    )
    both = jnp.concatenate([low(keys), low(values)], 2)
    pieces = z_ring(place, both)
    key_index = jnp.concatenate(
        [((place.z - dz) % depth) * block_rows + block_index for dz in range(depth)]
    )
    everyone = jnp.concatenate(pieces, 1)
    all_keys = everyone[:, :, :local_groups]
    all_values = everyone[:, :, local_groups:]
    visible = (key_index[None, None, :] <= row_index[None, :, None]) | (
        key_index[None, None, :] < prefix[:, None, None]
    )

    def all_scores():
        scores = jnp.einsum(
            "sbkgd,sjkd->skgbj", query_low, all_keys, preferred_element_type=jnp.float32
        )
        return jnp.where(visible[:, None, None], scores, MASKED)

    scores = all_scores()
    highest = jnp.max(scores, axis=-1, keepdims=True)
    log_total = highest + jnp.log(jnp.sum(jnp.exp(scores - highest), axis=-1, keepdims=True))
    probs = jnp.exp(scores - log_total)
    probs_low = low(probs)
    attended = jnp.einsum(
        "skgbj,sjkd->sbkgd", probs_low, all_values, preferred_element_type=jnp.float32
    )
    attended_low = attended.astype(jnp.bfloat16).reshape(
        sequences * block_rows, local_heads * HEAD_SIZE
    )
    attention = sum_two(matmul_t(attended_low, out_full).reshape(sequences, block_rows, width))
    laurel_mid = matmul(flat_normed, laurel_down).astype(jnp.bfloat16)
    laurel_out = matmul_t(laurel_mid, laurel_up_t).reshape(shape)
    mixed, mix_pull = jax.vjp(
        attention_mix, inputs, attention, normed, laurel_out, attention_gain, laurel_gain
    )
    hidden_in, pre_pull = jax.vjp(scaled_norm, mixed, hidden_in_gain)
    hidden_block = share_four(
        to_fixed(place, low(hidden_in).reshape(-1, width))
    )

    hidden_block = add_core(hidden_block)
    gate_up_out = matmul(hidden_block, gate_up_full)
    hidden, hidden_pull = jax.vjp(
        geglu, gate_up_out[:, :hidden_part], gate_up_out[:, hidden_part:]
    )
    hidden_low = low(hidden)
    token_rows = sequences * own_rows

    def down_product(value):
        return matmul_t(value, down_full_t)

    far_out = low(down_product(hidden_low[4 * token_rows :]))
    own, _, above_half, beside_half, beside_first, above_last = sum_across(
        hidden_low, core_swap(far_out), down_product
    )
    beside_last, above_first = sum_beside(token_rows, own, above_half, beside_half)
    hidden_out = add_halves(
        own(0, token_rows), (beside_first, beside_last), (above_first, above_last)
    )
    hidden_out = from_fixed(place, hidden_out).reshape(shape)
    layer_out, post_pull = jax.vjp(residual_mix, mixed, hidden_out, hidden_out_gain)
    layer_low = layer_out.astype(jnp.bfloat16).reshape(-1, width)
    side_pre = matmul(layer_low, side_gate_full)
    side_act, side_pull = jax.vjp(
        geglu, side_pre, side_input.astype(jnp.float32).reshape(-1, side_width)
    )
    side_low = side_act.astype(jnp.bfloat16)
    projected = matmul_t(side_low, side_out_t).reshape(shape)
    result, final_pull = jax.vjp(residual_mix, layer_out, projected, side_gain)
    result = low(result)
    out_grad_first, projected_grad, side_gain_grad = final_pull(cotangent.astype(jnp.float32))
    projected_low = projected_grad.astype(jnp.bfloat16).reshape(-1, width)
    side_out_grad_t = matmul(projected_low.T, side_low)
    side_grad = matmul(projected_low, side_out_t)
    side_pre_grad, side_input_grad = side_pull(side_grad)
    side_pre_low = side_pre_grad.astype(jnp.bfloat16)
    side_gate_grad = matmul(layer_low.T, side_pre_low)
    layer_grad = out_grad_first + matmul_t(side_pre_low, side_gate_full).reshape(shape)
    mixed_grad_first, hidden_out_grad, hidden_out_gain_grad = post_pull(layer_grad)
    hidden_out_block = add_core(
        share_four(to_fixed(place, low(hidden_out_grad).reshape(-1, width)))
    )

    side_grads = lax.psum_scatter(
        low(jnp.concatenate([side_gate_grad, side_out_grad_t], 1)),
        everywhere[:4],
        scatter_dimension=0,
        tiled=True,
    )
    down_grad = low(matmul(hidden_out_block.T, hidden_low))
    hidden_out_block, down_grad = tie(hidden_out_block, down_grad)
    down_grad, side_grads = tie(down_grad, side_grads)
    down_grad = lax.psum_scatter(down_grad, ("x", "pair"), scatter_dimension=0, tiled=True)
    hidden_grad = matmul(hidden_out_block, down_full_t)
    gate_grad_full, up_grad_full = hidden_pull(hidden_grad)
    gate_up_low = jnp.concatenate([low(gate_grad_full), low(up_grad_full)], 1)

    def gate_up_product(value):
        return matmul_t(value, gate_up_full)

    far_out = low(gate_up_product(gate_up_low[4 * token_rows :]))
    own, across, above_half, beside_half, beside_first, above_last = sum_across(
        gate_up_low, core_swap(far_out), gate_up_product
    )
    wgrad_low, across = tie(gate_up_low, across)
    gate_up_grad = low(matmul(hidden_block.T, wgrad_low))
    beside_last, above_first = sum_beside(token_rows, own, above_half, beside_half)
    hidden_in_sum = own(0, token_rows)
    hidden_in_sum, gate_up_grad = tie(hidden_in_sum, gate_up_grad)
    hidden_in_sum = add_halves(
        hidden_in_sum, (beside_first, beside_last), (above_first, above_last)
    )
    hidden_in_sum = from_fixed(place, hidden_in_sum).reshape(shape)
    gate_up_grad = lax.psum_scatter(
        gate_up_grad, ("x", "pair"), scatter_dimension=0, tiled=True
    )
    mixed_grad_second, hidden_in_gain_grad = pre_pull(hidden_in_sum)
    mixed_grad = mixed_grad_first + mixed_grad_second
    (
        inputs_grad_first,
        attention_grad,
        normed_grad_first,
        laurel_grad,
        attention_gain_grad,
        laurel_gain_grad,
    ) = mix_pull(mixed_grad)
    attention_grad, down_grad = tie(attention_grad, down_grad)
    attention_block = share_two(low(attention_grad)).reshape(-1, width)
    (down_grad_t,) = join_four(place, wide(down_grad), 1)

    attended_grad = (
        matmul(attention_block, out_full)
        .astype(jnp.bfloat16)
        .reshape(sequences, block_rows, local_groups, per_group, HEAD_SIZE)
    )
    laurel_low = laurel_grad.astype(jnp.bfloat16).reshape(-1, width)
    laurel_mid_grad = matmul(laurel_low, laurel_up_t).astype(jnp.bfloat16)
    normed_grad_second = matmul_t(laurel_mid_grad, laurel_down).reshape(shape)

    def scatter_attention(left, right, extra=None):
        def rows(start, end):
            value = matmul(left[:, start:end].T, right)
            return value if extra is None else jnp.concatenate([value, extra[start:end]], 1)

        arrived = core_swap(low(rows(half_width, width)))

        def partial(dx, first, last):
            start, end = (dx * depth + first) * shard_rows, (dx * depth + last) * shard_rows
            return rows(start, end) + wide(arrived[start:end])

        return scatter_x(place, partial, [(1, depth), (0, 1)])

    near_own = near_in.reshape(-1, width)
    laurel_near = place.move(laurel_low, place.whole_to_near)
    out_parts = scatter_attention(
        place.move(attention_block, place.whole_to_near),
        attended_low,
        jnp.concatenate(
            [matmul(near_own.T, laurel_mid_grad), matmul(laurel_near.T, laurel_mid)], 1
        ),
    )

    delta = jnp.transpose(
        jnp.sum(attended_grad.astype(jnp.float32) * attended, axis=-1), (0, 2, 3, 1)
    )
    probs = jnp.exp(all_scores() - log_total)
    probs_grad = jnp.einsum(
        "sbkgd,sjkd->skgbj", attended_grad, all_values, preferred_element_type=jnp.float32
    )
    scores_grad = low(probs * (probs_grad - delta[..., None]))
    query_grad = jnp.einsum(
        "skgbj,sjkd->sbkgd", scores_grad, all_keys, preferred_element_type=jnp.float32
    )
    keys_grad = jnp.einsum(
        "skgbj,sbkgd->sjkd", scores_grad, query_low, preferred_element_type=jnp.float32
    )
    values_grad = jnp.einsum(
        "skgbj,sbkgd->sjkd", low(probs), attended_grad, preferred_element_type=jnp.float32
    )
    both_grad = jnp.concatenate([keys_grad, values_grad], 2)
    passing = None
    for step in range(1, depth + 1):
        dz = step % depth
        value = both_grad[:, dz * block_rows : (dz + 1) * block_rows]
        if passing is not None:
            value = value + wide(passing)
        if dz:
            passing = z_shift(low(value))
    value, gate_up_grad = tie(value, gate_up_grad)
    out_parts, value = tie(out_parts, value)
    out_sum = scatter_z(place, out_parts)
    query_raw_grad, query_gain_grad = queries_pull(
        query_grad.reshape(sequences, block_rows, local_heads, HEAD_SIZE)
    )
    keys_raw_grad, key_gain_grad = keys_pull(
        (value[:, :, :local_groups], value[:, :, local_groups:])
    )
    mixed_low = jnp.concatenate([low(query_raw_grad), low(keys_raw_grad)], 1)
    mixed_weight_grad = scatter_z(place, scatter_attention(flat_in, mixed_low))
    block_in_grad = jnp.concatenate(
        [matmul_t(mixed_low, mixed_near), matmul_t(mixed_low, mixed_far)], 1
    ).reshape(sequences, block_rows, width)
    block_in_sum = place.move(
        sum_two(block_in_grad).reshape(-1, width), place.near_to_whole
    ).reshape(shape)
    normed_grad = normed_grad_first + normed_grad_second + block_in_sum
    inputs_grad_second, input_gain_grad = input_pull(normed_grad)
    tokens_grad = inputs_grad_first + inputs_grad_second
    gain_grads = (
        jnp.stack(
            [
                input_gain_grad,
                laurel_gain_grad,
                attention_gain_grad,
                hidden_in_gain_grad,
                hidden_out_gain_grad,
                side_gain_grad,
            ]
        )
    )
    head_grads = jnp.concatenate(
        [query_gain_grad, key_gain_grad, jnp.zeros((width - 2 * HEAD_SIZE,), jnp.float32)]
    )
    gain_grads = sum_everywhere(place, jnp.concatenate([gain_grads, head_grads[None]], 0))
    gain_grads = tuple(gain_grads[:6]) + (
        gain_grads[6, :HEAD_SIZE],
        gain_grads[6, HEAD_SIZE : 2 * HEAD_SIZE],
    )
    gate_grad, up_grad = join_four(place, wide(gate_up_grad), 2)
    kept, sent = halves_of(
        jnp.concatenate([out_sum[:, query_width:], wide(side_grads)], 1), 0, place.y
    )
    small_grads = kept + wide(y_swap(low(sent)))
    side_input_grad = side_input_grad.reshape(sequences, own_rows, side_width)
    return (
        (result, tokens_grad, side_input_grad)
        + (
            mixed_weight_grad[:, :query_width],
            mixed_weight_grad[:, query_width : query_width + key_width],
            mixed_weight_grad[:, query_width + key_width :],
            out_sum[:, :query_width].T,
            gate_grad,
            up_grad,
            down_grad_t.T,
        )
        + (
            small_grads[:, :rank],
            small_grads[:, rank : 2 * rank].T,
            small_grads[:, 2 * rank : 2 * rank + side_width],
            small_grads[:, 2 * rank + side_width :].T,
        )
        + gain_grads
    )


def solution(mesh):
    sizes = (mesh.shape["fsdp"] // 2, 2, mesh.shape["ctx"] // 2, 2, mesh.shape["tp"])
    mesh = Mesh(mesh.devices.reshape(sizes), ("x", "core", "pair", "odd", "tp"))
    placed = (
        P(("x", "core"), ("pair", "odd", "tp"), None),
        P(("x", "core"), ("pair", "odd", "tp"), None),
        P(("x", "core")),
        P(("x", "core"), ("pair", "odd")),
        P(("x", "core"), ("pair", "odd", "tp"), None),
        P(("x", "core", "pair", "odd"), "tp"),
        P(("x", "core", "pair", "odd"), "tp"),
        P(("x", "core", "pair", "odd"), "tp"),
        P("tp", ("x", "core", "pair", "odd")),
        P(("x", "core", "pair", "odd"), "tp"),
        P(("x", "core", "pair", "odd"), "tp"),
        P("tp", ("x", "core", "pair", "odd")),
        P(("x", "core", "pair", "odd", "tp"), None),
        P(None, ("x", "core", "pair", "odd", "tp")),
        P(("x", "core", "pair", "odd", "tp"), None),
        P(None, ("x", "core", "pair", "odd", "tp")),
        P(),
        P(),
        P(),
        P(),
        P(),
        P(),
        P(),
        P(),
    )
    return jax.shard_map(
        on_device,
        mesh=mesh,
        in_specs=placed,
        out_specs=(
            P(("x", "core"), ("pair", "odd", "tp"), None),
            P(("x", "core"), ("pair", "odd", "tp"), None),
            P(("x", "core"), ("pair", "odd", "tp"), None),
            P(("x", "core", "pair", "odd"), "tp"),
            P(("x", "core", "pair", "odd"), "tp"),
            P(("x", "core", "pair", "odd"), "tp"),
            P("tp", ("x", "core", "pair", "odd")),
            P(("x", "core", "pair", "odd"), "tp"),
            P(("x", "core", "pair", "odd"), "tp"),
            P("tp", ("x", "core", "pair", "odd")),
            P(("x", "core", "pair", "odd", "tp"), None),
            P(None, ("x", "core", "pair", "odd", "tp")),
            P(("x", "core", "pair", "odd", "tp"), None),
            P(None, ("x", "core", "pair", "odd", "tp")),
            P(),
            P(),
            P(),
            P(),
            P(),
            P(),
            P(),
            P(),
        ),
        check_vma=False,
    )
```

time: 1210 us -> 1050 us (0.87)
  local copies, waits for them, and re-layouts: 236 us -> 122 us
  waiting for transfers between devices: 508 us -> 469 us
  starting transfers between devices: 105 us -> 76.2 us
  between operations: 3.84 us -> 17.1 us
    ppermute x110 -> x53, waiting for transfers between devices: 432 us -> 338 us  [the longest x18 150 us: z_shift(): lax.ppermute(value, CTX, [(i, (i + step) % size) for i in range(size)])]
    all_gather x0 -> x4, waiting for transfers between devices: none -> 80.4 us  [the longest x1 41.5 us: on_device(): lax.all_gather(gate_up_shard, ('x', 'pair'), axis=0, tiled=True)]
    dynamic_update_slice x37 -> x0, local copies, waits for them, and re-layouts: 66.5 us -> none  [the longest x14 34.2 us: assemble(): lax.dynamic_update_slice(whole, piece[None, :, None], (x, 0, z, 0, 0))]
    ppermute x110 -> x53, starting transfers between devices: 87.9 us -> 44.1 us  [the longest x18 27 us: z_shift(): lax.ppermute(value, CTX, [(i, (i + step) % size) for i in range(size)])]
    dot_general x46 -> x27, matrix products: 163 us -> 121 us  [matmul(): return jnp.dot(left, right, preferred_element_type=jnp.float32)]
    dot_general x8 -> x21, matrix products: 49.4 us -> 87.9 us  [matmul_t(): lax.dot_general(left, right, (((1,), (1,)), ((), ())), preferred_element_...]
    ppermute x13 -> x16, waiting for transfers between devices: 76 us -> 49.1 us  [y_swap(): return lax.ppermute(value, 'tp', [(0, 1), (1, 0)])]
    broadcast_in_dim x13 -> x1, local copies, waits for them, and re-layouts: 26.8 us -> 0.01 us  [on_device(): jnp.zeros((width - 2 * HEAD_SIZE,), jnp.float32)]
  transfers between devices with their start and end apart: 123 -> 76, of which waited for: 46 -> 42; matrix products, arithmetic and copies ran while one was open for 40% -> 38% of each run, Pallas kernels for 0% -> 1%
where the time goes in v2:
time: 1050 us; the launch traced here: 1040 us
  waiting for transfers between devices  469 us (45%)
  matrix products  230 us (22%)
  local copies, waits for them, and re-layouts  122 us (12%)
  other arithmetic  110 us (10%)
  starting transfers between devices  76.2 us (7%)
  between operations  17.1 us (2%)
  Pallas kernels  12 us (1%)
    ppermute x18, waiting for transfers between devices, z_shift(): lax.ppermute(value, CTX, [(i, (i + step) % size) for i in range(size)])  150 us
    ppermute x14, waiting for transfers between devices, odd_swap(): return lax.ppermute(value, 'odd', [(0, 1), (1, 0)])  123 us
    dot_general x27, matrix products, matmul(): return jnp.dot(left, right, preferred_element_type=jnp.float32)  121 us
    dot_general x21, matrix products, matmul_t(): lax.dot_general(left, right, (((1,), (1,)), ((), ())), preferred_element_...  87.9 us
    unnamed x371, local copies, waits for them, and re-layouts  70.3 us
    ppermute x9, waiting for transfers between devices, x_shift(): lax.ppermute(value, 'x', [(i, (i + step) % size) for i in range(size)])  55 us
    ppermute x16, waiting for transfers between devices, y_swap(): return lax.ppermute(value, 'tp', [(0, 1), (1, 0)])  49.1 us
    all_gather x1, waiting for transfers between devices, on_device(): lax.all_gather(gate_up_shard, ('x', 'pair'), axis=0, tiled=True)  41.5 us
  transfers between devices with their start and end apart: 76, of which 42 were waited for; matrix products, arithmetic and copies ran while one was open for 38% of the time, Pallas kernels for 1%

profile of v2, /device:TPU:0, one launch (start us, length us, event | category | flops | bytes accessed | tf_op | source)
XLA Modules:
  0.0 1036.1 jit_solution(11757402537699130012)
XLA Ops:
  37.7 32.8 %collective-permute-done.1 = bf16[128,1536]{1,0:T(8,128)(2,1)S(1)} collective-permute-done((bf16[128,1536]{1,0:T(8,128)(2,1)}, bf16[128,1536]{1,0:T(8,128)(2,1)S(1)}, u32[]{:S(2)}, u32[]{:S(2)}) %collective-permute-start.1) | collective-permute-done | bytes 393248 | tf_op jit(solution)/shard_map/ppermute | solution.py:85
  75.0 9.3 collective-permute-done.6
  106.8 4.4 collective-permute-done.12
  123.0 15.6 %collective-permute-done.13 = bf16[2,256,2,256]{3,1,0,2:T(8,128)(2,1)} collective-permute-done((bf16[2,256,2,256]{3,1,0,2:T(8,128)(2,1)S(1)}, bf16[2,256,2,256]{3,1,0,2:T(8,128)(2,1)}, u32[]{:S(2)}, u32[]{:S(2)}) %collective-permute-start.13) | collective-permute-done | bytes 524320 | tf_op jit(solution)/shard_map/ppermute | solution.py:85
  147.5 15.3 %collective-permute-done.14 = bf16[2,256,2,256]{3,1,0,2:T(8,128)(2,1)} collective-permute-done((bf16[2,256,2,256]{3,1,0,2:T(8,128)(2,1)}, bf16[2,256,2,256]{3,1,0,2:T(8,128)(2,1)}, u32[]{:S(2)}, u32[]{:S(2)}) %collective-permute-start.14) | collective-permute-done | bytes 524320 | tf_op jit(solution)/shard_map/ppermute | solution.py:85
  165.5 12.4 %collective-permute-done.15 = bf16[2,256,2,256]{3,1,0,2:T(8,128)(2,1)S(1)} collective-permute-done((bf16[2,256,2,256]{3,1,0,2:T(8,128)(2,1)}, bf16[2,256,2,256]{3,1,0,2:T(8,128)(2,1)S(1)}, u32[]{:S(2)}, u32[]{:S(2)}) %collective-permute-start.15) | collective-permute-done | bytes 524320 | tf_op jit(solution)/shard_map/ppermute | solution.py:85
  198.0 17.3 %collective-permute-done.16 = bf16[2,128,2048]{2,1,0:T(8,128)(2,1)S(1)} collective-permute-done((bf16[2,128,2048]{2,1,0:T(8,128)(2,1)S(1)}, bf16[2,128,2048]{2,1,0:T(8,128)(2,1)S(1)}, u32[]{:S(2)}, u32[]{:S(2)}) %collective-permute-start.16) | collective-permute-done | bytes 1048608 | tf_op jit(solution)/shard_map/ppermute | solution.py:98
  224.7 35.8 %collective-permute-done.18 = bf16[256,2048]{1,0:T(8,128)(2,1)S(1)} collective-permute-done((bf16[256,2048]{1,0:T(8,128)(2,1)S(1)}, bf16[256,2048]{1,0:T(8,128)(2,1)S(1)}, u32[]{:S(2)}, u32[]{:S(2)}) %collective-permute-start.18) | collective-permute-done | bytes 1048608 | tf_op jit(solution)/shard_map/ppermute | solution.py:94
  264.0 10.5 %collective-permute-done.19 = bf16[128,2048]{1,0:T(8,128)(2,1)S(1)} collective-permute-done((bf16[128,2048]{1,0:T(8,128)(2,1)S(1)}, bf16[128,2048]{1,0:T(8,128)(2,1)S(1)}, u32[]{:S(2)}, u32[]{:S(2)}) %collective-permute-start.19) | collective-permute-done | bytes 524320 | tf_op jit(solution)/shard_map/ppermute | solution.py:98
  275.4 10.6 %collective-permute-done.20 = bf16[128,2048]{1,0:T(8,128)(2,1)S(1)} collective-permute-done((bf16[128,2048]{1,0:T(8,128)(2,1)S(1)}, bf16[128,2048]{1,0:T(8,128)(2,1)S(1)}, u32[]{:S(2)}, u32[]{:S(2)}) %collective-permute-start.20) | collective-permute-done | bytes 524320 | tf_op jit(solution)/shard_map/ppermute | solution.py:94
  291.2 41.5 %all-gather.9.cloned.1.call-done = bf16[2048,2048]{1,0:T(8,128)(2,1)} async-done(((bf16[512,2048]{1,0:T(8,128)(2,1)}), bf16[2048,2048]{1,0:T(8,128)(2,1)}) %all-gather.9.cloned.1.call-update) | async-done | bytes 8388624 | tf_op jit(solution)/shard_map/all_gather | solution.py:429
  332.7 12.9 %reduce-scatter.10.cloned.1.call-start = ((), (), s32[]{:S(2)}) async-start(), calls=%async_computation.9 | async-start | bytes 2228224
  345.7 5.1 constant_dynamic-update-slice_fusion.27
  351.8 21.9 %fusion.270 = f32[2048,2048]{0,1:T(8,128)} fusion(bf16[2048,2048]{1,0:T(8,128)(2,1)} %constant_dynamic-update-slice_fusion.27, bf16[2048,2048]{1,0:T(8,128)(2,1)S(1)} %copy-done), kind=kOutput, calls=%fused_computation.617 | convolution fusion | flops 17179869184 | bytes 33554432 | tf_op jit(solution)/shard_map/dot_general | solution.py:50
  373.7 8.6 multiply_convert_fusion.1
  382.4 38.9 %all-gather.11.cloned.1.call-done = bf16[2048,1024]{1,0:T(8,128)(2,1)} async-done(((bf16[512,1024]{1,0:T(8,128)(2,1)}), bf16[2048,1024]{1,0:T(8,128)(2,1)}) %all-gather.11.cloned.1.call-update) | async-done | bytes 4194320 | tf_op jit(solution)/shard_map/all_gather | solution.py:432
  421.2 7.5 convolution_convert_fusion.2
  444.7 7.5 collective-permute-done.24
  456.7 8.3 collective-permute-done.28
  465.0 10.1 collective-permute-done.25
  492.4 23.4 %collective-permute-done.30 = bf16[256,2048]{1,0:T(8,128)(2,1)S(1)} collective-permute-done((bf16[256,2048]{1,0:T(8,128)(2,1)S(1)}, bf16[256,2048]{1,0:T(8,128)(2,1)S(1)}, u32[]{:S(2)}, u32[]{:S(2)}) %collective-permute-start.30) | collective-permute-done | bytes 1048608 | tf_op jit(solution)/shard_map/ppermute | solution.py:94
  520.3 7.2 collective-permute-done.31
  537.1 4.9 constant_dynamic-update-slice_fusion.54
  542.0 12.9 %convolution_convert_fusion.3 = bf16[2048,1024]{1,0:T(8,128)(2,1)} fusion(bf16[2048,2048]{1,0:T(8,128)(2,1)} %constant_dynamic-update-slice_fusion.54, bf16[2048,1024]{0,1:T(8,128)(2,1)S(1)} %copy-done.51), kind=kOutput, calls=%fused_computation.63 | convolution fusion | flops 8592031744 | bytes 16777216 | tf_op jit(solution)/shard_map/dot_general | solution.py:50
  554.9 24.3 %multiply_convert_fusion = (bf16[2048,1024]{0,1:T(8,128)(2,1)}, bf16[2048,1024]{0,1:T(8,128)(2,1)}) fusion(f32[2048,2048]{0,1:T(8,128)} %fusion.270, bf16[2048,2048]{1,0:T(8,128)(2,1)} %constant_dynamic-update-slice_fusion.54, bf16[2048,1024]{1,0:T(8,128)(2,1)} %all-gather.11.cloned.1.call-done), kind=kOutput, calls=%fused_computation.28 | convolution fusion | flops 8640266240 | bytes 37748736 | tf_op jit(solution)/shard_map/dot_general | solution.py:50
  579.2 14.8 %fusion.18 = bf16[1024,2048]{1,0:T(8,128)(2,1)} fusion(bf16[2048,2048]{1,0:T(8,128)(2,1)} %all-gather.9.cloned.1.call-done, bf16[2048,1024]{0,1:T(8,128)(2,1)} %get-tuple-element.257, bf16[2048,1024]{0,1:T(8,128)(2,1)} %get-tuple-element.256), kind=kOutput, calls=%fused_computation.62 | convolution fusion | flops 8600420352 | bytes 20971520 | tf_op jit(solution)/shard_map/dot_general | solution.py:54
  597.9 6.6 fusion.122
  604.5 6.7 fusion.119
  612.1 8.4 pad_maximum_fusion
  620.5 7.7 add_convert_fusion.5
  629.9 6.3 add_convert_fusion.1
  639.6 21.8 %convolution_convert_fusion = bf16[2048,2048]{1,0:T(8,128)(2,1)} fusion(bf16[2048,2048]{1,0:T(8,128)(2,1)} %constant_dynamic-update-slice_fusion.27, bf16[2048,2048]{0,1:T(8,128)(2,1)S(1)} %bitcast.416), kind=kOutput, calls=%fused_computation.33 | convolution fusion | flops 17184063488 | bytes 25165824 | tf_op jit(solution)/shard_map/dot_general | solution.py:50
  661.4 7.5 add_convert_fusion.8
  675.3 6.1 convert_add_fusion.3
  684.1 11.4 %collective-permute-done.37 = bf16[128,2048]{1,0:T(8,128)(2,1)} collective-permute-done((bf16[128,2048]{1,0:T(8,128)(2,1)}, bf16[128,2048]{1,0:T(8,128)(2,1)}, u32[]{:S(2)}, u32[]{:S(2)}) %collective-permute-start.37) | collective-permute-done | bytes 524320 | tf_op jit(solution)/shard_map/ppermute | solution.py:94
  726.1 20.3 %collective-permute-done.60 = bf16[2,128,1024]{2,1,0:T(8,128)(2,1)S(1)} collective-permute-done((bf16[2,128,1024]{2,1,0:T(8,128)(2,1)S(1)}, bf16[2,128,1024]{2,1,0:T(8,128)(2,1)S(1)}, u32[]{:S(2)}, u32[]{:S(2)}) %collective-permute-start.60) | collective-permute-done | bytes 524320 | tf_op jit(solution)/shard_map/ppermute | solution.py:94
  773.0 5.1 fusion.12
  779.3 6.1 convolution_bitcast_fusion.1
  799.3 7.4 collective-permute-done.45
  806.9 9.4 collective-permute-start.46
  818.9 14.1 %collective-permute-done.46 = bf16[2,256,2,256]{3,1,0,2:T(8,128)(2,1)S(1)} collective-permute-done((bf16[2,256,2,256]{3,1,0,2:T(8,128)(2,1)S(1)}, bf16[2,256,2,256]{3,1,0,2:T(8,128)(2,1)S(1)}, u32[]{:S(2)}, u32[]{:S(2)}) %collective-permute-start.46) | collective-permute-done | bytes 524320 | tf_op jit(solution)/shard_map/ppermute | solution.py:85
  833.2 8.5 collective-permute-start.47
  853.0 20.0 %collective-permute-done.43 = bf16[128,1152]{1,0:T(8,128)(2,1)} collective-permute-done((bf16[128,1152]{1,0:T(8,128)(2,1)}, bf16[128,1152]{1,0:T(8,128)(2,1)}, u32[]{:S(2)}, u32[]{:S(2)}) %collective-permute-start.43) | collective-permute-done | bytes 294944 | tf_op jit(solution)/shard_map/ppermute | solution.py:80
  904.3 9.2 collective-permute-done.56
  916.2 18.6 %collective-permute-done.57 = bf16[128,1152]{1,0:T(8,128)(2,1)S(1)} collective-permute-done((bf16[128,1152]{1,0:T(8,128)(2,1)S(1)}, bf16[128,1152]{1,0:T(8,128)(2,1)S(1)}, u32[]{:S(2)}, u32[]{:S(2)}) %collective-permute-start.57) | collective-permute-done | bytes 294944 | tf_op jit(solution)/shard_map/ppermute | solution.py:85
  972.3 19.1 %collective-permute-done.51 = bf16[384,1536]{1,0:T(8,128)(2,1)S(1)} collective-permute-done((bf16[384,1536]{1,0:T(8,128)(2,1)S(1)}, bf16[384,1536]{1,0:T(8,128)(2,1)S(1)}, u32[]{:S(2)}, u32[]{:S(2)}) %collective-permute-start.51) | collective-permute-done | bytes 1179680 | tf_op jit(solution)/shard_map/ppermute | solution.py:80
  993.9 10.7 %collective-permute-done.52 = bf16[128,1536]{1,0:T(8,128)(2,1)S(1)} collective-permute-done((bf16[128,1536]{1,0:T(8,128)(2,1)S(1)}, bf16[128,1536]{1,0:T(8,128)(2,1)S(1)}, u32[]{:S(2)}, u32[]{:S(2)}) %collective-permute-start.52) | collective-permute-done | bytes 393248 | tf_op jit(solution)/shard_map/ppermute | solution.py:85
  1008.0 7.3 collective-permute-done.53
  (732 shorter events, 366.7 us)
Async XLA Ops:
  7.2 90.6 %all-gather.5.cloned.1.call-start = ((), (), s32[]{:S(2)}) async-start(), calls=%async_computation.3 | async-start | bytes 2703360 | tf_op jit(solution)/shard_map/all_gather | solution.py:384
  10.0 23.6 %collective-permute-start = (bf16[128,1536]{1,0:T(8,128)(2,1)S(1)}, bf16[128,1536]{1,0:T(8,128)(2,1)}, u32[]{:S(2)}, u32[]{:S(2)}) collective-permute-start(bf16[128,1536]{1,0:T(8,128)(2,1)S(1)} %constant_dynamic-update-slice_fusion), channel_id=1, source_target_pairs={{0,2},{2,4},{4,6},{6,0},{1,3},{3,5},{5,7},{7,1},{8,10},{10,12},{12... | collective-permute-start | bytes 1179656 | tf_op jit(solution)/shard_map/ppermute | solution.py:85
  13.0 24.7 %collective-permute-start.2 = (bf16[128,1536]{1,0:T(8,128)(2,1)S(1)}, bf16[128,1536]{1,0:T(8,128)(2,1)}, u32[]{:S(2)}, u32[]{:S(2)}) collective-permute-start(bf16[128,1536]{1,0:T(8,128)(2,1)S(1)} %constant_dynamic-update-slice_fusion), channel_id=1, source_target_pairs={{0,16},{16,0},{1,17},{17,1},{2,18},{18,2},{3,19},{19,3},{4,20},{20... | collective-permute-start | bytes 1179656 | tf_op jit(solution)/shard_map/ppermute | solution.py:80
  16.8 162.4 %all-gather.7.cloned.1.call-start = ((), (), s32[]{:S(2)}) async-start(), calls=%async_computation.4 | async-start | bytes 4456448 | tf_op jit(solution)/shard_map/all_gather | solution.py:386
  25.8 44.7 %collective-permute-start.3 = (bf16[128,2,2048]{2,0,1:T(8,128)(2,1)}, bf16[128,2,2048]{2,0,1:T(8,128)(2,1)}, u32[]{:S(2)}, u32[]{:S(2)}) collective-permute-start(bf16[128,2,2048]{2,0,1:T(8,128)(2,1)} %bitcast.458), channel_id=1, source_target_pairs={{0,2},{2,0},{1,3},{3,1},{4,6},{6,4},{5,7},{7,5},{8,10},{10,8},{9,1... | collective-permute-start | bytes 3145736 | tf_op jit(solution)/shard_map/ppermute | solution.py:94
  33.6 36.9 %collective-permute-start.1 = (bf16[128,1536]{1,0:T(8,128)(2,1)}, bf16[128,1536]{1,0:T(8,128)(2,1)S(1)}, u32[]{:S(2)}, u32[]{:S(2)}) collective-permute-start(bf16[128,1536]{1,0:T(8,128)(2,1)} %collective-permute-done), channel_id=1, source_target_pairs={{0,2},{2,4},{4,6},{6,0},{1,3},{3,5},{5,7},{7,1},{8,10},{10,12},{12... | collective-permute-start | bytes 1179656 | tf_op jit(solution)/shard_map/ppermute | solution.py:85
  34.0 53.3 %collective-permute-start.8 = (bf16[2,128,2048]{2,1,0:T(8,128)(2,1)}, bf16[2,128,2048]{2,1,0:T(8,128)(2,1)S(1)}, u32[]{:S(2)}, u32[]{:S(2)}) collective-permute-start(bf16[2,128,2048]{2,1,0:T(8,128)(2,1)} %bitcast.413), channel_id=1, source_target_pairs={{0,1},{1,0},{2,3},{3,2},{4,5},{5,4},{6,7},{7,6},{8,9},{9,8},{10,11... | collective-permute-start | bytes 3145736 | tf_op jit(solution)/shard_map/ppermute | solution.py:98
  72.0 20.2 %collective-permute-start.9 = (bf16[2,128,2048]{2,1,0:T(8,128)(2,1)S(1)}, bf16[2,128,2048]{2,1,0:T(8,128)(2,1)S(1)}, u32[]{:S(2)}, u32[]{:S(2)}) collective-permute-start(bf16[2,128,2048]{2,1,0:T(8,128)(2,1)S(1)} %fusion.71), channel_id=1, source_target_pairs={{0,8},{8,0},{1,9},{9,1},{2,10},{10,2},{3,11},{11,3},{4,12},{12,4},... | collective-permute-start | bytes 3145736 | tf_op jit(solution)/shard_map/ppermute | solution.py:75
  73.0 19.2 %collective-permute-start.7 = (bf16[128,1536]{1,0:T(8,128)(2,1)S(1)}, bf16[128,1536]{1,0:T(8,128)(2,1)S(1)}, u32[]{:S(2)}, u32[]{:S(2)}) collective-permute-start(bf16[128,1536]{1,0:T(8,128)(2,1)S(1)} %collective-permute-done.1), channel_id=1, source_target_pairs={{0,16},{16,0},{1,17},{17,1},{2,18},{18,2},{3,19},{19,3},{4,20},{20... | collective-permute-start | bytes 1179656 | tf_op jit(solution)/shard_map/ppermute | solution.py:80
  84.3 20.9 %collective-permute-start.11 = (bf16[2,128,1024]{2,1,0:T(8,128)(2,1)}, bf16[2,128,1024]{2,1,0:T(8,128)(2,1)}, u32[]{:S(2)}, u32[]{:S(2)}) collective-permute-start(bf16[2,128,1024]{2,1,0:T(8,128)(2,1)} %get-tuple-element.79), channel_id=1, source_target_pairs={{0,2},{2,0},{1,3},{3,1},{4,6},{6,4},{5,7},{7,5},{8,10},{10,8},{9,1... | collective-permute-start | bytes 1572872 | tf_op jit(solution)/shard_map/ppermute | solution.py:94
  97.8 234.8 %all-gather.9.cloned.1.call-start = ((), (), s32[]{:S(2)}) async-start(), calls=%async_computation.5 | async-start | bytes 10485760 | tf_op jit(solution)/shard_map/all_gather | solution.py:429
  118.2 20.5 %collective-permute-start.13 = (bf16[2,256,2,256]{3,1,0,2:T(8,128)(2,1)S(1)}, bf16[2,256,2,256]{3,1,0,2:T(8,128)(2,1)}, u32[]{:S(2)}, u32[]{:S(2)}) collective-permute-start(bf16[2,256,2,256]{3,1,0,2:T(8,128)(2,1)S(1)} %pad_maximum_fusion.17), channel_id=1, source_target_pairs={{0,2},{2,4},{4,6},{6,0},{1,3},{3,5},{5,7},{7,1},{8,10},{10,12},{12... | collective-permute-start | bytes 1572872 | tf_op jit(solution)/shard_map/ppermute | solution.py:85
  138.6 24.2 %collective-permute-start.14 = (bf16[2,256,2,256]{3,1,0,2:T(8,128)(2,1)}, bf16[2,256,2,256]{3,1,0,2:T(8,128)(2,1)}, u32[]{:S(2)}, u32[]{:S(2)}) collective-permute-start(bf16[2,256,2,256]{3,1,0,2:T(8,128)(2,1)} %collective-permute-done.13), channel_id=1, source_target_pairs={{0,2},{2,4},{4,6},{6,0},{1,3},{3,5},{5,7},{7,1},{8,10},{10,12},{12... | collective-permute-start | bytes 1572872 | tf_op jit(solution)/shard_map/ppermute | solution.py:85
  179.2 242.0 %all-gather.11.cloned.1.call-start = ((), (), s32[]{:S(2)}) async-start(), calls=%async_computation.6 | async-start | bytes 5242880 | tf_op jit(solution)/shard_map/all_gather | solution.py:432
  192.9 22.5 %collective-permute-start.16 = (bf16[2,128,2048]{2,1,0:T(8,128)(2,1)S(1)}, bf16[2,128,2048]{2,1,0:T(8,128)(2,1)S(1)}, u32[]{:S(2)}, u32[]{:S(2)}) collective-permute-start(bf16[2,128,2048]{2,1,0:T(8,128)(2,1)S(1)} %slice.1134), channel_id=1, source_target_pairs={{0,1},{1,0},{2,3},{3,2},{4,5},{5,4},{6,7},{7,6},{8,9},{9,8},{10,11... | collective-permute-start | bytes 3145736 | tf_op jit(solution)/shard_map/ppermute | solution.py:98
  223.2 38.3 %collective-permute-start.17 = (bf16[256,2048]{1,0:T(8,128)(2,1)S(1)}, bf16[256,2048]{1,0:T(8,128)(2,1)S(1)}, u32[]{:S(2)}, u32[]{:S(2)}) collective-permute-start(bf16[256,2048]{1,0:T(8,128)(2,1)S(1)} %get-tuple-element.325), channel_id=1, source_target_pairs={{0,1},{1,0},{2,3},{3,2},{4,5},{5,4},{6,7},{7,6},{8,9},{9,8},{10,11... | collective-permute-start | bytes 3145736 | tf_op jit(solution)/shard_map/ppermute | solution.py:98
  224.5 35.9 %collective-permute-start.18 = (bf16[256,2048]{1,0:T(8,128)(2,1)S(1)}, bf16[256,2048]{1,0:T(8,128)(2,1)S(1)}, u32[]{:S(2)}, u32[]{:S(2)}) collective-permute-start(bf16[256,2048]{1,0:T(8,128)(2,1)S(1)} %get-tuple-element.325), channel_id=1, source_target_pairs={{0,2},{2,0},{1,3},{3,1},{4,6},{6,4},{5,7},{7,5},{8,10},{10,8},{9,1... | collective-permute-start | bytes 3145736 | tf_op jit(solution)/shard_map/ppermute | solution.py:94
  261.6 24.5 %collective-permute-start.20 = (bf16[128,2048]{1,0:T(8,128)(2,1)S(1)}, bf16[128,2048]{1,0:T(8,128)(2,1)S(1)}, u32[]{:S(2)}, u32[]{:S(2)}) collective-permute-start(bf16[128,2048]{1,0:T(8,128)(2,1)S(1)} %slice.632), channel_id=1, source_target_pairs={{0,2},{2,0},{1,3},{3,1},{4,6},{6,4},{5,7},{7,5},{8,10},{10,8},{9,1... | collective-permute-start | bytes 1572872 | tf_op jit(solution)/shard_map/ppermute | solution.py:94
  286.9 58.7 %collective-permute-start.21 = (bf16[1024,2048]{1,0:T(8,128)(2,1)}, bf16[1024,2048]{1,0:T(8,128)(2,1)}, u32[]{:S(2)}, u32[]{:S(2)}) collective-permute-start(bf16[1024,2048]{1,0:T(8,128)(2,1)} %get-tuple-element.358), channel_id=1, source_target_pairs={{0,8},{8,0},{1,9},{9,1},{2,10},{10,2},{3,11},{11,3},{4,12},{12,4},... | collective-permute-start | bytes 12582920 | tf_op jit(solution)/shard_map/ppermute | solution.py:75
  332.7 263.7 %reduce-scatter.10.cloned.1.call-start = ((), (), s32[]{:S(2)}) async-start(), calls=%async_computation.9 | async-start | bytes 2228224
  440.5 24.5 %collective-permute-start.28 = (bf16[128,2048]{1,0:T(8,128)(2,1)S(1)}, bf16[128,2048]{1,0:T(8,128)(2,1)S(1)}, u32[]{:S(2)}, u32[]{:S(2)}) collective-permute-start(bf16[128,2048]{1,0:T(8,128)(2,1)S(1)} %add_convert_fusion.9), channel_id=1, source_target_pairs={{0,2},{2,0},{1,3},{3,1},{4,6},{6,4},{5,7},{7,5},{8,10},{10,8},{9,1... | collective-permute-start | bytes 1572872 | tf_op jit(solution)/shard_map/ppermute | solution.py:94
  444.1 20.9 %collective-permute-start.23 = (bf16[128,2048]{1,0:T(8,128)(2,1)S(1)}, bf16[128,2048]{1,0:T(8,128)(2,1)S(1)}, u32[]{:S(2)}, u32[]{:S(2)}) collective-permute-start(bf16[128,2048]{1,0:T(8,128)(2,1)S(1)} %add_convert_fusion.12), channel_id=1, source_target_pairs={{0,1},{1,0},{2,3},{3,2},{4,5},{5,4},{6,7},{7,6},{8,9},{9,8},{10,11... | collective-permute-start | bytes 1572872 | tf_op jit(solution)/shard_map/ppermute | solution.py:98
  454.2 20.9 %collective-permute-start.25 = (bf16[128,2048]{1,0:T(8,128)(2,1)S(1)}, bf16[128,2048]{1,0:T(8,128)(2,1)S(1)}, u32[]{:S(2)}, u32[]{:S(2)}) collective-permute-start(bf16[128,2048]{1,0:T(8,128)(2,1)S(1)} %get-tuple-element.267), channel_id=1, source_target_pairs={{0,2},{2,0},{1,3},{3,1},{4,6},{6,4},{5,7},{7,5},{8,10},{10,8},{9,1... | collective-permute-start | bytes 1572872 | tf_op jit(solution)/shard_map/ppermute | solution.py:94
  454.3 20.8 %collective-permute-start.27 = (bf16[128,2048]{1,0:T(8,128)(2,1)S(1)}, bf16[128,2048]{1,0:T(8,128)(2,1)S(1)}, u32[]{:S(2)}, u32[]{:S(2)}) collective-permute-start(bf16[128,2048]{1,0:T(8,128)(2,1)S(1)} %get-tuple-element.268), channel_id=1, source_target_pairs={{0,1},{1,0},{2,3},{3,2},{4,5},{5,4},{6,7},{7,6},{8,9},{9,8},{10,11... | collective-permute-start | bytes 1572872 | tf_op jit(solution)/shard_map/ppermute | solution.py:98
  491.4 25.9 %collective-permute-start.29 = (bf16[256,2048]{1,0:T(8,128)(2,1)S(1)}, bf16[256,2048]{1,0:T(8,128)(2,1)S(1)}, u32[]{:S(2)}, u32[]{:S(2)}) collective-permute-start(bf16[256,2048]{1,0:T(8,128)(2,1)S(1)} %get-tuple-element.304), channel_id=1, source_target_pairs={{0,1},{1,0},{2,3},{3,2},{4,5},{5,4},{6,7},{7,6},{8,9},{9,8},{10,11... | collective-permute-start | bytes 3145736 | tf_op jit(solution)/shard_map/ppermute | solution.py:98
  491.9 23.8 %collective-permute-start.30 = (bf16[256,2048]{1,0:T(8,128)(2,1)S(1)}, bf16[256,2048]{1,0:T(8,128)(2,1)S(1)}, u32[]{:S(2)}, u32[]{:S(2)}) collective-permute-start(bf16[256,2048]{1,0:T(8,128)(2,1)S(1)} %get-tuple-element.304), channel_id=1, source_target_pairs={{0,2},{2,0},{1,3},{3,1},{4,6},{6,4},{5,7},{7,5},{8,10},{10,8},{9,1... | collective-permute-start | bytes 3145736 | tf_op jit(solution)/shard_map/ppermute | solution.py:94
  536.0 182.3 %reduce-scatter.6.cloned.1.call-start = ((), (), s32[]{:S(2)}) async-start(), calls=%async_computation.7 | async-start | bytes 5242880 | tf_op jit(solution)/shard_map/reduce_scatter | solution.py:547
  594.0 26.5 %collective-permute-start.34 = (bf16[1024,2048]{1,0:T(8,128)(2,1)}, bf16[1024,2048]{1,0:T(8,128)(2,1)}, u32[]{:S(2)}, u32[]{:S(2)}) collective-permute-start(bf16[1024,2048]{1,0:T(8,128)(2,1)} %fusion.18), channel_id=1, source_target_pairs={{0,8},{8,0},{1,9},{9,1},{2,10},{10,2},{3,11},{11,3},{4,12},{12,4},... | collective-permute-start | bytes 12582920 | tf_op jit(solution)/shard_map/ppermute | solution.py:75
  597.4 279.1 %reduce-scatter.8.cloned.1.call-start = ((), (), s32[]{:S(2)}) async-start(), calls=%async_computation.8 | async-start | bytes 10485760 | tf_op jit(solution)/shard_map/reduce_scatter | solution.py:568
  628.3 53.1 %collective-permute-start.40 = (bf16[128,2048]{1,0:T(8,128)(2,1)}, bf16[128,2048]{1,0:T(8,128)(2,1)}, u32[]{:S(2)}, u32[]{:S(2)}) collective-permute-start(bf16[128,2048]{1,0:T(8,128)(2,1)} %add_convert_fusion.5), channel_id=1, source_target_pairs={{0,2},{2,0},{1,3},{3,1},{4,6},{6,4},{5,7},{7,5},{8,10},{10,8},{9,1... | collective-permute-start | bytes 1572872 | tf_op jit(solution)/shard_map/ppermute | solution.py:94
  637.3 31.8 %collective-permute-start.36 = (bf16[128,2048]{1,0:T(8,128)(2,1)}, bf16[128,2048]{1,0:T(8,128)(2,1)}, u32[]{:S(2)}, u32[]{:S(2)}) collective-permute-start(bf16[128,2048]{1,0:T(8,128)(2,1)} %get-tuple-element.296), channel_id=1, source_target_pairs={{0,1},{1,0},{2,3},{3,2},{4,5},{5,4},{6,7},{7,6},{8,9},{9,8},{10,11... | collective-permute-start | bytes 1572872 | tf_op jit(solution)/shard_map/ppermute | solution.py:98
  638.5 32.4 %collective-permute-start.38 = (bf16[128,2048]{1,0:T(8,128)(2,1)}, bf16[128,2048]{1,0:T(8,128)(2,1)}, u32[]{:S(2)}, u32[]{:S(2)}) collective-permute-start(bf16[128,2048]{1,0:T(8,128)(2,1)} %get-tuple-element.297), channel_id=1, source_target_pairs={{0,2},{2,0},{1,3},{3,1},{4,6},{6,4},{5,7},{7,5},{8,10},{10,8},{9,1... | collective-permute-start | bytes 1572872 | tf_op jit(solution)/shard_map/ppermute | solution.py:94
  673.9 21.7 %collective-permute-start.37 = (bf16[128,2048]{1,0:T(8,128)(2,1)}, bf16[128,2048]{1,0:T(8,128)(2,1)}, u32[]{:S(2)}, u32[]{:S(2)}) collective-permute-start(bf16[128,2048]{1,0:T(8,128)(2,1)} %get-tuple-element.265), channel_id=1, source_target_pairs={{0,2},{2,0},{1,3},{3,1},{4,6},{6,4},{5,7},{7,5},{8,10},{10,8},{9,1... | collective-permute-start | bytes 1572872 | tf_op jit(solution)/shard_map/ppermute | solution.py:94
  674.1 21.4 %collective-permute-start.39 = (bf16[128,2048]{1,0:T(8,128)(2,1)}, bf16[128,2048]{1,0:T(8,128)(2,1)}, u32[]{:S(2)}, u32[]{:S(2)}) collective-permute-start(bf16[128,2048]{1,0:T(8,128)(2,1)} %get-tuple-element.266), channel_id=1, source_target_pairs={{0,1},{1,0},{2,3},{3,2},{4,5},{5,4},{6,7},{7,6},{8,9},{9,8},{10,11... | collective-permute-start | bytes 1572872 | tf_op jit(solution)/shard_map/ppermute | solution.py:98
  718.4 30.5 %collective-permute-start.41 = (bf16[2,128,2048]{2,1,0:T(8,128)(2,1)}, bf16[2,128,2048]{2,1,0:T(8,128)(2,1)S(1)}, u32[]{:S(2)}, u32[]{:S(2)}) collective-permute-start(bf16[2,128,2048]{2,1,0:T(8,128)(2,1)} %add_add_fusion.2), channel_id=1, source_target_pairs={{0,1},{1,0},{2,3},{3,2},{4,5},{5,4},{6,7},{7,6},{8,9},{9,8},{10,11... | collective-permute-start | bytes 3145736 | tf_op jit(solution)/shard_map/ppermute | solution.py:98
  721.8 24.6 %collective-permute-start.60 = (bf16[2,128,1024]{2,1,0:T(8,128)(2,1)S(1)}, bf16[2,128,1024]{2,1,0:T(8,128)(2,1)S(1)}, u32[]{:S(2)}, u32[]{:S(2)}) collective-permute-start(bf16[2,128,1024]{2,1,0:T(8,128)(2,1)S(1)} %fusion.129), channel_id=1, source_target_pairs={{0,2},{2,0},{1,3},{3,1},{4,6},{6,4},{5,7},{7,5},{8,10},{10,8},{9,1... | collective-permute-start | bytes 1572872 | tf_op jit(solution)/shard_map/ppermute | solution.py:94
  748.8 68.6 %collective-permute-start.61 = (f32[128,2,1024]{2,0,1:T(8,128)}, f32[128,2,1024]{2,0,1:T(8,128)}, u32[]{:S(2)}, u32[]{:S(2)}) collective-permute-start(f32[128,2,1024]{2,0,1:T(8,128)} %fusion.75), channel_id=1, source_target_pairs={{0,8},{8,0},{1,9},{9,1},{2,10},{10,2},{3,11},{11,3},{4,12},{12,4},... | collective-permute-start | bytes 3145736 | tf_op jit(solution)/shard_map/ppermute | solution.py:75
  785.5 21.2 %collective-permute-start.45 = (bf16[2,256,2,256]{3,1,0,2:T(8,128)(2,1)S(1)}, bf16[2,256,2,256]{3,1,0,2:T(8,128)(2,1)S(1)}, u32[]{:S(2)}, u32[]{:S(2)}) collective-permute-start(bf16[2,256,2,256]{3,1,0,2:T(8,128)(2,1)S(1)} %fusion.86), channel_id=1, source_target_pairs={{0,2},{2,4},{4,6},{6,0},{1,3},{3,5},{5,7},{7,1},{8,10},{10,12},{12... | collective-permute-start | bytes 1572872 | tf_op jit(solution)/shard_map/ppermute | solution.py:85
  789.3 52.4 %collective-permute-start.42 = (bf16[1024,1152]{1,0:T(8,128)(2,1)S(1)}, bf16[1024,1152]{1,0:T(8,128)(2,1)S(1)}, u32[]{:S(2)}, u32[]{:S(2)}) collective-permute-start(bf16[1024,1152]{1,0:T(8,128)(2,1)S(1)} %pad_maximum_fusion.2), channel_id=1, source_target_pairs={{0,8},{8,0},{1,9},{9,1},{2,10},{10,2},{3,11},{11,3},{4,12},{12,4},... | collective-permute-start | bytes 7077896 | tf_op jit(solution)/shard_map/ppermute | solution.py:75
  806.9 26.1 %collective-permute-start.46 = (bf16[2,256,2,256]{3,1,0,2:T(8,128)(2,1)S(1)}, bf16[2,256,2,256]{3,1,0,2:T(8,128)(2,1)S(1)}, u32[]{:S(2)}, u32[]{:S(2)}) collective-permute-start(bf16[2,256,2,256]{3,1,0,2:T(8,128)(2,1)S(1)} %fusion.80), channel_id=1, source_target_pairs={{0,2},{2,4},{4,6},{6,0},{1,3},{3,5},{5,7},{7,1},{8,10},{10,12},{12... | collective-permute-start | bytes 1572872 | tf_op jit(solution)/shard_map/ppermute | solution.py:85
  843.2 31.7 %collective-permute-start.44 = (bf16[384,1152]{1,0:T(8,128)(2,1)}, bf16[384,1152]{1,0:T(8,128)(2,1)S(1)}, u32[]{:S(2)}, u32[]{:S(2)}) collective-permute-start(bf16[384,1152]{1,0:T(8,128)(2,1)} %fusion.54), channel_id=1, source_target_pairs={{0,16},{16,0},{1,17},{17,1},{2,18},{18,2},{3,19},{19,3},{4,20},{20... | collective-permute-start | bytes 2654216 | tf_op jit(solution)/shard_map/ppermute | solution.py:80
  844.2 28.8 %collective-permute-start.43 = (bf16[128,1152]{1,0:T(8,128)(2,1)}, bf16[128,1152]{1,0:T(8,128)(2,1)}, u32[]{:S(2)}, u32[]{:S(2)}) collective-permute-start(bf16[128,1152]{1,0:T(8,128)(2,1)} %fusion.113), channel_id=1, source_target_pairs={{0,16},{16,0},{1,17},{17,1},{2,18},{18,2},{3,19},{19,3},{4,20},{20... | collective-permute-start | bytes 884744 | tf_op jit(solution)/shard_map/ppermute | solution.py:80
  890.9 50.5 %collective-permute-start.48 = (bf16[2,128,2048]{2,1,0:T(8,128)(2,1)}, bf16[2,128,2048]{2,1,0:T(8,128)(2,1)}, u32[]{:S(2)}, u32[]{:S(2)}) collective-permute-start(bf16[2,128,2048]{2,1,0:T(8,128)(2,1)} %slice.1133), channel_id=1, source_target_pairs={{0,1},{1,0},{2,3},{3,2},{4,5},{5,4},{6,7},{7,6},{8,9},{9,8},{10,11... | collective-permute-start | bytes 3145736 | tf_op jit(solution)/shard_map/ppermute | solution.py:98
  903.0 49.7 %collective-permute-start.58 = (bf16[2,128,2048]{2,1,0:T(8,128)(2,1)}, bf16[2,128,2048]{2,1,0:T(8,128)(2,1)}, u32[]{:S(2)}, u32[]{:S(2)}) collective-permute-start(bf16[2,128,2048]{2,1,0:T(8,128)(2,1)} %fusion.67), channel_id=1, source_target_pairs={{0,2},{2,0},{1,3},{3,1},{4,6},{6,4},{5,7},{7,5},{8,10},{10,8},{9,1... | collective-permute-start | bytes 3145736 | tf_op jit(solution)/shard_map/ppermute | solution.py:94
  903.0 58.7 %collective-permute-start.49 = (bf16[1024,1536]{1,0:T(8,128)(2,1)}, bf16[1024,1536]{1,0:T(8,128)(2,1)}, u32[]{:S(2)}, u32[]{:S(2)}) collective-permute-start(bf16[1024,1536]{1,0:T(8,128)(2,1)} %convolution_convert_fusion.1), channel_id=1, source_target_pairs={{0,8},{8,0},{1,9},{9,1},{2,10},{10,2},{3,11},{11,3},{4,12},{12,4},... | collective-permute-start | bytes 9437192 | tf_op jit(solution)/shard_map/ppermute | solution.py:75
  913.6 21.1 %collective-permute-start.57 = (bf16[128,1152]{1,0:T(8,128)(2,1)S(1)}, bf16[128,1152]{1,0:T(8,128)(2,1)S(1)}, u32[]{:S(2)}, u32[]{:S(2)}) collective-permute-start(bf16[128,1152]{1,0:T(8,128)(2,1)S(1)} %add_convert_fusion.15), channel_id=1, source_target_pairs={{0,2},{2,4},{4,6},{6,0},{1,3},{3,5},{5,7},{7,1},{8,10},{10,12},{12... | collective-permute-start | bytes 884744 | tf_op jit(solution)/shard_map/ppermute | solution.py:85
  957.3 58.1 %collective-permute-start.59 = (f32[128,2,2048]{2,0,1:T(8,128)S(1)}, f32[128,2,2048]{2,0,1:T(8,128)S(1)}, u32[]{:S(2)}, u32[]{:S(2)}) collective-permute-start(f32[128,2,2048]{2,0,1:T(8,128)S(1)} %fusion.43), channel_id=1, source_target_pairs={{0,8},{8,0},{1,9},{9,1},{2,10},{10,2},{3,11},{11,3},{4,12},{12,4},... | collective-permute-start | bytes 6291464 | tf_op jit(solution)/shard_map/ppermute | solution.py:75
  963.9 27.4 %collective-permute-start.51 = (bf16[384,1536]{1,0:T(8,128)(2,1)S(1)}, bf16[384,1536]{1,0:T(8,128)(2,1)S(1)}, u32[]{:S(2)}, u32[]{:S(2)}) collective-permute-start(bf16[384,1536]{1,0:T(8,128)(2,1)S(1)} %add_convert_fusion), channel_id=1, source_target_pairs={{0,16},{16,0},{1,17},{17,1},{2,18},{18,2},{3,19},{19,3},{4,20},{20... | collective-permute-start | bytes 3538952 | tf_op jit(solution)/shard_map/ppermute | solution.py:80
  (187 other events, 1798.2 us)
Sparse Core Ops, SparseCore 0:
  17.0 59.5 all-gather.4
  98.0 65.9 all-gather.6
  179.4 153.2 all-gather.8
  334.9 86.2 all-gather.10
  536.2 60.1 reduce-scatter.9
  599.4 86.2 reduce-scatter.5
  688.8 182.4 reduce-scatter.7

commit v3 on v2

--- a/solution.py
+++ b/solution.py
@@ -314,6 +314,59 @@
 def sum_two(value):
     rows = value.shape[1] // 2
     return value[:, :rows] + wide(y_swap(low(value[:, rows:])))
+
+
+GELU_SCALE = 0.7978845608028654
+GELU_CUBE = 0.044715
+
+
+def gelu_parts(gate):
+    square = gate * gate
+    bend = jnp.tanh(GELU_SCALE * gate * (1.0 + GELU_CUBE * square))
+    half = 0.5 + 0.5 * bend
+    slope = half + 0.5 * gate * (1.0 - bend * bend) * (
+        GELU_SCALE * (1.0 + 3.0 * GELU_CUBE * square)
+    )
+    return gate * half, slope
+
+
+def hidden_backward(block, weights, both):
+    rows, width = block.shape
+    units = weights.shape[1]
+    tile, chunk = min(512, rows), min(256, units)
+
+    def kernel(block_ref, weights_ref, both_ref, out_ref):
+        for start in range(0, units, chunk):
+            grad = jnp.dot(
+                block_ref[...],
+                weights_ref[:, start : start + chunk],
+                preferred_element_type=jnp.float32,
+            )
+            value, slope = gelu_parts(both_ref[:, start : start + chunk])
+            up = both_ref[:, units + start : units + start + chunk]
+            out_ref[:, start : start + chunk] = (grad * up * slope).astype(jnp.bfloat16)
+            out_ref[:, units + start : units + start + chunk] = (grad * value).astype(
+                jnp.bfloat16
+            )
+
+    return pl.pallas_call(
+        kernel,
+        grid=(rows // tile,),
+        in_specs=[
+            pl.BlockSpec((tile, width), lambda i: (i, 0)),
+            pl.BlockSpec((width, units), lambda i: (0, 0)),
+            pl.BlockSpec((tile, 2 * units), lambda i: (i, 0)),
+        ],
+        out_specs=pl.BlockSpec((tile, 2 * units), lambda i: (i, 0)),
+        out_shape=jax.ShapeDtypeStruct((rows, 2 * units), jnp.bfloat16),
+        compiler_params=pltpu.CompilerParams(vmem_limit_bytes=56 * 2**20),
+        cost_estimate=pl.CostEstimate(
+            flops=2 * rows * width * units,
+            transcendentals=rows * units,
+            bytes_accessed=2 * rows * width + 2 * width * units + 12 * rows * units,
+        ),
+        name="hidden_backward",
+    )(block, weights, both)
 
 
 def on_device(
@@ -494,10 +547,7 @@
 
     hidden_block = add_core(hidden_block)
     gate_up_out = matmul(hidden_block, gate_up_full)
-    hidden, hidden_pull = jax.vjp(
-        geglu, gate_up_out[:, :hidden_part], gate_up_out[:, hidden_part:]
-    )
-    hidden_low = low(hidden)
+    hidden_low = low(geglu(gate_up_out[:, :hidden_part], gate_up_out[:, hidden_part:]))
     token_rows = sequences * own_rows
 
     def down_product(value):
@@ -545,9 +595,7 @@
     hidden_out_block, down_grad = tie(hidden_out_block, down_grad)
     down_grad, side_grads = tie(down_grad, side_grads)
     down_grad = lax.psum_scatter(down_grad, ("x", "pair"), scatter_dimension=0, tiled=True)
-    hidden_grad = matmul(hidden_out_block, down_full_t)
-    gate_grad_full, up_grad_full = hidden_pull(hidden_grad)
-    gate_up_low = jnp.concatenate([low(gate_grad_full), low(up_grad_full)], 1)
+    gate_up_low = hidden_backward(hidden_out_block, down_full_t, gate_up_out)
 
     def gate_up_product(value):
         return matmul_t(value, gate_up_full)

time: 1050 us -> 1040 us (level)
  matrix products: 230 us -> 200 us
  waiting for transfers between devices: 469 us -> 491 us
  starting transfers between devices: 76.2 us -> 55.8 us
  Pallas kernels: 12 us -> 31.5 us
  other arithmetic: 110 us -> 97.9 us
  local copies, waits for them, and re-layouts: 122 us -> 134 us
    dot_general x27 -> x26, matrix products: 121 us -> 96.3 us  [matmul(): return jnp.dot(left, right, preferred_element_type=jnp.float32)]
    pallas_call x0 -> x1, Pallas kernels: none -> 19.3 us  [hidden_backward(): pl.pallas_call(kernel, grid=(rows // tile,), in_specs=[pl.BlockSpec((tile...]
    ppermute x18, waiting for transfers between devices: 150 us -> 167 us  [z_shift(): lax.ppermute(value, CTX, [(i, (i + step) % size) for i in range(size)])]
    all_gather x1, waiting for transfers between devices: 38.9 us -> 51.4 us  [on_device(): down_full_t = lax.all_gather(down_shard, ('x', 'pair'), axis=0, tiled=True)]
    unnamed x1, starting transfers between devices: 12.9 us -> 0.44 us
    ppermute x14, waiting for transfers between devices: 123 us -> 136 us  [odd_swap(): return lax.ppermute(value, 'odd', [(0, 1), (1, 0)])]
    all_gather x1, waiting for transfers between devices: 41.5 us -> 30.8 us  [on_device(): lax.all_gather(gate_up_shard, ('x', 'pair'), axis=0, tiled=True)]
    unnamed x371 -> x377, local copies, waits for them, and re-layouts: 70.3 us -> 79.8 us
  transfers between devices with their start and end apart: 76 -> 76, of which waited for: 42 -> 43; matrix products, arithmetic and copies ran while one was open for 38% -> 35% of each run, Pallas kernels for 1% -> 3%
where the time goes in v3:
time: 1040 us; the launch traced here: 1030 us
  waiting for transfers between devices  491 us (47%)
  matrix products  200 us (19%)
  local copies, waits for them, and re-layouts  134 us (13%)
  other arithmetic  97.9 us (9%)
  starting transfers between devices  55.8 us (5%)
  Pallas kernels  31.5 us (3%)
  between operations  17.3 us (2%)
    ppermute x18, waiting for transfers between devices, z_shift(): lax.ppermute(value, CTX, [(i, (i + step) % size) for i in range(size)])  167 us
    ppermute x14, waiting for transfers between devices, odd_swap(): return lax.ppermute(value, 'odd', [(0, 1), (1, 0)])  136 us
    dot_general x26, matrix products, matmul(): return jnp.dot(left, right, preferred_element_type=jnp.float32)  96.3 us
    dot_general x21, matrix products, matmul_t(): lax.dot_general(left, right, (((1,), (1,)), ((), ())), preferred_element_...  85 us
    unnamed x377, local copies, waits for them, and re-layouts  79.8 us
    all_gather x1, waiting for transfers between devices, on_device(): down_full_t = lax.all_gather(down_shard, ('x', 'pair'), axis=0, tiled=True)  51.4 us
    ppermute x9, waiting for transfers between devices, x_shift(): lax.ppermute(value, 'x', [(i, (i + step) % size) for i in range(size)])  45.1 us
    ppermute x16, waiting for transfers between devices, y_swap(): return lax.ppermute(value, 'tp', [(0, 1), (1, 0)])  41 us
  transfers between devices with their start and end apart: 76, of which 43 were waited for; matrix products, arithmetic and copies ran while one was open for 35% of the time, Pallas kernels for 3%

profile of v3, /device:TPU:0, one launch (start us, length us, event | category | flops | bytes accessed | tf_op | source)
XLA Modules:
  0.0 1027.4 jit_solution(4912046779734111481)
XLA Ops:
  37.8 34.1 %collective-permute-done.1 = bf16[128,1536]{1,0:T(8,128)(2,1)S(1)} collective-permute-done((bf16[128,1536]{1,0:T(8,128)(2,1)}, bf16[128,1536]{1,0:T(8,128)(2,1)S(1)}, u32[]{:S(2)}, u32[]{:S(2)}) %collective-permute-start.1) | collective-permute-done | bytes 393248 | tf_op jit(solution)/shard_map/ppermute | solution.py:85
  76.3 9.3 collective-permute-done.6
  108.2 4.4 collective-permute-done.12
  124.5 16.2 %collective-permute-done.13 = bf16[2,256,2,256]{3,1,0,2:T(8,128)(2,1)} collective-permute-done((bf16[2,256,2,256]{3,1,0,2:T(8,128)(2,1)S(1)}, bf16[2,256,2,256]{3,1,0,2:T(8,128)(2,1)}, u32[]{:S(2)}, u32[]{:S(2)}) %collective-permute-start.13) | collective-permute-done | bytes 524320 | tf_op jit(solution)/shard_map/ppermute | solution.py:85
  149.6 14.3 %collective-permute-done.14 = bf16[2,256,2,256]{3,1,0,2:T(8,128)(2,1)} collective-permute-done((bf16[2,256,2,256]{3,1,0,2:T(8,128)(2,1)}, bf16[2,256,2,256]{3,1,0,2:T(8,128)(2,1)}, u32[]{:S(2)}, u32[]{:S(2)}) %collective-permute-start.14) | collective-permute-done | bytes 524320 | tf_op jit(solution)/shard_map/ppermute | solution.py:85
  165.7 13.3 %collective-permute-done.15 = bf16[2,256,2,256]{3,1,0,2:T(8,128)(2,1)} collective-permute-done((bf16[2,256,2,256]{3,1,0,2:T(8,128)(2,1)}, bf16[2,256,2,256]{3,1,0,2:T(8,128)(2,1)}, u32[]{:S(2)}, u32[]{:S(2)}) %collective-permute-start.15) | collective-permute-done | bytes 524320 | tf_op jit(solution)/shard_map/ppermute | solution.py:85
  196.4 18.4 %collective-permute-done.16 = bf16[2,128,2048]{2,1,0:T(8,128)(2,1)S(1)} collective-permute-done((bf16[2,128,2048]{2,1,0:T(8,128)(2,1)S(1)}, bf16[2,128,2048]{2,1,0:T(8,128)(2,1)S(1)}, u32[]{:S(2)}, u32[]{:S(2)}) %collective-permute-start.16) | collective-permute-done | bytes 1048608 | tf_op jit(solution)/shard_map/ppermute | solution.py:98
  223.9 38.6 %collective-permute-done.18 = bf16[256,2048]{1,0:T(8,128)(2,1)S(1)} collective-permute-done((bf16[256,2048]{1,0:T(8,128)(2,1)S(1)}, bf16[256,2048]{1,0:T(8,128)(2,1)S(1)}, u32[]{:S(2)}, u32[]{:S(2)}) %collective-permute-start.18) | collective-permute-done | bytes 1048608 | tf_op jit(solution)/shard_map/ppermute | solution.py:94
  267.6 4.2 collective-permute-done.19
  272.7 14.0 %collective-permute-done.20 = bf16[128,2048]{1,0:T(8,128)(2,1)S(1)} collective-permute-done((bf16[128,2048]{1,0:T(8,128)(2,1)S(1)}, bf16[128,2048]{1,0:T(8,128)(2,1)S(1)}, u32[]{:S(2)}, u32[]{:S(2)}) %collective-permute-start.20) | collective-permute-done | bytes 524320 | tf_op jit(solution)/shard_map/ppermute | solution.py:94
  291.9 30.8 %all-gather.9.cloned.1.call-done = bf16[2048,2048]{1,0:T(8,128)(2,1)} async-done(((bf16[512,2048]{1,0:T(8,128)(2,1)}), bf16[2048,2048]{1,0:T(8,128)(2,1)}) %all-gather.9.cloned.1.call-update) | async-done | bytes 8388624 | tf_op jit(solution)/shard_map/all_gather | solution.py:482
  323.2 5.1 constant_dynamic-update-slice_fusion.27
  329.3 20.4 %fusion.258.both_ref = f32[2048,2048]{1,0:T(8,128)S(1)} fusion(bf16[2048,2048]{1,0:T(8,128)(2,1)} %constant_dynamic-update-slice_fusion.27, bf16[2048,2048]{1,0:T(8,128)(2,1)S(1)} %copy-done), kind=kOutput, calls=%fused_computation.593 | convolution fusion | flops 17179869184 | bytes 33554432 | tf_op jit(solution)/shard_map/dot_general | solution.py:50
  349.8 5.7 copy-done.4
  355.5 4.4 fusion.8
  359.9 51.4 %all-gather.11.cloned.1.call-done.weights_ref = bf16[2048,1024]{1,0:T(8,128)(2,1)} async-done(((bf16[512,1024]{1,0:T(8,128)(2,1)}), bf16[2048,1024]{1,0:T(8,128)(2,1)}) %all-gather.11.cloned.1.call-update) | async-done | bytes 4194320 | tf_op jit(solution)/shard_map/all_gather | solution.py:485
  411.3 7.5 convolution_convert_fusion.2
  434.7 7.6 collective-permute-done.24
  446.2 8.8 collective-permute-done.28
  455.0 10.1 collective-permute-done.25
  486.6 19.3 %collective-permute-done.30 = bf16[256,2048]{1,0:T(8,128)(2,1)S(1)} collective-permute-done((bf16[256,2048]{1,0:T(8,128)(2,1)S(1)}, bf16[256,2048]{1,0:T(8,128)(2,1)S(1)}, u32[]{:S(2)}, u32[]{:S(2)}) %collective-permute-start.30) | collective-permute-done | bytes 1048608 | tf_op jit(solution)/shard_map/ppermute | solution.py:94
  511.4 6.3 collective-permute-done.31
  527.4 4.8 constant_dynamic-update-slice_fusion.54.block_ref
  532.3 13.3 %convolution_convert_fusion.3 = bf16[2048,1024]{1,0:T(8,128)(2,1)} fusion(bf16[2048,2048]{1,0:T(8,128)(2,1)} %constant_dynamic-update-slice_fusion.54.block_ref, bf16[2048,1024]{1,0:T(8,128)(2,1)S(1)} %copy-done.46), kind=kOutput, calls=%fused_computation.46 | convolution fusion | flops 8592031744 | bytes 16777216 | tf_op jit(solution)/shard_map/dot_general | solution.py:50
  545.6 19.3 %hidden_backward.1 = bf16[2048,2048]{1,0:T(8,128)(2,1)} custom-call(bf16[2048,2048]{1,0:T(8,128)(2,1)} %constant_dynamic-update-slice_fusion.54.block_ref, bf16[2048,1024]{1,0:T(8,128)(2,1)} %all-gather.11.cloned.1.call-done.weights_ref, f32[2048,2048]{1,0:T(8,128)} %copy-done.4), custom_call_target="tpu_custom_call" | custom-call | flops 8589934592 | bytes 37748736 | tf_op jit(solution)/shard_map/hidden_backward/pallas_call | solution.py:352
  564.9 14.1 %fusion.19 = bf16[1024,2048]{1,0:T(8,128)(2,1)} fusion(bf16[2048,2048]{1,0:T(8,128)(2,1)} %all-gather.9.cloned.1.call-done, bf16[2048,2048]{1,0:T(8,128)(2,1)} %hidden_backward.1), kind=kOutput, calls=%fused_computation.43 | convolution fusion | flops 8592031744 | bytes 16777216 | tf_op jit(solution)/shard_map/dot_general | solution.py:54
  582.5 4.6 reduce-scatter.10.cloned.1.call-done
  589.3 7.6 fusion.133
  596.9 7.5 fusion.135
  604.4 5.1 add_convert_fusion.5
  617.6 21.4 %convolution_convert_fusion = bf16[2048,2048]{1,0:T(8,128)(2,1)} fusion(bf16[2048,2048]{1,0:T(8,128)(2,1)} %constant_dynamic-update-slice_fusion.27, bf16[2048,2048]{1,0:T(8,128)(2,1)S(1)} %bitcast.382), kind=kOutput, calls=%fused_computation.16 | convolution fusion | flops 17184063488 | bytes 25165824 | tf_op jit(solution)/shard_map/dot_general | solution.py:50
  639.0 7.5 add_convert_fusion.8
  647.4 8.7 collective-permute-done.38
  660.6 7.6 convert_add_fusion.3
  668.2 14.7 %collective-permute-done.37 = bf16[128,2048]{1,0:T(8,128)(2,1)} collective-permute-done((bf16[128,2048]{1,0:T(8,128)(2,1)}, bf16[128,2048]{1,0:T(8,128)(2,1)}, u32[]{:S(2)}, u32[]{:S(2)}) %collective-permute-start.37) | collective-permute-done | bytes 524320 | tf_op jit(solution)/shard_map/ppermute | solution.py:94
  714.0 20.0 %collective-permute-done.60 = bf16[2,128,1024]{2,1,0:T(8,128)(2,1)S(1)} collective-permute-done((bf16[2,128,1024]{2,1,0:T(8,128)(2,1)S(1)}, bf16[2,128,1024]{2,1,0:T(8,128)(2,1)S(1)}, u32[]{:S(2)}, u32[]{:S(2)}) %collective-permute-start.60) | collective-permute-done | bytes 524320 | tf_op jit(solution)/shard_map/ppermute | solution.py:94
  760.8 4.8 fusion.14
  766.9 6.2 convolution_bitcast_fusion.1
  792.5 20.1 %collective-permute-done.46 = bf16[2,256,2,256]{3,1,0,2:T(8,128)(2,1)S(1)} collective-permute-done((bf16[2,256,2,256]{3,1,0,2:T(8,128)(2,1)S(1)}, bf16[2,256,2,256]{3,1,0,2:T(8,128)(2,1)S(1)}, u32[]{:S(2)}, u32[]{:S(2)}) %collective-permute-start.46) | collective-permute-done | bytes 524320 | tf_op jit(solution)/shard_map/ppermute | solution.py:85
  812.7 7.4 collective-permute-start.47
  829.0 9.3 collective-permute-done.47
  840.7 11.8 %collective-permute-done.43 = bf16[128,1152]{1,0:T(8,128)(2,1)} collective-permute-done((bf16[128,1152]{1,0:T(8,128)(2,1)}, bf16[128,1152]{1,0:T(8,128)(2,1)}, u32[]{:S(2)}, u32[]{:S(2)}) %collective-permute-start.43) | collective-permute-done | bytes 294944 | tf_op jit(solution)/shard_map/ppermute | solution.py:80
  855.9 6.0 reduce-scatter.8.cloned.1.call-done
  890.4 8.6 collective-permute-done.56
  901.7 24.3 %collective-permute-done.57 = bf16[128,1152]{1,0:T(8,128)(2,1)S(1)} collective-permute-done((bf16[128,1152]{1,0:T(8,128)(2,1)S(1)}, bf16[128,1152]{1,0:T(8,128)(2,1)S(1)}, u32[]{:S(2)}, u32[]{:S(2)}) %collective-permute-start.57) | collective-permute-done | bytes 294944 | tf_op jit(solution)/shard_map/ppermute | solution.py:85
  963.6 19.1 %collective-permute-done.51 = bf16[384,1536]{1,0:T(8,128)(2,1)S(1)} collective-permute-done((bf16[384,1536]{1,0:T(8,128)(2,1)S(1)}, bf16[384,1536]{1,0:T(8,128)(2,1)S(1)}, u32[]{:S(2)}, u32[]{:S(2)}) %collective-permute-start.51) | collective-permute-done | bytes 1179680 | tf_op jit(solution)/shard_map/ppermute | solution.py:80
  985.2 10.7 %collective-permute-done.52 = bf16[128,1536]{1,0:T(8,128)(2,1)S(1)} collective-permute-done((bf16[128,1536]{1,0:T(8,128)(2,1)S(1)}, bf16[128,1536]{1,0:T(8,128)(2,1)S(1)}, u32[]{:S(2)}, u32[]{:S(2)}) %collective-permute-start.52) | collective-permute-done | bytes 393248 | tf_op jit(solution)/shard_map/ppermute | solution.py:85
  999.6 6.8 collective-permute-done.53
  (739 shorter events, 374.7 us)
Async XLA Ops:
  7.2 91.2 %all-gather.5.cloned.1.call-start = ((), (), s32[]{:S(2)}) async-start(), calls=%async_computation.3 | async-start | bytes 2703360 | tf_op jit(solution)/shard_map/all_gather | solution.py:437
  9.7 156.0 %all-gather.7.cloned.1.call-start = ((), (), s32[]{:S(2)}) async-start(), calls=%async_computation.4 | async-start | bytes 4456448 | tf_op jit(solution)/shard_map/all_gather | solution.py:439
  12.4 21.3 %collective-permute-start = (bf16[128,1536]{1,0:T(8,128)(2,1)S(1)}, bf16[128,1536]{1,0:T(8,128)(2,1)}, u32[]{:S(2)}, u32[]{:S(2)}) collective-permute-start(bf16[128,1536]{1,0:T(8,128)(2,1)S(1)} %constant_dynamic-update-slice_fusion), channel_id=1, source_target_pairs={{0,2},{2,4},{4,6},{6,0},{1,3},{3,5},{5,7},{7,1},{8,10},{10,12},{12... | collective-permute-start | bytes 1179656 | tf_op jit(solution)/shard_map/ppermute | solution.py:85
  15.4 22.4 %collective-permute-start.2 = (bf16[128,1536]{1,0:T(8,128)(2,1)S(1)}, bf16[128,1536]{1,0:T(8,128)(2,1)}, u32[]{:S(2)}, u32[]{:S(2)}) collective-permute-start(bf16[128,1536]{1,0:T(8,128)(2,1)S(1)} %constant_dynamic-update-slice_fusion), channel_id=1, source_target_pairs={{0,16},{16,0},{1,17},{17,1},{2,18},{18,2},{3,19},{19,3},{4,20},{20... | collective-permute-start | bytes 1179656 | tf_op jit(solution)/shard_map/ppermute | solution.py:80
  25.8 46.2 %collective-permute-start.3 = (bf16[128,2,2048]{2,0,1:T(8,128)(2,1)}, bf16[128,2,2048]{2,0,1:T(8,128)(2,1)}, u32[]{:S(2)}, u32[]{:S(2)}) collective-permute-start(bf16[128,2,2048]{2,0,1:T(8,128)(2,1)} %bitcast.458), channel_id=1, source_target_pairs={{0,2},{2,0},{1,3},{3,1},{4,6},{6,4},{5,7},{7,5},{8,10},{10,8},{9,1... | collective-permute-start | bytes 3145736 | tf_op jit(solution)/shard_map/ppermute | solution.py:94
  33.6 38.3 %collective-permute-start.1 = (bf16[128,1536]{1,0:T(8,128)(2,1)}, bf16[128,1536]{1,0:T(8,128)(2,1)S(1)}, u32[]{:S(2)}, u32[]{:S(2)}) collective-permute-start(bf16[128,1536]{1,0:T(8,128)(2,1)} %collective-permute-done), channel_id=1, source_target_pairs={{0,2},{2,4},{4,6},{6,0},{1,3},{3,5},{5,7},{7,1},{8,10},{10,12},{12... | collective-permute-start | bytes 1179656 | tf_op jit(solution)/shard_map/ppermute | solution.py:85
  34.0 54.6 %collective-permute-start.8 = (bf16[2,128,2048]{2,1,0:T(8,128)(2,1)}, bf16[2,128,2048]{2,1,0:T(8,128)(2,1)S(1)}, u32[]{:S(2)}, u32[]{:S(2)}) collective-permute-start(bf16[2,128,2048]{2,1,0:T(8,128)(2,1)} %bitcast.415), channel_id=1, source_target_pairs={{0,1},{1,0},{2,3},{3,2},{4,5},{5,4},{6,7},{7,6},{8,9},{9,8},{10,11... | collective-permute-start | bytes 3145736 | tf_op jit(solution)/shard_map/ppermute | solution.py:98
  73.4 20.3 %collective-permute-start.9 = (bf16[2,128,2048]{2,1,0:T(8,128)(2,1)S(1)}, bf16[2,128,2048]{2,1,0:T(8,128)(2,1)S(1)}, u32[]{:S(2)}, u32[]{:S(2)}) collective-permute-start(bf16[2,128,2048]{2,1,0:T(8,128)(2,1)S(1)} %fusion.66), channel_id=1, source_target_pairs={{0,8},{8,0},{1,9},{9,1},{2,10},{10,2},{3,11},{11,3},{4,12},{12,4},... | collective-permute-start | bytes 3145736 | tf_op jit(solution)/shard_map/ppermute | solution.py:75
  85.7 20.9 %collective-permute-start.11 = (bf16[2,128,1024]{2,1,0:T(8,128)(2,1)}, bf16[2,128,1024]{2,1,0:T(8,128)(2,1)}, u32[]{:S(2)}, u32[]{:S(2)}) collective-permute-start(bf16[2,128,1024]{2,1,0:T(8,128)(2,1)} %get-tuple-element.79), channel_id=1, source_target_pairs={{0,2},{2,0},{1,3},{3,1},{4,6},{6,4},{5,7},{7,5},{8,10},{10,8},{9,1... | collective-permute-start | bytes 1572872 | tf_op jit(solution)/shard_map/ppermute | solution.py:94
  98.5 224.2 %all-gather.9.cloned.1.call-start = ((), (), s32[]{:S(2)}) async-start(), calls=%async_computation.5 | async-start | bytes 10485760 | tf_op jit(solution)/shard_map/all_gather | solution.py:482
  119.6 21.1 %collective-permute-start.13 = (bf16[2,256,2,256]{3,1,0,2:T(8,128)(2,1)S(1)}, bf16[2,256,2,256]{3,1,0,2:T(8,128)(2,1)}, u32[]{:S(2)}, u32[]{:S(2)}) collective-permute-start(bf16[2,256,2,256]{3,1,0,2:T(8,128)(2,1)S(1)} %pad_maximum_fusion.16), channel_id=1, source_target_pairs={{0,2},{2,4},{4,6},{6,0},{1,3},{3,5},{5,7},{7,1},{8,10},{10,12},{12... | collective-permute-start | bytes 1572872 | tf_op jit(solution)/shard_map/ppermute | solution.py:85
  140.7 23.3 %collective-permute-start.14 = (bf16[2,256,2,256]{3,1,0,2:T(8,128)(2,1)}, bf16[2,256,2,256]{3,1,0,2:T(8,128)(2,1)}, u32[]{:S(2)}, u32[]{:S(2)}) collective-permute-start(bf16[2,256,2,256]{3,1,0,2:T(8,128)(2,1)} %collective-permute-done.13), channel_id=1, source_target_pairs={{0,2},{2,4},{4,6},{6,0},{1,3},{3,5},{5,7},{7,1},{8,10},{10,12},{12... | collective-permute-start | bytes 1572872 | tf_op jit(solution)/shard_map/ppermute | solution.py:85
  165.7 245.6 %all-gather.11.cloned.1.call-start = ((), (), s32[]{:S(2)}) async-start(), calls=%async_computation.6 | async-start | bytes 5242880 | tf_op jit(solution)/shard_map/all_gather | solution.py:485
  191.3 23.5 %collective-permute-start.16 = (bf16[2,128,2048]{2,1,0:T(8,128)(2,1)S(1)}, bf16[2,128,2048]{2,1,0:T(8,128)(2,1)S(1)}, u32[]{:S(2)}, u32[]{:S(2)}) collective-permute-start(bf16[2,128,2048]{2,1,0:T(8,128)(2,1)S(1)} %slice.1064), channel_id=1, source_target_pairs={{0,1},{1,0},{2,3},{3,2},{4,5},{5,4},{6,7},{7,6},{8,9},{9,8},{10,11... | collective-permute-start | bytes 3145736 | tf_op jit(solution)/shard_map/ppermute | solution.py:98
  222.5 40.2 %collective-permute-start.17 = (bf16[256,2048]{1,0:T(8,128)(2,1)S(1)}, bf16[256,2048]{1,0:T(8,128)(2,1)S(1)}, u32[]{:S(2)}, u32[]{:S(2)}) collective-permute-start(bf16[256,2048]{1,0:T(8,128)(2,1)S(1)} %get-tuple-element.323), channel_id=1, source_target_pairs={{0,1},{1,0},{2,3},{3,2},{4,5},{5,4},{6,7},{7,6},{8,9},{9,8},{10,11... | collective-permute-start | bytes 3145736 | tf_op jit(solution)/shard_map/ppermute | solution.py:98
  223.8 38.8 %collective-permute-start.18 = (bf16[256,2048]{1,0:T(8,128)(2,1)S(1)}, bf16[256,2048]{1,0:T(8,128)(2,1)S(1)}, u32[]{:S(2)}, u32[]{:S(2)}) collective-permute-start(bf16[256,2048]{1,0:T(8,128)(2,1)S(1)} %get-tuple-element.323), channel_id=1, source_target_pairs={{0,2},{2,0},{1,3},{3,1},{4,6},{6,4},{5,7},{7,5},{8,10},{10,8},{9,1... | collective-permute-start | bytes 3145736 | tf_op jit(solution)/shard_map/ppermute | solution.py:94
  262.7 24.0 %collective-permute-start.20 = (bf16[128,2048]{1,0:T(8,128)(2,1)S(1)}, bf16[128,2048]{1,0:T(8,128)(2,1)S(1)}, u32[]{:S(2)}, u32[]{:S(2)}) collective-permute-start(bf16[128,2048]{1,0:T(8,128)(2,1)S(1)} %slice.632), channel_id=1, source_target_pairs={{0,2},{2,0},{1,3},{3,1},{4,6},{6,4},{5,7},{7,5},{8,10},{10,8},{9,1... | collective-permute-start | bytes 1572872 | tf_op jit(solution)/shard_map/ppermute | solution.py:94
  287.6 35.6 %collective-permute-start.21 = (bf16[1024,2048]{1,0:T(8,128)(2,1)}, bf16[1024,2048]{1,0:T(8,128)(2,1)}, u32[]{:S(2)}, u32[]{:S(2)}) collective-permute-start(bf16[1024,2048]{1,0:T(8,128)(2,1)} %get-tuple-element.356), channel_id=1, source_target_pairs={{0,8},{8,0},{1,9},{9,1},{2,10},{10,2},{3,11},{11,3},{4,12},{12,4},... | collective-permute-start | bytes 12582920 | tf_op jit(solution)/shard_map/ppermute | solution.py:75
  322.7 264.4 %reduce-scatter.10.cloned.1.call-start = ((), (), s32[]{:S(2)}) async-start(), calls=%async_computation.9 | async-start | bytes 2228224
  430.4 24.5 %collective-permute-start.28 = (bf16[128,2048]{1,0:T(8,128)(2,1)S(1)}, bf16[128,2048]{1,0:T(8,128)(2,1)S(1)}, u32[]{:S(2)}, u32[]{:S(2)}) collective-permute-start(bf16[128,2048]{1,0:T(8,128)(2,1)S(1)} %add_convert_fusion.9), channel_id=1, source_target_pairs={{0,2},{2,0},{1,3},{3,1},{4,6},{6,4},{5,7},{7,5},{8,10},{10,8},{9,1... | collective-permute-start | bytes 1572872 | tf_op jit(solution)/shard_map/ppermute | solution.py:94
  434.0 20.9 %collective-permute-start.23 = (bf16[128,2048]{1,0:T(8,128)(2,1)S(1)}, bf16[128,2048]{1,0:T(8,128)(2,1)S(1)}, u32[]{:S(2)}, u32[]{:S(2)}) collective-permute-start(bf16[128,2048]{1,0:T(8,128)(2,1)S(1)} %add_convert_fusion.12), channel_id=1, source_target_pairs={{0,1},{1,0},{2,3},{3,2},{4,5},{5,4},{6,7},{7,6},{8,9},{9,8},{10,11... | collective-permute-start | bytes 1572872 | tf_op jit(solution)/shard_map/ppermute | solution.py:98
  444.2 20.9 %collective-permute-start.25 = (bf16[128,2048]{1,0:T(8,128)(2,1)S(1)}, bf16[128,2048]{1,0:T(8,128)(2,1)S(1)}, u32[]{:S(2)}, u32[]{:S(2)}) collective-permute-start(bf16[128,2048]{1,0:T(8,128)(2,1)S(1)} %get-tuple-element.265), channel_id=1, source_target_pairs={{0,2},{2,0},{1,3},{3,1},{4,6},{6,4},{5,7},{7,5},{8,10},{10,8},{9,1... | collective-permute-start | bytes 1572872 | tf_op jit(solution)/shard_map/ppermute | solution.py:94
  444.3 20.8 %collective-permute-start.27 = (bf16[128,2048]{1,0:T(8,128)(2,1)S(1)}, bf16[128,2048]{1,0:T(8,128)(2,1)S(1)}, u32[]{:S(2)}, u32[]{:S(2)}) collective-permute-start(bf16[128,2048]{1,0:T(8,128)(2,1)S(1)} %get-tuple-element.266), channel_id=1, source_target_pairs={{0,1},{1,0},{2,3},{3,2},{4,5},{5,4},{6,7},{7,6},{8,9},{9,8},{10,11... | collective-permute-start | bytes 1572872 | tf_op jit(solution)/shard_map/ppermute | solution.py:98
  481.5 25.9 %collective-permute-start.29 = (bf16[256,2048]{1,0:T(8,128)(2,1)S(1)}, bf16[256,2048]{1,0:T(8,128)(2,1)S(1)}, u32[]{:S(2)}, u32[]{:S(2)}) collective-permute-start(bf16[256,2048]{1,0:T(8,128)(2,1)S(1)} %get-tuple-element.302), channel_id=1, source_target_pairs={{0,1},{1,0},{2,3},{3,2},{4,5},{5,4},{6,7},{7,6},{8,9},{9,8},{10,11... | collective-permute-start | bytes 3145736 | tf_op jit(solution)/shard_map/ppermute | solution.py:98
  482.0 23.8 %collective-permute-start.30 = (bf16[256,2048]{1,0:T(8,128)(2,1)S(1)}, bf16[256,2048]{1,0:T(8,128)(2,1)S(1)}, u32[]{:S(2)}, u32[]{:S(2)}) collective-permute-start(bf16[256,2048]{1,0:T(8,128)(2,1)S(1)} %get-tuple-element.302), channel_id=1, source_target_pairs={{0,2},{2,0},{1,3},{3,1},{4,6},{6,4},{5,7},{7,5},{8,10},{10,8},{9,1... | collective-permute-start | bytes 3145736 | tf_op jit(solution)/shard_map/ppermute | solution.py:94
  526.4 179.7 %reduce-scatter.6.cloned.1.call-start = ((), (), s32[]{:S(2)}) async-start(), calls=%async_computation.7 | async-start | bytes 5242880 | tf_op jit(solution)/shard_map/reduce_scatter | solution.py:597
  578.9 25.5 %collective-permute-start.34 = (bf16[1024,2048]{1,0:T(8,128)(2,1)}, bf16[1024,2048]{1,0:T(8,128)(2,1)}, u32[]{:S(2)}, u32[]{:S(2)}) collective-permute-start(bf16[1024,2048]{1,0:T(8,128)(2,1)} %fusion.19), channel_id=1, source_target_pairs={{0,8},{8,0},{1,9},{9,1},{2,10},{10,2},{3,11},{11,3},{4,12},{12,4},... | collective-permute-start | bytes 12582920 | tf_op jit(solution)/shard_map/ppermute | solution.py:75
  588.2 273.8 %reduce-scatter.8.cloned.1.call-start = ((), (), s32[]{:S(2)}) async-start(), calls=%async_computation.8 | async-start | bytes 10485760 | tf_op jit(solution)/shard_map/reduce_scatter | solution.py:616
  609.5 58.7 %collective-permute-start.40 = (bf16[128,2048]{1,0:T(8,128)(2,1)}, bf16[128,2048]{1,0:T(8,128)(2,1)}, u32[]{:S(2)}, u32[]{:S(2)}) collective-permute-start(bf16[128,2048]{1,0:T(8,128)(2,1)} %add_convert_fusion.5), channel_id=1, source_target_pairs={{0,2},{2,0},{1,3},{3,1},{4,6},{6,4},{5,7},{7,5},{8,10},{10,8},{9,1... | collective-permute-start | bytes 1572872 | tf_op jit(solution)/shard_map/ppermute | solution.py:94
  615.5 31.9 %collective-permute-start.36 = (bf16[128,2048]{1,0:T(8,128)(2,1)}, bf16[128,2048]{1,0:T(8,128)(2,1)}, u32[]{:S(2)}, u32[]{:S(2)}) collective-permute-start(bf16[128,2048]{1,0:T(8,128)(2,1)} %get-tuple-element.294), channel_id=1, source_target_pairs={{0,1},{1,0},{2,3},{3,2},{4,5},{5,4},{6,7},{7,6},{8,9},{9,8},{10,11... | collective-permute-start | bytes 1572872 | tf_op jit(solution)/shard_map/ppermute | solution.py:98
  617.0 39.1 %collective-permute-start.38 = (bf16[128,2048]{1,0:T(8,128)(2,1)}, bf16[128,2048]{1,0:T(8,128)(2,1)}, u32[]{:S(2)}, u32[]{:S(2)}) collective-permute-start(bf16[128,2048]{1,0:T(8,128)(2,1)} %get-tuple-element.295), channel_id=1, source_target_pairs={{0,2},{2,0},{1,3},{3,1},{4,6},{6,4},{5,7},{7,5},{8,10},{10,8},{9,1... | collective-permute-start | bytes 1572872 | tf_op jit(solution)/shard_map/ppermute | solution.py:94
  646.6 21.6 %collective-permute-start.35 = (bf16[128,2048]{1,0:T(8,128)(2,1)}, bf16[128,2048]{1,0:T(8,128)(2,1)}, u32[]{:S(2)}, u32[]{:S(2)}) collective-permute-start(bf16[128,2048]{1,0:T(8,128)(2,1)} %add_convert_fusion.8), channel_id=1, source_target_pairs={{0,1},{1,0},{2,3},{3,2},{4,5},{5,4},{6,7},{7,6},{8,9},{9,8},{10,11... | collective-permute-start | bytes 1572872 | tf_op jit(solution)/shard_map/ppermute | solution.py:98
  659.1 23.8 %collective-permute-start.37 = (bf16[128,2048]{1,0:T(8,128)(2,1)}, bf16[128,2048]{1,0:T(8,128)(2,1)}, u32[]{:S(2)}, u32[]{:S(2)}) collective-permute-start(bf16[128,2048]{1,0:T(8,128)(2,1)} %get-tuple-element.263), channel_id=1, source_target_pairs={{0,2},{2,0},{1,3},{3,1},{4,6},{6,4},{5,7},{7,5},{8,10},{10,8},{9,1... | collective-permute-start | bytes 1572872 | tf_op jit(solution)/shard_map/ppermute | solution.py:94
  659.1 23.8 %collective-permute-start.39 = (bf16[128,2048]{1,0:T(8,128)(2,1)}, bf16[128,2048]{1,0:T(8,128)(2,1)}, u32[]{:S(2)}, u32[]{:S(2)}) collective-permute-start(bf16[128,2048]{1,0:T(8,128)(2,1)} %get-tuple-element.264), channel_id=1, source_target_pairs={{0,1},{1,0},{2,3},{3,2},{4,5},{5,4},{6,7},{7,6},{8,9},{9,8},{10,11... | collective-permute-start | bytes 1572872 | tf_op jit(solution)/shard_map/ppermute | solution.py:98
  706.2 30.3 %collective-permute-start.41 = (bf16[2,128,2048]{2,1,0:T(8,128)(2,1)}, bf16[2,128,2048]{2,1,0:T(8,128)(2,1)S(1)}, u32[]{:S(2)}, u32[]{:S(2)}) collective-permute-start(bf16[2,128,2048]{2,1,0:T(8,128)(2,1)} %add_add_fusion.2), channel_id=1, source_target_pairs={{0,1},{1,0},{2,3},{3,2},{4,5},{5,4},{6,7},{7,6},{8,9},{9,8},{10,11... | collective-permute-start | bytes 3145736 | tf_op jit(solution)/shard_map/ppermute | solution.py:98
  709.5 24.5 %collective-permute-start.60 = (bf16[2,128,1024]{2,1,0:T(8,128)(2,1)S(1)}, bf16[2,128,1024]{2,1,0:T(8,128)(2,1)S(1)}, u32[]{:S(2)}, u32[]{:S(2)}) collective-permute-start(bf16[2,128,1024]{2,1,0:T(8,128)(2,1)S(1)} %fusion.120), channel_id=1, source_target_pairs={{0,2},{2,0},{1,3},{3,1},{4,6},{6,4},{5,7},{7,5},{8,10},{10,8},{9,1... | collective-permute-start | bytes 1572872 | tf_op jit(solution)/shard_map/ppermute | solution.py:94
  736.4 54.3 %collective-permute-start.61 = (f32[128,2,1024]{2,0,1:T(8,128)}, f32[128,2,1024]{2,0,1:T(8,128)}, u32[]{:S(2)}, u32[]{:S(2)}) collective-permute-start(f32[128,2,1024]{2,0,1:T(8,128)} %fusion.70), channel_id=1, source_target_pairs={{0,8},{8,0},{1,9},{9,1},{2,10},{10,2},{3,11},{11,3},{4,12},{12,4},... | collective-permute-start | bytes 3145736 | tf_op jit(solution)/shard_map/ppermute | solution.py:75
  777.0 43.1 %collective-permute-start.42 = (bf16[1024,1152]{1,0:T(8,128)(2,1)S(1)}, bf16[1024,1152]{1,0:T(8,128)(2,1)S(1)}, u32[]{:S(2)}, u32[]{:S(2)}) collective-permute-start(bf16[1024,1152]{1,0:T(8,128)(2,1)S(1)} %pad_maximum_fusion.1), channel_id=1, source_target_pairs={{0,8},{8,0},{1,9},{9,1},{2,10},{10,2},{3,11},{11,3},{4,12},{12,4},... | collective-permute-start | bytes 7077896 | tf_op jit(solution)/shard_map/ppermute | solution.py:75
  789.4 23.1 %collective-permute-start.46 = (bf16[2,256,2,256]{3,1,0,2:T(8,128)(2,1)S(1)}, bf16[2,256,2,256]{3,1,0,2:T(8,128)(2,1)S(1)}, u32[]{:S(2)}, u32[]{:S(2)}) collective-permute-start(bf16[2,256,2,256]{3,1,0,2:T(8,128)(2,1)S(1)} %fusion.75), channel_id=1, source_target_pairs={{0,2},{2,4},{4,6},{6,0},{1,3},{3,5},{5,7},{7,1},{8,10},{10,12},{12... | collective-permute-start | bytes 1572872 | tf_op jit(solution)/shard_map/ppermute | solution.py:85
  812.7 25.5 %collective-permute-start.47 = (bf16[2,256,2,256]{3,1,0,2:T(8,128)(2,1)S(1)}, bf16[2,256,2,256]{3,1,0,2:T(8,128)(2,1)}, u32[]{:S(2)}, u32[]{:S(2)}) collective-permute-start(bf16[2,256,2,256]{3,1,0,2:T(8,128)(2,1)S(1)} %fusion.80), channel_id=1, source_target_pairs={{0,2},{2,4},{4,6},{6,0},{1,3},{3,5},{5,7},{7,1},{8,10},{10,12},{12... | collective-permute-start | bytes 1572872 | tf_op jit(solution)/shard_map/ppermute | solution.py:85
  821.8 32.6 %collective-permute-start.44 = (bf16[384,1152]{1,0:T(8,128)(2,1)}, bf16[384,1152]{1,0:T(8,128)(2,1)S(1)}, u32[]{:S(2)}, u32[]{:S(2)}) collective-permute-start(bf16[384,1152]{1,0:T(8,128)(2,1)} %fusion.55), channel_id=1, source_target_pairs={{0,16},{16,0},{1,17},{17,1},{2,18},{18,2},{3,19},{19,3},{4,20},{20... | collective-permute-start | bytes 2654216 | tf_op jit(solution)/shard_map/ppermute | solution.py:80
  824.4 28.1 %collective-permute-start.43 = (bf16[128,1152]{1,0:T(8,128)(2,1)}, bf16[128,1152]{1,0:T(8,128)(2,1)}, u32[]{:S(2)}, u32[]{:S(2)}) collective-permute-start(bf16[128,1152]{1,0:T(8,128)(2,1)} %fusion.116), channel_id=1, source_target_pairs={{0,16},{16,0},{1,17},{17,1},{2,18},{18,2},{3,19},{19,3},{4,20},{20... | collective-permute-start | bytes 884744 | tf_op jit(solution)/shard_map/ppermute | solution.py:80
  876.4 56.1 %collective-permute-start.48 = (bf16[2,128,2048]{2,1,0:T(8,128)(2,1)}, bf16[2,128,2048]{2,1,0:T(8,128)(2,1)}, u32[]{:S(2)}, u32[]{:S(2)}) collective-permute-start(bf16[2,128,2048]{2,1,0:T(8,128)(2,1)} %slice.1063), channel_id=1, source_target_pairs={{0,1},{1,0},{2,3},{3,2},{4,5},{5,4},{6,7},{7,6},{8,9},{9,8},{10,11... | collective-permute-start | bytes 3145736 | tf_op jit(solution)/shard_map/ppermute | solution.py:98
  888.4 55.5 %collective-permute-start.58 = (bf16[2,128,2048]{2,1,0:T(8,128)(2,1)}, bf16[2,128,2048]{2,1,0:T(8,128)(2,1)}, u32[]{:S(2)}, u32[]{:S(2)}) collective-permute-start(bf16[2,128,2048]{2,1,0:T(8,128)(2,1)} %fusion.62), channel_id=1, source_target_pairs={{0,2},{2,0},{1,3},{3,1},{4,6},{6,4},{5,7},{7,5},{8,10},{10,8},{9,1... | collective-permute-start | bytes 3145736 | tf_op jit(solution)/shard_map/ppermute | solution.py:94
  889.1 64.0 %collective-permute-start.49 = (bf16[1024,1536]{1,0:T(8,128)(2,1)}, bf16[1024,1536]{1,0:T(8,128)(2,1)}, u32[]{:S(2)}, u32[]{:S(2)}) collective-permute-start(bf16[1024,1536]{1,0:T(8,128)(2,1)} %convolution_convert_fusion.1), channel_id=1, source_target_pairs={{0,8},{8,0},{1,9},{9,1},{2,10},{10,2},{3,11},{11,3},{4,12},{12,4},... | collective-permute-start | bytes 9437192 | tf_op jit(solution)/shard_map/ppermute | solution.py:75
  899.1 26.8 %collective-permute-start.57 = (bf16[128,1152]{1,0:T(8,128)(2,1)S(1)}, bf16[128,1152]{1,0:T(8,128)(2,1)S(1)}, u32[]{:S(2)}, u32[]{:S(2)}) collective-permute-start(bf16[128,1152]{1,0:T(8,128)(2,1)S(1)} %add_convert_fusion.15), channel_id=1, source_target_pairs={{0,2},{2,4},{4,6},{6,0},{1,3},{3,5},{5,7},{7,1},{8,10},{10,12},{12... | collective-permute-start | bytes 884744 | tf_op jit(solution)/shard_map/ppermute | solution.py:85
  948.1 58.5 %collective-permute-start.59 = (f32[128,2,2048]{2,0,1:T(8,128)S(1)}, f32[128,2,2048]{2,0,1:T(8,128)S(1)}, u32[]{:S(2)}, u32[]{:S(2)}) collective-permute-start(f32[128,2,2048]{2,0,1:T(8,128)S(1)} %fusion.44), channel_id=1, source_target_pairs={{0,8},{8,0},{1,9},{9,1},{2,10},{10,2},{3,11},{11,3},{4,12},{12,4},... | collective-permute-start | bytes 6291464 | tf_op jit(solution)/shard_map/ppermute | solution.py:75
  955.3 27.4 %collective-permute-start.51 = (bf16[384,1536]{1,0:T(8,128)(2,1)S(1)}, bf16[384,1536]{1,0:T(8,128)(2,1)S(1)}, u32[]{:S(2)}, u32[]{:S(2)}) collective-permute-start(bf16[384,1536]{1,0:T(8,128)(2,1)S(1)} %add_convert_fusion), channel_id=1, source_target_pairs={{0,16},{16,0},{1,17},{17,1},{2,18},{18,2},{3,19},{19,3},{4,20},{20... | collective-permute-start | bytes 3538952 | tf_op jit(solution)/shard_map/ppermute | solution.py:80
  (190 other events, 1608.2 us)
Sparse Core Ops, SparseCore 0:
  11.5 64.8 all-gather.4
  98.6 65.4 all-gather.6
  166.5 156.1 all-gather.8
  325.0 86.2 all-gather.10
  526.5 60.5 reduce-scatter.9
  590.2 86.2 reduce-scatter.5
  679.6 182.3 reduce-scatter.7

commit v4 on v3

--- a/solution.py
+++ b/solution.py
@@ -333,7 +333,7 @@
 def hidden_backward(block, weights, both):
     rows, width = block.shape
     units = weights.shape[1]
-    tile, chunk = min(512, rows), min(256, units)
+    tile, chunk = min(1024, rows), min(256, units)
 
     def kernel(block_ref, weights_ref, both_ref, out_ref):
         for start in range(0, units, chunk):

time: 1040 us -> 1040 us (level)
  no operation moved by 1% of the time
where the time goes in v4:
time: 1040 us; the launch traced here: 1030 us
  waiting for transfers between devices  489 us (47%)
  matrix products  200 us (19%)
  local copies, waits for them, and re-layouts  134 us (13%)
  other arithmetic  97.9 us (9%)
  starting transfers between devices  55.5 us (5%)
  Pallas kernels  33.7 us (3%)
  between operations  17.3 us (2%)
    ppermute x18, waiting for transfers between devices, z_shift(): lax.ppermute(value, CTX, [(i, (i + step) % size) for i in range(size)])  167 us
    ppermute x14, waiting for transfers between devices, odd_swap(): return lax.ppermute(value, 'odd', [(0, 1), (1, 0)])  136 us
    dot_general x26, matrix products, matmul(): return jnp.dot(left, right, preferred_element_type=jnp.float32)  96.4 us
    dot_general x21, matrix products, matmul_t(): lax.dot_general(left, right, (((1,), (1,)), ((), ())), preferred_element_...  84.9 us
    unnamed x377, local copies, waits for them, and re-layouts  79.7 us
    all_gather x1, waiting for transfers between devices, on_device(): down_full_t = lax.all_gather(down_shard, ('x', 'pair'), axis=0, tiled=True)  51.4 us
    ppermute x9, waiting for transfers between devices, x_shift(): lax.ppermute(value, 'x', [(i, (i + step) % size) for i in range(size)])  45 us
    ppermute x16, waiting for transfers between devices, y_swap(): return lax.ppermute(value, 'tp', [(0, 1), (1, 0)])  41 us
  transfers between devices with their start and end apart: 76, of which 43 were waited for; matrix products, arithmetic and copies ran while one was open for 35% of the time, Pallas kernels for 3%

profile of v4, /device:TPU:0, one launch (start us, length us, event | category | flops | bytes accessed | tf_op | source)
XLA Modules:
  0.0 1027.5 jit_solution(16445071947874871847)
XLA Ops:
  37.8 34.1 %collective-permute-done.1 = bf16[128,1536]{1,0:T(8,128)(2,1)S(1)} collective-permute-done((bf16[128,1536]{1,0:T(8,128)(2,1)}, bf16[128,1536]{1,0:T(8,128)(2,1)S(1)}, u32[]{:S(2)}, u32[]{:S(2)}) %collective-permute-start.1) | collective-permute-done | bytes 393248 | tf_op jit(solution)/shard_map/ppermute | solution.py:85
  76.3 9.3 collective-permute-done.6
  108.2 4.4 collective-permute-done.12
  124.5 16.2 %collective-permute-done.13 = bf16[2,256,2,256]{3,1,0,2:T(8,128)(2,1)} collective-permute-done((bf16[2,256,2,256]{3,1,0,2:T(8,128)(2,1)S(1)}, bf16[2,256,2,256]{3,1,0,2:T(8,128)(2,1)}, u32[]{:S(2)}, u32[]{:S(2)}) %collective-permute-start.13) | collective-permute-done | bytes 524320 | tf_op jit(solution)/shard_map/ppermute | solution.py:85
  149.6 14.3 %collective-permute-done.14 = bf16[2,256,2,256]{3,1,0,2:T(8,128)(2,1)} collective-permute-done((bf16[2,256,2,256]{3,1,0,2:T(8,128)(2,1)}, bf16[2,256,2,256]{3,1,0,2:T(8,128)(2,1)}, u32[]{:S(2)}, u32[]{:S(2)}) %collective-permute-start.14) | collective-permute-done | bytes 524320 | tf_op jit(solution)/shard_map/ppermute | solution.py:85
  165.7 13.3 %collective-permute-done.15 = bf16[2,256,2,256]{3,1,0,2:T(8,128)(2,1)} collective-permute-done((bf16[2,256,2,256]{3,1,0,2:T(8,128)(2,1)}, bf16[2,256,2,256]{3,1,0,2:T(8,128)(2,1)}, u32[]{:S(2)}, u32[]{:S(2)}) %collective-permute-start.15) | collective-permute-done | bytes 524320 | tf_op jit(solution)/shard_map/ppermute | solution.py:85
  196.4 18.4 %collective-permute-done.16 = bf16[2,128,2048]{2,1,0:T(8,128)(2,1)S(1)} collective-permute-done((bf16[2,128,2048]{2,1,0:T(8,128)(2,1)S(1)}, bf16[2,128,2048]{2,1,0:T(8,128)(2,1)S(1)}, u32[]{:S(2)}, u32[]{:S(2)}) %collective-permute-start.16) | collective-permute-done | bytes 1048608 | tf_op jit(solution)/shard_map/ppermute | solution.py:98
  223.9 38.6 %collective-permute-done.18 = bf16[256,2048]{1,0:T(8,128)(2,1)S(1)} collective-permute-done((bf16[256,2048]{1,0:T(8,128)(2,1)S(1)}, bf16[256,2048]{1,0:T(8,128)(2,1)S(1)}, u32[]{:S(2)}, u32[]{:S(2)}) %collective-permute-start.18) | collective-permute-done | bytes 1048608 | tf_op jit(solution)/shard_map/ppermute | solution.py:94
  267.6 4.2 collective-permute-done.19
  272.7 14.0 %collective-permute-done.20 = bf16[128,2048]{1,0:T(8,128)(2,1)S(1)} collective-permute-done((bf16[128,2048]{1,0:T(8,128)(2,1)S(1)}, bf16[128,2048]{1,0:T(8,128)(2,1)S(1)}, u32[]{:S(2)}, u32[]{:S(2)}) %collective-permute-start.20) | collective-permute-done | bytes 524320 | tf_op jit(solution)/shard_map/ppermute | solution.py:94
  291.9 30.8 %all-gather.9.cloned.1.call-done = bf16[2048,2048]{1,0:T(8,128)(2,1)} async-done(((bf16[512,2048]{1,0:T(8,128)(2,1)}), bf16[2048,2048]{1,0:T(8,128)(2,1)}) %all-gather.9.cloned.1.call-update) | async-done | bytes 8388624 | tf_op jit(solution)/shard_map/all_gather | solution.py:482
  323.2 5.1 constant_dynamic-update-slice_fusion.27
  329.3 20.4 %fusion.258.both_ref = f32[2048,2048]{1,0:T(8,128)S(1)} fusion(bf16[2048,2048]{1,0:T(8,128)(2,1)} %constant_dynamic-update-slice_fusion.27, bf16[2048,2048]{1,0:T(8,128)(2,1)S(1)} %copy-done), kind=kOutput, calls=%fused_computation.593 | convolution fusion | flops 17179869184 | bytes 33554432 | tf_op jit(solution)/shard_map/dot_general | solution.py:50
  349.8 5.7 copy-done.4
  355.5 4.4 fusion.8
  359.9 51.4 %all-gather.11.cloned.1.call-done.weights_ref = bf16[2048,1024]{1,0:T(8,128)(2,1)} async-done(((bf16[512,1024]{1,0:T(8,128)(2,1)}), bf16[2048,1024]{1,0:T(8,128)(2,1)}) %all-gather.11.cloned.1.call-update) | async-done | bytes 4194320 | tf_op jit(solution)/shard_map/all_gather | solution.py:485
  411.3 7.5 convolution_convert_fusion.2
  434.7 7.6 collective-permute-done.24
  446.2 8.8 collective-permute-done.28
  455.0 10.1 collective-permute-done.25
  486.6 19.3 %collective-permute-done.30 = bf16[256,2048]{1,0:T(8,128)(2,1)S(1)} collective-permute-done((bf16[256,2048]{1,0:T(8,128)(2,1)S(1)}, bf16[256,2048]{1,0:T(8,128)(2,1)S(1)}, u32[]{:S(2)}, u32[]{:S(2)}) %collective-permute-start.30) | collective-permute-done | bytes 1048608 | tf_op jit(solution)/shard_map/ppermute | solution.py:94
  511.4 6.3 collective-permute-done.31
  527.4 4.8 constant_dynamic-update-slice_fusion.54.block_ref
  532.3 13.3 %convolution_convert_fusion.3 = bf16[2048,1024]{1,0:T(8,128)(2,1)} fusion(bf16[2048,2048]{1,0:T(8,128)(2,1)} %constant_dynamic-update-slice_fusion.54.block_ref, bf16[2048,1024]{1,0:T(8,128)(2,1)S(1)} %copy-done.46), kind=kOutput, calls=%fused_computation.46 | convolution fusion | flops 8592031744 | bytes 16777216 | tf_op jit(solution)/shard_map/dot_general | solution.py:50
  545.6 21.5 %hidden_backward.1 = bf16[2048,2048]{1,0:T(8,128)(2,1)} custom-call(bf16[2048,2048]{1,0:T(8,128)(2,1)} %constant_dynamic-update-slice_fusion.54.block_ref, bf16[2048,1024]{1,0:T(8,128)(2,1)} %all-gather.11.cloned.1.call-done.weights_ref, f32[2048,2048]{1,0:T(8,128)} %copy-done.4), custom_call_target="tpu_custom_call" | custom-call | flops 8589934592 | bytes 37748736 | tf_op jit(solution)/shard_map/hidden_backward/pallas_call | solution.py:352
  567.1 14.3 %fusion.19 = bf16[1024,2048]{1,0:T(8,128)(2,1)} fusion(bf16[2048,2048]{1,0:T(8,128)(2,1)} %all-gather.9.cloned.1.call-done, bf16[2048,2048]{1,0:T(8,128)(2,1)} %hidden_backward.1), kind=kOutput, calls=%fused_computation.43 | convolution fusion | flops 8592031744 | bytes 16777216 | tf_op jit(solution)/shard_map/dot_general | solution.py:54
  589.1 7.6 fusion.133
  596.7 7.5 fusion.135
  604.3 5.1 add_convert_fusion.5
  617.4 21.6 %convolution_convert_fusion = bf16[2048,2048]{1,0:T(8,128)(2,1)} fusion(bf16[2048,2048]{1,0:T(8,128)(2,1)} %constant_dynamic-update-slice_fusion.27, bf16[2048,2048]{1,0:T(8,128)(2,1)S(1)} %bitcast.382), kind=kOutput, calls=%fused_computation.16 | convolution fusion | flops 17184063488 | bytes 25165824 | tf_op jit(solution)/shard_map/dot_general | solution.py:50
  639.0 7.5 add_convert_fusion.8
  647.3 8.8 collective-permute-done.38
  660.6 7.6 convert_add_fusion.3
  668.2 14.7 %collective-permute-done.37 = bf16[128,2048]{1,0:T(8,128)(2,1)} collective-permute-done((bf16[128,2048]{1,0:T(8,128)(2,1)}, bf16[128,2048]{1,0:T(8,128)(2,1)}, u32[]{:S(2)}, u32[]{:S(2)}) %collective-permute-start.37) | collective-permute-done | bytes 524320 | tf_op jit(solution)/shard_map/ppermute | solution.py:94
  713.7 20.2 %collective-permute-done.60 = bf16[2,128,1024]{2,1,0:T(8,128)(2,1)S(1)} collective-permute-done((bf16[2,128,1024]{2,1,0:T(8,128)(2,1)S(1)}, bf16[2,128,1024]{2,1,0:T(8,128)(2,1)S(1)}, u32[]{:S(2)}, u32[]{:S(2)}) %collective-permute-start.60) | collective-permute-done | bytes 524320 | tf_op jit(solution)/shard_map/ppermute | solution.py:94
  760.8 4.8 fusion.14
  766.9 6.2 convolution_bitcast_fusion.1
  792.4 20.1 %collective-permute-done.46 = bf16[2,256,2,256]{3,1,0,2:T(8,128)(2,1)S(1)} collective-permute-done((bf16[2,256,2,256]{3,1,0,2:T(8,128)(2,1)S(1)}, bf16[2,256,2,256]{3,1,0,2:T(8,128)(2,1)S(1)}, u32[]{:S(2)}, u32[]{:S(2)}) %collective-permute-start.46) | collective-permute-done | bytes 524320 | tf_op jit(solution)/shard_map/ppermute | solution.py:85
  812.7 7.4 collective-permute-start.47
  829.0 9.3 collective-permute-done.47
  840.7 11.8 %collective-permute-done.43 = bf16[128,1152]{1,0:T(8,128)(2,1)} collective-permute-done((bf16[128,1152]{1,0:T(8,128)(2,1)}, bf16[128,1152]{1,0:T(8,128)(2,1)}, u32[]{:S(2)}, u32[]{:S(2)}) %collective-permute-start.43) | collective-permute-done | bytes 294944 | tf_op jit(solution)/shard_map/ppermute | solution.py:80
  855.9 6.1 reduce-scatter.8.cloned.1.call-done
  890.3 8.7 collective-permute-done.56
  901.7 24.2 %collective-permute-done.57 = bf16[128,1152]{1,0:T(8,128)(2,1)S(1)} collective-permute-done((bf16[128,1152]{1,0:T(8,128)(2,1)S(1)}, bf16[128,1152]{1,0:T(8,128)(2,1)S(1)}, u32[]{:S(2)}, u32[]{:S(2)}) %collective-permute-start.57) | collective-permute-done | bytes 294944 | tf_op jit(solution)/shard_map/ppermute | solution.py:85
  939.5 4.2 fusion.29
  963.6 19.1 %collective-permute-done.51 = bf16[384,1536]{1,0:T(8,128)(2,1)S(1)} collective-permute-done((bf16[384,1536]{1,0:T(8,128)(2,1)S(1)}, bf16[384,1536]{1,0:T(8,128)(2,1)S(1)}, u32[]{:S(2)}, u32[]{:S(2)}) %collective-permute-start.51) | collective-permute-done | bytes 1179680 | tf_op jit(solution)/shard_map/ppermute | solution.py:80
  985.2 10.7 %collective-permute-done.52 = bf16[128,1536]{1,0:T(8,128)(2,1)S(1)} collective-permute-done((bf16[128,1536]{1,0:T(8,128)(2,1)S(1)}, bf16[128,1536]{1,0:T(8,128)(2,1)S(1)}, u32[]{:S(2)}, u32[]{:S(2)}) %collective-permute-start.52) | collective-permute-done | bytes 393248 | tf_op jit(solution)/shard_map/ppermute | solution.py:85
  999.6 6.8 collective-permute-done.53
  (739 shorter events, 372.0 us)
Async XLA Ops:
  7.2 91.2 %all-gather.5.cloned.1.call-start = ((), (), s32[]{:S(2)}) async-start(), calls=%async_computation.3 | async-start | bytes 2703360 | tf_op jit(solution)/shard_map/all_gather | solution.py:437
  9.7 156.0 %all-gather.7.cloned.1.call-start = ((), (), s32[]{:S(2)}) async-start(), calls=%async_computation.4 | async-start | bytes 4456448 | tf_op jit(solution)/shard_map/all_gather | solution.py:439
  12.4 21.3 %collective-permute-start = (bf16[128,1536]{1,0:T(8,128)(2,1)S(1)}, bf16[128,1536]{1,0:T(8,128)(2,1)}, u32[]{:S(2)}, u32[]{:S(2)}) collective-permute-start(bf16[128,1536]{1,0:T(8,128)(2,1)S(1)} %constant_dynamic-update-slice_fusion), channel_id=1, source_target_pairs={{0,2},{2,4},{4,6},{6,0},{1,3},{3,5},{5,7},{7,1},{8,10},{10,12},{12... | collective-permute-start | bytes 1179656 | tf_op jit(solution)/shard_map/ppermute | solution.py:85
  15.4 22.4 %collective-permute-start.2 = (bf16[128,1536]{1,0:T(8,128)(2,1)S(1)}, bf16[128,1536]{1,0:T(8,128)(2,1)}, u32[]{:S(2)}, u32[]{:S(2)}) collective-permute-start(bf16[128,1536]{1,0:T(8,128)(2,1)S(1)} %constant_dynamic-update-slice_fusion), channel_id=1, source_target_pairs={{0,16},{16,0},{1,17},{17,1},{2,18},{18,2},{3,19},{19,3},{4,20},{20... | collective-permute-start | bytes 1179656 | tf_op jit(solution)/shard_map/ppermute | solution.py:80
  25.8 46.2 %collective-permute-start.3 = (bf16[128,2,2048]{2,0,1:T(8,128)(2,1)}, bf16[128,2,2048]{2,0,1:T(8,128)(2,1)}, u32[]{:S(2)}, u32[]{:S(2)}) collective-permute-start(bf16[128,2,2048]{2,0,1:T(8,128)(2,1)} %bitcast.458), channel_id=1, source_target_pairs={{0,2},{2,0},{1,3},{3,1},{4,6},{6,4},{5,7},{7,5},{8,10},{10,8},{9,1... | collective-permute-start | bytes 3145736 | tf_op jit(solution)/shard_map/ppermute | solution.py:94
  33.6 38.3 %collective-permute-start.1 = (bf16[128,1536]{1,0:T(8,128)(2,1)}, bf16[128,1536]{1,0:T(8,128)(2,1)S(1)}, u32[]{:S(2)}, u32[]{:S(2)}) collective-permute-start(bf16[128,1536]{1,0:T(8,128)(2,1)} %collective-permute-done), channel_id=1, source_target_pairs={{0,2},{2,4},{4,6},{6,0},{1,3},{3,5},{5,7},{7,1},{8,10},{10,12},{12... | collective-permute-start | bytes 1179656 | tf_op jit(solution)/shard_map/ppermute | solution.py:85
  34.0 54.6 %collective-permute-start.8 = (bf16[2,128,2048]{2,1,0:T(8,128)(2,1)}, bf16[2,128,2048]{2,1,0:T(8,128)(2,1)S(1)}, u32[]{:S(2)}, u32[]{:S(2)}) collective-permute-start(bf16[2,128,2048]{2,1,0:T(8,128)(2,1)} %bitcast.415), channel_id=1, source_target_pairs={{0,1},{1,0},{2,3},{3,2},{4,5},{5,4},{6,7},{7,6},{8,9},{9,8},{10,11... | collective-permute-start | bytes 3145736 | tf_op jit(solution)/shard_map/ppermute | solution.py:98
  73.4 20.3 %collective-permute-start.9 = (bf16[2,128,2048]{2,1,0:T(8,128)(2,1)S(1)}, bf16[2,128,2048]{2,1,0:T(8,128)(2,1)S(1)}, u32[]{:S(2)}, u32[]{:S(2)}) collective-permute-start(bf16[2,128,2048]{2,1,0:T(8,128)(2,1)S(1)} %fusion.66), channel_id=1, source_target_pairs={{0,8},{8,0},{1,9},{9,1},{2,10},{10,2},{3,11},{11,3},{4,12},{12,4},... | collective-permute-start | bytes 3145736 | tf_op jit(solution)/shard_map/ppermute | solution.py:75
  85.7 20.9 %collective-permute-start.11 = (bf16[2,128,1024]{2,1,0:T(8,128)(2,1)}, bf16[2,128,1024]{2,1,0:T(8,128)(2,1)}, u32[]{:S(2)}, u32[]{:S(2)}) collective-permute-start(bf16[2,128,1024]{2,1,0:T(8,128)(2,1)} %get-tuple-element.79), channel_id=1, source_target_pairs={{0,2},{2,0},{1,3},{3,1},{4,6},{6,4},{5,7},{7,5},{8,10},{10,8},{9,1... | collective-permute-start | bytes 1572872 | tf_op jit(solution)/shard_map/ppermute | solution.py:94
  98.5 224.2 %all-gather.9.cloned.1.call-start = ((), (), s32[]{:S(2)}) async-start(), calls=%async_computation.5 | async-start | bytes 10485760 | tf_op jit(solution)/shard_map/all_gather | solution.py:482
  119.6 21.1 %collective-permute-start.13 = (bf16[2,256,2,256]{3,1,0,2:T(8,128)(2,1)S(1)}, bf16[2,256,2,256]{3,1,0,2:T(8,128)(2,1)}, u32[]{:S(2)}, u32[]{:S(2)}) collective-permute-start(bf16[2,256,2,256]{3,1,0,2:T(8,128)(2,1)S(1)} %pad_maximum_fusion.16), channel_id=1, source_target_pairs={{0,2},{2,4},{4,6},{6,0},{1,3},{3,5},{5,7},{7,1},{8,10},{10,12},{12... | collective-permute-start | bytes 1572872 | tf_op jit(solution)/shard_map/ppermute | solution.py:85
  140.7 23.3 %collective-permute-start.14 = (bf16[2,256,2,256]{3,1,0,2:T(8,128)(2,1)}, bf16[2,256,2,256]{3,1,0,2:T(8,128)(2,1)}, u32[]{:S(2)}, u32[]{:S(2)}) collective-permute-start(bf16[2,256,2,256]{3,1,0,2:T(8,128)(2,1)} %collective-permute-done.13), channel_id=1, source_target_pairs={{0,2},{2,4},{4,6},{6,0},{1,3},{3,5},{5,7},{7,1},{8,10},{10,12},{12... | collective-permute-start | bytes 1572872 | tf_op jit(solution)/shard_map/ppermute | solution.py:85
  165.7 245.6 %all-gather.11.cloned.1.call-start = ((), (), s32[]{:S(2)}) async-start(), calls=%async_computation.6 | async-start | bytes 5242880 | tf_op jit(solution)/shard_map/all_gather | solution.py:485
  191.3 23.5 %collective-permute-start.16 = (bf16[2,128,2048]{2,1,0:T(8,128)(2,1)S(1)}, bf16[2,128,2048]{2,1,0:T(8,128)(2,1)S(1)}, u32[]{:S(2)}, u32[]{:S(2)}) collective-permute-start(bf16[2,128,2048]{2,1,0:T(8,128)(2,1)S(1)} %slice.1064), channel_id=1, source_target_pairs={{0,1},{1,0},{2,3},{3,2},{4,5},{5,4},{6,7},{7,6},{8,9},{9,8},{10,11... | collective-permute-start | bytes 3145736 | tf_op jit(solution)/shard_map/ppermute | solution.py:98
  222.5 40.2 %collective-permute-start.17 = (bf16[256,2048]{1,0:T(8,128)(2,1)S(1)}, bf16[256,2048]{1,0:T(8,128)(2,1)S(1)}, u32[]{:S(2)}, u32[]{:S(2)}) collective-permute-start(bf16[256,2048]{1,0:T(8,128)(2,1)S(1)} %get-tuple-element.323), channel_id=1, source_target_pairs={{0,1},{1,0},{2,3},{3,2},{4,5},{5,4},{6,7},{7,6},{8,9},{9,8},{10,11... | collective-permute-start | bytes 3145736 | tf_op jit(solution)/shard_map/ppermute | solution.py:98
  223.8 38.8 %collective-permute-start.18 = (bf16[256,2048]{1,0:T(8,128)(2,1)S(1)}, bf16[256,2048]{1,0:T(8,128)(2,1)S(1)}, u32[]{:S(2)}, u32[]{:S(2)}) collective-permute-start(bf16[256,2048]{1,0:T(8,128)(2,1)S(1)} %get-tuple-element.323), channel_id=1, source_target_pairs={{0,2},{2,0},{1,3},{3,1},{4,6},{6,4},{5,7},{7,5},{8,10},{10,8},{9,1... | collective-permute-start | bytes 3145736 | tf_op jit(solution)/shard_map/ppermute | solution.py:94
  262.7 24.0 %collective-permute-start.20 = (bf16[128,2048]{1,0:T(8,128)(2,1)S(1)}, bf16[128,2048]{1,0:T(8,128)(2,1)S(1)}, u32[]{:S(2)}, u32[]{:S(2)}) collective-permute-start(bf16[128,2048]{1,0:T(8,128)(2,1)S(1)} %slice.632), channel_id=1, source_target_pairs={{0,2},{2,0},{1,3},{3,1},{4,6},{6,4},{5,7},{7,5},{8,10},{10,8},{9,1... | collective-permute-start | bytes 1572872 | tf_op jit(solution)/shard_map/ppermute | solution.py:94
  287.6 35.6 %collective-permute-start.21 = (bf16[1024,2048]{1,0:T(8,128)(2,1)}, bf16[1024,2048]{1,0:T(8,128)(2,1)}, u32[]{:S(2)}, u32[]{:S(2)}) collective-permute-start(bf16[1024,2048]{1,0:T(8,128)(2,1)} %get-tuple-element.356), channel_id=1, source_target_pairs={{0,8},{8,0},{1,9},{9,1},{2,10},{10,2},{3,11},{11,3},{4,12},{12,4},... | collective-permute-start | bytes 12582920 | tf_op jit(solution)/shard_map/ppermute | solution.py:75
  322.7 264.4 %reduce-scatter.10.cloned.1.call-start = ((), (), s32[]{:S(2)}) async-start(), calls=%async_computation.9 | async-start | bytes 2228224
  430.4 24.5 %collective-permute-start.28 = (bf16[128,2048]{1,0:T(8,128)(2,1)S(1)}, bf16[128,2048]{1,0:T(8,128)(2,1)S(1)}, u32[]{:S(2)}, u32[]{:S(2)}) collective-permute-start(bf16[128,2048]{1,0:T(8,128)(2,1)S(1)} %add_convert_fusion.9), channel_id=1, source_target_pairs={{0,2},{2,0},{1,3},{3,1},{4,6},{6,4},{5,7},{7,5},{8,10},{10,8},{9,1... | collective-permute-start | bytes 1572872 | tf_op jit(solution)/shard_map/ppermute | solution.py:94
  434.0 20.9 %collective-permute-start.23 = (bf16[128,2048]{1,0:T(8,128)(2,1)S(1)}, bf16[128,2048]{1,0:T(8,128)(2,1)S(1)}, u32[]{:S(2)}, u32[]{:S(2)}) collective-permute-start(bf16[128,2048]{1,0:T(8,128)(2,1)S(1)} %add_convert_fusion.12), channel_id=1, source_target_pairs={{0,1},{1,0},{2,3},{3,2},{4,5},{5,4},{6,7},{7,6},{8,9},{9,8},{10,11... | collective-permute-start | bytes 1572872 | tf_op jit(solution)/shard_map/ppermute | solution.py:98
  444.2 20.9 %collective-permute-start.25 = (bf16[128,2048]{1,0:T(8,128)(2,1)S(1)}, bf16[128,2048]{1,0:T(8,128)(2,1)S(1)}, u32[]{:S(2)}, u32[]{:S(2)}) collective-permute-start(bf16[128,2048]{1,0:T(8,128)(2,1)S(1)} %get-tuple-element.265), channel_id=1, source_target_pairs={{0,2},{2,0},{1,3},{3,1},{4,6},{6,4},{5,7},{7,5},{8,10},{10,8},{9,1... | collective-permute-start | bytes 1572872 | tf_op jit(solution)/shard_map/ppermute | solution.py:94
  444.3 20.8 %collective-permute-start.27 = (bf16[128,2048]{1,0:T(8,128)(2,1)S(1)}, bf16[128,2048]{1,0:T(8,128)(2,1)S(1)}, u32[]{:S(2)}, u32[]{:S(2)}) collective-permute-start(bf16[128,2048]{1,0:T(8,128)(2,1)S(1)} %get-tuple-element.266), channel_id=1, source_target_pairs={{0,1},{1,0},{2,3},{3,2},{4,5},{5,4},{6,7},{7,6},{8,9},{9,8},{10,11... | collective-permute-start | bytes 1572872 | tf_op jit(solution)/shard_map/ppermute | solution.py:98
  481.5 25.9 %collective-permute-start.29 = (bf16[256,2048]{1,0:T(8,128)(2,1)S(1)}, bf16[256,2048]{1,0:T(8,128)(2,1)S(1)}, u32[]{:S(2)}, u32[]{:S(2)}) collective-permute-start(bf16[256,2048]{1,0:T(8,128)(2,1)S(1)} %get-tuple-element.302), channel_id=1, source_target_pairs={{0,1},{1,0},{2,3},{3,2},{4,5},{5,4},{6,7},{7,6},{8,9},{9,8},{10,11... | collective-permute-start | bytes 3145736 | tf_op jit(solution)/shard_map/ppermute | solution.py:98
  482.0 23.8 %collective-permute-start.30 = (bf16[256,2048]{1,0:T(8,128)(2,1)S(1)}, bf16[256,2048]{1,0:T(8,128)(2,1)S(1)}, u32[]{:S(2)}, u32[]{:S(2)}) collective-permute-start(bf16[256,2048]{1,0:T(8,128)(2,1)S(1)} %get-tuple-element.302), channel_id=1, source_target_pairs={{0,2},{2,0},{1,3},{3,1},{4,6},{6,4},{5,7},{7,5},{8,10},{10,8},{9,1... | collective-permute-start | bytes 3145736 | tf_op jit(solution)/shard_map/ppermute | solution.py:94
  526.4 179.8 %reduce-scatter.6.cloned.1.call-start = ((), (), s32[]{:S(2)}) async-start(), calls=%async_computation.7 | async-start | bytes 5242880 | tf_op jit(solution)/shard_map/reduce_scatter | solution.py:597
  581.3 22.9 %collective-permute-start.34 = (bf16[1024,2048]{1,0:T(8,128)(2,1)}, bf16[1024,2048]{1,0:T(8,128)(2,1)}, u32[]{:S(2)}, u32[]{:S(2)}) collective-permute-start(bf16[1024,2048]{1,0:T(8,128)(2,1)} %fusion.19), channel_id=1, source_target_pairs={{0,8},{8,0},{1,9},{9,1},{2,10},{10,2},{3,11},{11,3},{4,12},{12,4},... | collective-permute-start | bytes 12582920 | tf_op jit(solution)/shard_map/ppermute | solution.py:75
  588.2 273.8 %reduce-scatter.8.cloned.1.call-start = ((), (), s32[]{:S(2)}) async-start(), calls=%async_computation.8 | async-start | bytes 10485760 | tf_op jit(solution)/shard_map/reduce_scatter | solution.py:616
  609.3 58.9 %collective-permute-start.40 = (bf16[128,2048]{1,0:T(8,128)(2,1)}, bf16[128,2048]{1,0:T(8,128)(2,1)}, u32[]{:S(2)}, u32[]{:S(2)}) collective-permute-start(bf16[128,2048]{1,0:T(8,128)(2,1)} %add_convert_fusion.5), channel_id=1, source_target_pairs={{0,2},{2,0},{1,3},{3,1},{4,6},{6,4},{5,7},{7,5},{8,10},{10,8},{9,1... | collective-permute-start | bytes 1572872 | tf_op jit(solution)/shard_map/ppermute | solution.py:94
  615.3 32.0 %collective-permute-start.36 = (bf16[128,2048]{1,0:T(8,128)(2,1)}, bf16[128,2048]{1,0:T(8,128)(2,1)}, u32[]{:S(2)}, u32[]{:S(2)}) collective-permute-start(bf16[128,2048]{1,0:T(8,128)(2,1)} %get-tuple-element.294), channel_id=1, source_target_pairs={{0,1},{1,0},{2,3},{3,2},{4,5},{5,4},{6,7},{7,6},{8,9},{9,8},{10,11... | collective-permute-start | bytes 1572872 | tf_op jit(solution)/shard_map/ppermute | solution.py:98
  616.8 39.3 %collective-permute-start.38 = (bf16[128,2048]{1,0:T(8,128)(2,1)}, bf16[128,2048]{1,0:T(8,128)(2,1)}, u32[]{:S(2)}, u32[]{:S(2)}) collective-permute-start(bf16[128,2048]{1,0:T(8,128)(2,1)} %get-tuple-element.295), channel_id=1, source_target_pairs={{0,2},{2,0},{1,3},{3,1},{4,6},{6,4},{5,7},{7,5},{8,10},{10,8},{9,1... | collective-permute-start | bytes 1572872 | tf_op jit(solution)/shard_map/ppermute | solution.py:94
  646.6 21.7 %collective-permute-start.35 = (bf16[128,2048]{1,0:T(8,128)(2,1)}, bf16[128,2048]{1,0:T(8,128)(2,1)}, u32[]{:S(2)}, u32[]{:S(2)}) collective-permute-start(bf16[128,2048]{1,0:T(8,128)(2,1)} %add_convert_fusion.8), channel_id=1, source_target_pairs={{0,1},{1,0},{2,3},{3,2},{4,5},{5,4},{6,7},{7,6},{8,9},{9,8},{10,11... | collective-permute-start | bytes 1572872 | tf_op jit(solution)/shard_map/ppermute | solution.py:98
  659.1 23.8 %collective-permute-start.37 = (bf16[128,2048]{1,0:T(8,128)(2,1)}, bf16[128,2048]{1,0:T(8,128)(2,1)}, u32[]{:S(2)}, u32[]{:S(2)}) collective-permute-start(bf16[128,2048]{1,0:T(8,128)(2,1)} %get-tuple-element.263), channel_id=1, source_target_pairs={{0,2},{2,0},{1,3},{3,1},{4,6},{6,4},{5,7},{7,5},{8,10},{10,8},{9,1... | collective-permute-start | bytes 1572872 | tf_op jit(solution)/shard_map/ppermute | solution.py:94
  659.1 23.8 %collective-permute-start.39 = (bf16[128,2048]{1,0:T(8,128)(2,1)}, bf16[128,2048]{1,0:T(8,128)(2,1)}, u32[]{:S(2)}, u32[]{:S(2)}) collective-permute-start(bf16[128,2048]{1,0:T(8,128)(2,1)} %get-tuple-element.264), channel_id=1, source_target_pairs={{0,1},{1,0},{2,3},{3,2},{4,5},{5,4},{6,7},{7,6},{8,9},{9,8},{10,11... | collective-permute-start | bytes 1572872 | tf_op jit(solution)/shard_map/ppermute | solution.py:98
  706.2 30.3 %collective-permute-start.41 = (bf16[2,128,2048]{2,1,0:T(8,128)(2,1)}, bf16[2,128,2048]{2,1,0:T(8,128)(2,1)S(1)}, u32[]{:S(2)}, u32[]{:S(2)}) collective-permute-start(bf16[2,128,2048]{2,1,0:T(8,128)(2,1)} %add_add_fusion.2), channel_id=1, source_target_pairs={{0,1},{1,0},{2,3},{3,2},{4,5},{5,4},{6,7},{7,6},{8,9},{9,8},{10,11... | collective-permute-start | bytes 3145736 | tf_op jit(solution)/shard_map/ppermute | solution.py:98
  709.5 24.5 %collective-permute-start.60 = (bf16[2,128,1024]{2,1,0:T(8,128)(2,1)S(1)}, bf16[2,128,1024]{2,1,0:T(8,128)(2,1)S(1)}, u32[]{:S(2)}, u32[]{:S(2)}) collective-permute-start(bf16[2,128,1024]{2,1,0:T(8,128)(2,1)S(1)} %fusion.120), channel_id=1, source_target_pairs={{0,2},{2,0},{1,3},{3,1},{4,6},{6,4},{5,7},{7,5},{8,10},{10,8},{9,1... | collective-permute-start | bytes 1572872 | tf_op jit(solution)/shard_map/ppermute | solution.py:94
  736.4 54.2 %collective-permute-start.61 = (f32[128,2,1024]{2,0,1:T(8,128)}, f32[128,2,1024]{2,0,1:T(8,128)}, u32[]{:S(2)}, u32[]{:S(2)}) collective-permute-start(f32[128,2,1024]{2,0,1:T(8,128)} %fusion.70), channel_id=1, source_target_pairs={{0,8},{8,0},{1,9},{9,1},{2,10},{10,2},{3,11},{11,3},{4,12},{12,4},... | collective-permute-start | bytes 3145736 | tf_op jit(solution)/shard_map/ppermute | solution.py:75
  777.1 43.1 %collective-permute-start.42 = (bf16[1024,1152]{1,0:T(8,128)(2,1)S(1)}, bf16[1024,1152]{1,0:T(8,128)(2,1)S(1)}, u32[]{:S(2)}, u32[]{:S(2)}) collective-permute-start(bf16[1024,1152]{1,0:T(8,128)(2,1)S(1)} %pad_maximum_fusion.1), channel_id=1, source_target_pairs={{0,8},{8,0},{1,9},{9,1},{2,10},{10,2},{3,11},{11,3},{4,12},{12,4},... | collective-permute-start | bytes 7077896 | tf_op jit(solution)/shard_map/ppermute | solution.py:75
  789.4 23.1 %collective-permute-start.46 = (bf16[2,256,2,256]{3,1,0,2:T(8,128)(2,1)S(1)}, bf16[2,256,2,256]{3,1,0,2:T(8,128)(2,1)S(1)}, u32[]{:S(2)}, u32[]{:S(2)}) collective-permute-start(bf16[2,256,2,256]{3,1,0,2:T(8,128)(2,1)S(1)} %fusion.75), channel_id=1, source_target_pairs={{0,2},{2,4},{4,6},{6,0},{1,3},{3,5},{5,7},{7,1},{8,10},{10,12},{12... | collective-permute-start | bytes 1572872 | tf_op jit(solution)/shard_map/ppermute | solution.py:85
  812.7 25.6 %collective-permute-start.47 = (bf16[2,256,2,256]{3,1,0,2:T(8,128)(2,1)S(1)}, bf16[2,256,2,256]{3,1,0,2:T(8,128)(2,1)}, u32[]{:S(2)}, u32[]{:S(2)}) collective-permute-start(bf16[2,256,2,256]{3,1,0,2:T(8,128)(2,1)S(1)} %fusion.80), channel_id=1, source_target_pairs={{0,2},{2,4},{4,6},{6,0},{1,3},{3,5},{5,7},{7,1},{8,10},{10,12},{12... | collective-permute-start | bytes 1572872 | tf_op jit(solution)/shard_map/ppermute | solution.py:85
  821.8 32.6 %collective-permute-start.44 = (bf16[384,1152]{1,0:T(8,128)(2,1)}, bf16[384,1152]{1,0:T(8,128)(2,1)S(1)}, u32[]{:S(2)}, u32[]{:S(2)}) collective-permute-start(bf16[384,1152]{1,0:T(8,128)(2,1)} %fusion.55), channel_id=1, source_target_pairs={{0,16},{16,0},{1,17},{17,1},{2,18},{18,2},{3,19},{19,3},{4,20},{20... | collective-permute-start | bytes 2654216 | tf_op jit(solution)/shard_map/ppermute | solution.py:80
  824.4 28.1 %collective-permute-start.43 = (bf16[128,1152]{1,0:T(8,128)(2,1)}, bf16[128,1152]{1,0:T(8,128)(2,1)}, u32[]{:S(2)}, u32[]{:S(2)}) collective-permute-start(bf16[128,1152]{1,0:T(8,128)(2,1)} %fusion.116), channel_id=1, source_target_pairs={{0,16},{16,0},{1,17},{17,1},{2,18},{18,2},{3,19},{19,3},{4,20},{20... | collective-permute-start | bytes 884744 | tf_op jit(solution)/shard_map/ppermute | solution.py:80
  876.4 56.1 %collective-permute-start.48 = (bf16[2,128,2048]{2,1,0:T(8,128)(2,1)}, bf16[2,128,2048]{2,1,0:T(8,128)(2,1)}, u32[]{:S(2)}, u32[]{:S(2)}) collective-permute-start(bf16[2,128,2048]{2,1,0:T(8,128)(2,1)} %slice.1063), channel_id=1, source_target_pairs={{0,1},{1,0},{2,3},{3,2},{4,5},{5,4},{6,7},{7,6},{8,9},{9,8},{10,11... | collective-permute-start | bytes 3145736 | tf_op jit(solution)/shard_map/ppermute | solution.py:98
  888.4 55.5 %collective-permute-start.58 = (bf16[2,128,2048]{2,1,0:T(8,128)(2,1)}, bf16[2,128,2048]{2,1,0:T(8,128)(2,1)}, u32[]{:S(2)}, u32[]{:S(2)}) collective-permute-start(bf16[2,128,2048]{2,1,0:T(8,128)(2,1)} %fusion.62), channel_id=1, source_target_pairs={{0,2},{2,0},{1,3},{3,1},{4,6},{6,4},{5,7},{7,5},{8,10},{10,8},{9,1... | collective-permute-start | bytes 3145736 | tf_op jit(solution)/shard_map/ppermute | solution.py:94
  889.0 64.1 %collective-permute-start.49 = (bf16[1024,1536]{1,0:T(8,128)(2,1)}, bf16[1024,1536]{1,0:T(8,128)(2,1)}, u32[]{:S(2)}, u32[]{:S(2)}) collective-permute-start(bf16[1024,1536]{1,0:T(8,128)(2,1)} %convolution_convert_fusion.1), channel_id=1, source_target_pairs={{0,8},{8,0},{1,9},{9,1},{2,10},{10,2},{3,11},{11,3},{4,12},{12,4},... | collective-permute-start | bytes 9437192 | tf_op jit(solution)/shard_map/ppermute | solution.py:75
  899.1 26.8 %collective-permute-start.57 = (bf16[128,1152]{1,0:T(8,128)(2,1)S(1)}, bf16[128,1152]{1,0:T(8,128)(2,1)S(1)}, u32[]{:S(2)}, u32[]{:S(2)}) collective-permute-start(bf16[128,1152]{1,0:T(8,128)(2,1)S(1)} %add_convert_fusion.15), channel_id=1, source_target_pairs={{0,2},{2,4},{4,6},{6,0},{1,3},{3,5},{5,7},{7,1},{8,10},{10,12},{12... | collective-permute-start | bytes 884744 | tf_op jit(solution)/shard_map/ppermute | solution.py:85
  948.1 58.5 %collective-permute-start.59 = (f32[128,2,2048]{2,0,1:T(8,128)S(1)}, f32[128,2,2048]{2,0,1:T(8,128)S(1)}, u32[]{:S(2)}, u32[]{:S(2)}) collective-permute-start(f32[128,2,2048]{2,0,1:T(8,128)S(1)} %fusion.44), channel_id=1, source_target_pairs={{0,8},{8,0},{1,9},{9,1},{2,10},{10,2},{3,11},{11,3},{4,12},{12,4},... | collective-permute-start | bytes 6291464 | tf_op jit(solution)/shard_map/ppermute | solution.py:75
  955.3 27.4 %collective-permute-start.51 = (bf16[384,1536]{1,0:T(8,128)(2,1)S(1)}, bf16[384,1536]{1,0:T(8,128)(2,1)S(1)}, u32[]{:S(2)}, u32[]{:S(2)}) collective-permute-start(bf16[384,1536]{1,0:T(8,128)(2,1)S(1)} %add_convert_fusion), channel_id=1, source_target_pairs={{0,16},{16,0},{1,17},{17,1},{2,18},{18,2},{3,19},{19,3},{4,20},{20... | collective-permute-start | bytes 3538952 | tf_op jit(solution)/shard_map/ppermute | solution.py:80
  (190 other events, 1609.1 us)
Sparse Core Ops, SparseCore 0:
  11.5 64.8 all-gather.4
  98.6 65.4 all-gather.6
  166.5 156.1 all-gather.8
  325.0 86.2 all-gather.10
  526.5 60.5 reduce-scatter.9
  590.2 86.2 reduce-scatter.5
  679.6 182.3 reduce-scatter.7
